TPU v7x, 256 devices: a whole 4x4x8 slice. The times are simulated.
256 devices in a mesh: ma: 64 (over x, z, core), lev: 4 (over y).
Axes of the slice: x: 4, y: 4, z: 8, core: 2. Of those that a mesh axis runs over, the one named last changes fastest.
Arguments:
- forcing: float32 [72, 2, 1280, 1280], P('lev', None, 'ma'), may hold values from -80 to 80
- coupling: float32 [4, 1280, 1280], P(None, 'ma'), may hold values from -0.3 to 0.3
- helmholtz: float32 [1280], replicated, may hold values from 0.5 to 5
- vertical: float32 [72, 72], replicated, may hold values from -1 to 3, as said below
Outputs:
- solution: float32 [72, 2, 1280, 1280], P('lev', None, 'ma')
- norms: float32 [2], replicated
Inputs may be any that keep to these rules, and one draw needn't show every extreme that they name: `vertical`: the diagonal entries lie between 1 and 3.
All inputs are finite; a program needn't handle non-finite values.
Results may differ from a plain program's by a relative error of at most 0.000071.
Values sent between devices are 32-bit elements; how exact they have to be, the bound alone decides.
No kernel may reach another device: no remote copies, remote signals or barrier semaphores. Data moves between devices by JAX's collectives and lax.ppermute only.
A program may use at most 192 MiB of HBM per device.

v0:
```python
import jax
import jax.numpy as jnp
from jax import lax
from jax.sharding import Mesh
from jax.sharding import PartitionSpec as P

LEV = 72
WAVES = 1280
MA = ("ma_0", "ma_1", "ma_2")
MA_LEV = ("ma_0", "ma_1", "ma_2", "lev")


OFFSETS = (-2, -1, 1, 2)


def shifted(block, axis, distance):
    devices = range(lax.axis_size(axis))
    route = [(i - distance, i) for i in devices if i - distance in devices]
    return lax.ppermute(block, axis, route)


def by_axis(x, axes):
    for axis in axes:
        x = lax.psum(x, axis)
    return x


def owned_waves(rows, owners, index):
    fold = jnp.arange(rows, dtype=jnp.int32)
    return fold * owners + jnp.where(fold % 2 == 0, index, owners - 1 - index)


def next_row(block, direction):
    empty = jnp.zeros_like(block[:, :, :1])
    if direction > 0:
        return jnp.concatenate([block[:, :, 1:], empty], axis=2)
    return jnp.concatenate([empty, block[:, :, :-1]], axis=2)


def coupled(nearby, offset, owners, index, rows):
    fold = jnp.arange(rows, dtype=jnp.int32)
    even_fold = fold % 2 == 0
    source = jnp.where(even_fold, index + offset, index - offset)
    inside = (source >= 0) & (source < owners)
    upper = 2 * owners - 1 - 2 * index
    lower = -1 - 2 * index
    beyond = jnp.where(
        even_fold,
        jnp.where(source >= owners, upper - offset, lower - offset),
        jnp.where(source < 0, lower + offset, upper + offset),
    )
    picked = jnp.where(even_fold[None, None, :, None], nearby[offset], nearby[-offset])
    result = picked * inside.astype(jnp.float32)[None, None, :, None]
    direction = 1 if offset > 0 else -1
    for delta in (-1, 0, 1):
        weight = (~inside & (beyond == delta)).astype(jnp.float32)
        result = result + next_row(nearby[delta], direction) * weight[None, None, :, None]
    return result


def square_neighbours(values):
    nearby = {0: values}
    for distance in (1, 2, -1, -2):
        nearby[-distance] = shifted(values, MA, distance)
    return nearby


def norm_total(value):
    return by_axis(value, MA_LEV)


def body(forcing, coupling, helmholtz, vertical):
    owners = lax.axis_size(MA)
    index = lax.axis_index(MA)
    rows = forcing.shape[2]
    waves = owned_waves(rows, owners, index)
    width = forcing.shape[3]
    levels = forcing.shape[0]
    weights = lax.dynamic_slice_in_dim(vertical, lax.axis_index("lev") * levels, levels, 0)
    diagonal = lax.dynamic_slice_in_dim(
        jnp.diagonal(vertical), lax.axis_index("lev") * levels, levels, 0
    )
    positions = jnp.arange(width, dtype=jnp.int32)
    live = (positions[None, :] >= waves[:, None]).astype(jnp.float32)[None, None]
    scale = (1.0 / (1.0 + helmholtz[None, :] * diagonal[:, None]))[:, None, None, :]
    rhs = forcing * live
    first_sum = norm_total(jnp.sum(rhs * rhs))
    first = scale * rhs
    mixed = jnp.einsum(
        "kl,lcin->kcin",
        weights,
        lax.all_gather(first, "lev", axis=0, tiled=True),
        precision=lax.Precision.HIGHEST,
    )
    nearby = square_neighbours(first)
    result = first + helmholtz[None, None, None, :] * mixed
    for place, offset in enumerate(OFFSETS):
        result = result + coupling[place][None, None] * coupled(nearby, offset, owners, index, rows)
    residual = rhs - result * live
    solution = first + scale * residual
    second_sum = norm_total(jnp.sum(residual * residual))
    count = LEV * WAVES * (WAVES + 1)
    norms = jnp.sqrt(jnp.stack([first_sum, second_sum]) / count)
    return (solution, norms)


def solution(mesh):
    split = Mesh(mesh.devices.reshape(4, 8, 2, mesh.shape["lev"]), ("ma_0", "ma_1", "ma_2", "lev"))
    return jax.shard_map(
        body,
        mesh=split,
        in_specs=(P("lev", None, MA, None), P(None, MA, None), P(), P()),
        out_specs=(P("lev", None, MA, None), P()),
        check_vma=False,
    )
```

profile of v0, /device:TPU:1, one launch (start us, length us, event | category | flops | bytes accessed | tf_op | source)
XLA Modules:
  0.0 245.4 jit_solution(4459062973413210070)
XLA Ops:
  7.2 0.0 copy-start
  7.2 0.0 all-gather.2.cloned.1.call-start
  7.3 0.1 fusion.23
  7.3 0.6 copy-done
  7.9 1.7 gather_fusion
  9.6 0.1 dynamic_slice.6
  9.7 0.8 add_divide_fusion
  10.5 3.3 %fusion.19 = f32[18,2,20,1280]{3,0,2,1:T(8,128)S(1)} fusion(f32[18,2,20,1280]{3,1,2,0:T(2,128)} %param.4, f32[20,1280]{1,0:T(8,128)S(1)} %fusion.23, f32[18,1280]{1,0:T(8,128)S(1)} %add_divide_fusion), kind=kLoop, calls=%fused_computation.23 | loop fusion | flops 1843200 | bytes 7567360 | tf_op jit(solution)/shard_map/mul | solution.py:88
  13.8 0.0 copy-start.1
  13.8 2.2 copy-done.1
  16.0 0.0 copy-start.2
  16.0 4.7 %copy.15 = f32[18,2,20,1280]{3,1,2,0:T(2,128)} copy(f32[18,2,20,1280]{3,0,2,1:T(8,128)S(1)} %fusion.19) | data formatting | bytes 7372800 | tf_op jit(solution)/shard_map/mul | solution.py:88
  20.7 0.0 all-gather.2.cloned.1.call-update
  20.7 5.2 %collective-permute-start.3 = (f32[18,2,20,1280]{3,1,2,0:T(2,128)}, f32[18,2,20,1280]{3,1,2,0:T(2,128)}, u32[]{:S(2)}, u32[]{:S(2)}) collective-permute-start(f32[18,2,20,1280]{3,1,2,0:T(2,128)} %copy.15), channel_id=1, source_target_pairs={{4,0},{8,4},{12,8},{16,12},{20,16},{24,20},{28,24},{32,28},{36,32}... | collective-permute-start | bytes 11059208 | tf_op jit(solution)/shard_map/ppermute | solution.py:19
  25.8 1.9 collective-permute-start.2
  27.8 1.3 collective-permute-start.1
  29.1 5.9 %collective-permute-start = (f32[18,2,20,1280]{3,1,2,0:T(2,128)}, f32[18,2,20,1280]{3,1,2,0:T(2,128)}, u32[]{:S(2)}, u32[]{:S(2)}) collective-permute-start(f32[18,2,20,1280]{3,1,2,0:T(2,128)} %copy.15), channel_id=1, source_target_pairs={{0,8},{4,12},{8,16},{12,20},{16,24},{20,28},{24,32},{28,36},{32,40... | collective-permute-start | bytes 11059208 | tf_op jit(solution)/shard_map/ppermute | solution.py:19
  35.1 0.0 copy-done.2
  35.1 0.3 fusion.44
  35.5 9.8 %fusion.41 = (f32[18,2,19,1280]{3,0,2,1:T(8,128)}, f32[18,2,19,1280]{3,0,2,1:T(8,128)}) fusion(f32[18,2,20,1280]{3,0,2,1:T(8,128)} %copy-done.1), kind=kLoop, calls=%fused_computation.75 | loop fusion | bytes 14008320 | tf_op jit(solution)/shard_map/slice | solution.py:37
  45.2 53.9 %collective-permute-done.2 = f32[18,2,20,1280]{3,1,2,0:T(2,128)} collective-permute-done((f32[18,2,20,1280]{3,1,2,0:T(2,128)}, f32[18,2,20,1280]{3,1,2,0:T(2,128)}, u32[]{:S(2)}, u32[]{:S(2)}) %collective-permute-start.2) | collective-permute-done | bytes 3686432 | tf_op jit(solution)/shard_map/ppermute | solution.py:19
  99.1 5.6 %fusion.42 = (f32[18,2,19,1280]{3,1,2,0:T(2,128)S(1)}, f32[18,2,19,1280]{3,1,2,0:T(2,128)S(1)}) fusion(f32[18,2,20,1280]{3,1,2,0:T(2,128)} %collective-permute-done.2), kind=kLoop, calls=%fused_computation.76 | loop fusion | bytes 14008320 | tf_op jit(solution)/shard_map/slice | solution.py:37
  104.6 2.5 %copy.141 = f32[18,2,19,1280]{3,0,2,1:T(8,128)} copy(f32[18,2,19,1280]{3,1,2,0:T(2,128)S(1)} %get-tuple-element.37) | data formatting | bytes 7004160
  107.1 2.6 %copy.139 = f32[18,2,19,1280]{3,0,2,1:T(8,128)} copy(f32[18,2,19,1280]{3,1,2,0:T(2,128)S(1)} %get-tuple-element.38) | data formatting | bytes 7004160
  109.8 0.0 collective-permute-done.3
  109.8 5.5 %fusion.43 = (f32[18,2,19,1280]{3,1,2,0:T(2,128)S(1)}, f32[18,2,19,1280]{3,1,2,0:T(2,128)S(1)}) fusion(f32[18,2,20,1280]{3,1,2,0:T(2,128)} %collective-permute-done.3), kind=kLoop, calls=%fused_computation.77 | loop fusion | bytes 14008320 | tf_op jit(solution)/shard_map/slice | solution.py:37
  115.2 2.5 %copy.140 = f32[18,2,19,1280]{3,0,2,1:T(8,128)} copy(f32[18,2,19,1280]{3,1,2,0:T(2,128)S(1)} %get-tuple-element.39) | data formatting | bytes 7004160
  117.7 0.0 copy-start.3
  117.7 2.5 %copy.138 = f32[18,2,19,1280]{3,0,2,1:T(8,128)} copy(f32[18,2,19,1280]{3,1,2,0:T(2,128)S(1)} %get-tuple-element.40) | data formatting | bytes 7004160
  120.2 0.0 collective-permute-done.1
  120.2 26.9 %collective-permute-done = f32[18,2,20,1280]{3,1,2,0:T(2,128)} collective-permute-done((f32[18,2,20,1280]{3,1,2,0:T(2,128)}, f32[18,2,20,1280]{3,1,2,0:T(2,128)}, u32[]{:S(2)}, u32[]{:S(2)}) %collective-permute-start) | collective-permute-done | bytes 3686432 | tf_op jit(solution)/shard_map/ppermute | solution.py:19
  147.1 17.0 %all-gather.2.cloned.1.call-done = f32[72,2,20,1280]{3,1,2,0:T(2,128)} async-done(((f32[18,2,20,1280]{3,1,2,0:T(2,128)}), f32[72,2,20,1280]{3,1,2,0:T(2,128)}) %all-gather.2.cloned.1.call-update) | async-done | bytes 14745616 | tf_op jit(solution)/shard_map/all_gather | solution.py:92
  164.1 0.0 copy-done.3
  164.1 27.1 %multiply_reduce_fusion = (f32[]{:T(128)}, f32[18,2,20,1280]{3,0,2,1:T(8,128)S(1)}, f32[]{:T(128)}) fusion(f32[20,1280]{1,0:T(8,128)S(1)} %fusion.23, f32[18,2,20,1280]{3,1,2,0:T(2,128)} %param.4, f32[18,1280]{1,0:T(8,128)S(1)} %add_divide_fusion, f32[20]{0:T(128)S(1)} %get-tuple-element.52, f32[20]{0:T(128)S(1)} %get-tuple-element.51, ...), kind=kOutput, calls=%fused_computation.25 | convolution fusion | flops 844185600 | bytes 58642956 | tf_op jit(solution)/shard_map/kl,lcin->kcin/dot_general | solution.py:89
  191.2 4.7 %copy.37 = f32[18,2,20,1280]{3,1,2,0:T(2,128)} copy(f32[18,2,20,1280]{3,0,2,1:T(8,128)S(1)} %get-tuple-element.33) | data formatting | bytes 7372800
  195.9 9.0 %all-reduce.8 = (f32[]{:T(128)}, f32[]{:T(128)}) all-reduce(f32[]{:T(128)} %get-tuple-element.32, f32[]{:T(128)} %get-tuple-element.36), channel_id=1, replica_groups=mesh['ma_0'=4,'ma_1'=8,'ma_2'=2,'lev'=4] {'ma_0'}, use_global_device_ids=true, to_apply=%region_6.7 | all-reduce | flops 2 | bytes 16 | tf_op jit(solution)/shard_map/psum | solution.py:24
  204.9 14.4 %all-reduce.6 = (f32[]{:T(128)}, f32[]{:T(128)}) all-reduce(f32[]{:T(128)} %get-tuple-element.12, f32[]{:T(128)} %get-tuple-element.13), channel_id=1, replica_groups=mesh['ma_0'=4,'ma_1'=8,'ma_2'=2,'lev'=4] {'ma_1'}, use_global_device_ids=true, to_apply=%region_7.8 | all-reduce | flops 2 | bytes 16 | tf_op jit(solution)/shard_map/psum | solution.py:24
  219.3 9.2 %all-reduce.9 = (f32[]{:T(128)}, f32[]{:T(128)}) all-reduce(f32[]{:T(128)} %get-tuple-element.8, f32[]{:T(128)} %get-tuple-element.9), channel_id=1, replica_groups=mesh['ma_0'=4,'ma_1'=8,'ma_2'=2,'lev'=4] {'ma_2'}, use_global_device_ids=true, to_apply=%region_8.9 | all-reduce | flops 2 | bytes 16 | tf_op jit(solution)/shard_map/psum | solution.py:24
  228.5 8.1 %all-reduce.7 = (f32[1]{0:T(128)}, f32[1]{0:T(128)}) all-reduce(f32[1]{0:T(128)} %bitcast.8, f32[1]{0:T(128)} %bitcast.7), channel_id=1, replica_groups=mesh['ma_0'=4,'ma_1'=8,'ma_2'=2,'lev'=4] {'lev'}, use_global_device_ids=true, to_apply=%region_9.10 | all-reduce | flops 2 | bytes 16 | tf_op jit(solution)/shard_map/psum | solution.py:24
  236.7 1.8 fusion.31
  (15 shorter events, 0.2 us)
Async XLA Ops:
  7.2 0.8 copy-start
  7.2 156.9 %all-gather.2.cloned.1.call-start = ((), (), s32[]{:S(2)}) async-start(), calls=%async_computation | async-start | bytes 18432000 | tf_op jit(solution)/shard_map/all_gather | solution.py:92
  13.8 2.2 copy-start.1
  16.0 19.1 %copy-start.2 = (f32[4,20,1280]{2,0,1:T(4,128)S(1)}, f32[4,20,1280]{2,0,1:T(4,128)}, u32[]{:S(2)}) copy-start(f32[4,20,1280]{2,0,1:T(4,128)} %param.5) | copy-start | bytes 1228804
  20.7 89.1 %collective-permute-start.3 = (f32[18,2,20,1280]{3,1,2,0:T(2,128)}, f32[18,2,20,1280]{3,1,2,0:T(2,128)}, u32[]{:S(2)}, u32[]{:S(2)}) collective-permute-start(f32[18,2,20,1280]{3,1,2,0:T(2,128)} %copy.15), channel_id=1, source_target_pairs={{4,0},{8,4},{12,8},{16,12},{20,16},{24,20},{28,24},{32,28},{36,32}... | collective-permute-start | bytes 11059208 | tf_op jit(solution)/shard_map/ppermute | solution.py:19
  25.8 73.2 %collective-permute-start.2 = (f32[18,2,20,1280]{3,1,2,0:T(2,128)}, f32[18,2,20,1280]{3,1,2,0:T(2,128)}, u32[]{:S(2)}, u32[]{:S(2)}) collective-permute-start(f32[18,2,20,1280]{3,1,2,0:T(2,128)} %copy.15), channel_id=1, source_target_pairs={{0,4},{4,8},{8,12},{12,16},{16,20},{20,24},{24,28},{28,32},{32,36}... | collective-permute-start | bytes 11059208 | tf_op jit(solution)/shard_map/ppermute | solution.py:19
  27.8 92.4 %collective-permute-start.1 = (f32[18,2,20,1280]{3,1,2,0:T(2,128)}, f32[18,2,20,1280]{3,1,2,0:T(2,128)}, u32[]{:S(2)}, u32[]{:S(2)}) collective-permute-start(f32[18,2,20,1280]{3,1,2,0:T(2,128)} %copy.15), channel_id=1, source_target_pairs={{8,0},{12,4},{16,8},{20,12},{24,16},{28,20},{32,24},{36,28},{40,32... | collective-permute-start | bytes 11059208 | tf_op jit(solution)/shard_map/ppermute | solution.py:19
  29.1 118.0 %collective-permute-start = (f32[18,2,20,1280]{3,1,2,0:T(2,128)}, f32[18,2,20,1280]{3,1,2,0:T(2,128)}, u32[]{:S(2)}, u32[]{:S(2)}) collective-permute-start(f32[18,2,20,1280]{3,1,2,0:T(2,128)} %copy.15), channel_id=1, source_target_pairs={{0,8},{4,12},{8,16},{12,20},{16,24},{20,28},{24,32},{28,36},{32,40... | collective-permute-start | bytes 11059208 | tf_op jit(solution)/shard_map/ppermute | solution.py:19
  117.7 46.4 %copy-start.3 = (f32[1280]{0:T(1024)S(1)}, f32[1280]{0:T(1024)}, u32[]{:S(2)}) copy-start(f32[1280]{0:T(1024)} %param.6) | copy-start | bytes 15364
Sparse Core Ops, SparseCore 0:
  20.8 143.2 all-gather.1
where the time goes:
time: 246 us; the launch traced here: 245 us
  waiting for transfers between devices  97.8 us (40%)
  local copies, waits for them, and re-layouts  45.2 us (18%)
  blocking collectives  40.8 us (17%)
  matrix products  27.1 us (11%)
  starting transfers between devices  14.3 us (6%)
  between operations  14.2 us (6%)
  other arithmetic  6.09 us (2%)
    ppermute x4, waiting for transfers between devices, shifted(): return lax.ppermute(block, axis, route)  80.7 us
    psum x4, blocking collectives, by_axis(): x = lax.psum(x, axis)  40.8 us
    dot_general x1, matrix products, body(): jnp.einsum('kl,lcin->kcin', weights, lax.all_gather(first, 'lev', axis=0,...  27.1 us
    slice x3, local copies, waits for them, and re-layouts, next_row(): return jnp.concatenate([empty, block[:, :, :-1]], axis=2)  20.8 us
    unnamed x13, local copies, waits for them, and re-layouts  17.6 us
    all_gather x1, waiting for transfers between devices, body(): lax.all_gather(first, 'lev', axis=0, tiled=True)  17 us
    ppermute x4, starting transfers between devices, shifted(): return lax.ppermute(block, axis, route)  14.2 us
  transfers between devices with their start and end apart: 5, of which 3 were waited for; matrix products, arithmetic and copies ran while one was open for 13% of the time, Pallas kernels for 0%

commit v1 on v0

v1 whole, which is shorter than its diff:
```python
import jax
import jax.numpy as jnp
from jax import lax
from jax.experimental import pallas as pl
from jax.experimental.pallas import tpu as pltpu
from jax.sharding import Mesh
from jax.sharding import PartitionSpec as P

LEV = 72
WAVES = 1280
OWNERS = 64
FOLDS = 20
TILES = 10
HALF = 112
QROWS = 56
OWN = 18
MA = ("ma_0", "ma_1", "ma_2")
F32 = jnp.float32


def start_row(t):
    return 20 * t - t * (t - 1)


def cut(moves):
    out = []
    for s, d, n in moves:
        while n:
            step = min(n, QROWS - d % QROWS, QROWS - s % QROWS)
            out.append((s, d, step))
            s, d, n = s + step, d + step, n - step
    return out


def cut_target(moves):
    out = []
    for s, d, n in moves:
        while n:
            step = min(n, QROWS - d % QROWS)
            out.append((s, d, step))
            s, d, n = s + step, d + step, n - step
    return out


PACK = cut_target(
    [((2 * t + par) * 20 + 2 * t, par * HALF + start_row(t), 20 - 2 * t) for par in range(2) for t in range(TILES)]
)
PACK_UP = [(s, (d + HALF) % (2 * HALF), n) for s, d, n in PACK]
PACK_DOWN = cut_target(
    [((2 * t + 2) * 20 + 2 * t + 2, HALF + start_row(t) + 2, 18 - 2 * t) for t in range(TILES - 1)]
    + [((2 * t - 1) * 20 + 2 * t, start_row(t), 20 - 2 * t) for t in range(1, TILES)]
)
DOWN_EMPTY = cut_target(
    [(0, HALF + start_row(t), 2) for t in range(TILES)] + [(0, 0, 20)]
)
PADS = [(0, 110, 2), (0, 222, 2)]


def pack_kernel(step_levels, info, x_ref, p_ref, px_ref, py_ref):
    def fill(ref, moves, empty):
        for l in range(step_levels):
            for s, d, n in moves:
                ref[d // QROWS, l, d % QROWS : d % QROWS + n, :] = x_ref[l, s : s + n, :]
            for _, d, n in empty:
                ref[d // QROWS, l, d % QROWS : d % QROWS + n, :] = jnp.zeros((n, 128), F32)

    fill(p_ref, PACK, PADS)
    for ref, slot in ((px_ref, 0), (py_ref, 1)):
        mode = info[slot]

        @pl.when(mode == 0)
        def _(ref=ref):
            fill(ref, PACK, PADS)

        @pl.when(mode == 1)
        def _(ref=ref):
            fill(ref, PACK_UP, PADS)

        @pl.when(mode == 2)
        def _(ref=ref):
            fill(ref, PACK_DOWN, DOWN_EMPTY + PADS)


def pack(info, x):
    tl = 3
    out = jax.ShapeDtypeStruct((4, OWN, QROWS, 128), F32)
    spec = pl.BlockSpec((4, tl, QROWS, 128), lambda i, s: (0, i, 0, 0))
    return pl.pallas_call(
        lambda *refs: pack_kernel(tl, *refs),
        out_shape=(out, out, out),
        grid_spec=pltpu.PrefetchScalarGridSpec(
            num_scalar_prefetch=1,
            grid=(OWN // tl,),
            in_specs=[pl.BlockSpec((tl, 400, 128), lambda i, s: (i, 0, 0))],
            out_specs=[spec, spec, spec],
        ),
        name="pack",
    )(info, x)


BASES = (1, 2, -2, -1)
PLACE = {-2: 0, -1: 1, 1: 2, 2: 3}


def prep_kernel(info, c_ref, h_ref, ck_ref, hp_ref, live_ref):
    owner = info[2]
    odd = info[3]
    for par in range(2):
        for t in range(TILES):
            fold = 2 * t + par
            n = TILES - t
            at = par * HALF + start_row(t)
            wave = fold * OWNERS + (owner if par == 0 else OWNERS - 1 - owner)
            col = lax.broadcasted_iota(jnp.int32, (n, 128), 0) * 128 + lax.broadcasted_iota(jnp.int32, (n, 128), 1) + 128 * t
            live = jnp.where(col >= wave, 1.0, 0.0).astype(F32)
            h = h_ref[t:TILES, :]
            for part in range(2):
                live_ref[pl.ds(at + part, n, stride=2), :] = live
                hp_ref[pl.ds(at + part, n, stride=2), :] = h
            for a, base in enumerate(BASES):
                s_even = base * (1 if par == 0 else -1)
                shift = jnp.where(odd == 1, -s_even, s_even)
                place = jnp.where(odd == 1, PLACE[-s_even], PLACE[s_even])
                low = jnp.where(wave + shift < 0, 2 * WAVES, jnp.maximum(wave, wave + shift))
                c = c_ref[pl.ds((fold * TILES + t) * 4 + place, n, stride=4), :]
                c = jnp.where(col >= low, c, 0.0)
                for part in range(2):
                    ck_ref[a, pl.ds(at + part, n, stride=2), :] = c
        pad = pl.ds(par * HALF + 110, 2)
        zero = jnp.zeros((2, 128), F32)
        live_ref[pad, :] = zero
        hp_ref[pad, :] = zero
        for a in range(4):
            ck_ref[a, pad, :] = zero


def prep(info, c, h):
    rows = jax.ShapeDtypeStruct((2 * HALF, 128), F32)
    vmem = pl.BlockSpec(memory_space=pltpu.VMEM)
    return pl.pallas_call(
        prep_kernel,
        out_shape=(jax.ShapeDtypeStruct((4, 2 * HALF, 128), F32), rows, rows),
        in_specs=[pl.BlockSpec(memory_space=pltpu.SMEM), vmem, vmem],
        out_specs=(vmem, vmem, vmem),
        name="prep",
    )(info, c, h)


def mix_kernel(info, w_ref, d_ref, h_ref, x_ref, o_ref):
    w = w_ref[...].astype(jnp.bfloat16)
    d = d_ref[...]
    x2 = x_ref.reshape(LEV * 8, 128)
    o2 = o_ref.reshape(LEV * 8, 128)
    for r in range(0, 8, 2):
        highs, lows = [], []
        for e in range(2):
            h = h_ref[0, r + e : r + e + 1, :]
            x = x2[pl.ds(r + e, LEV, stride=8), :]
            f = x * (1.0 / (1.0 + h * d))
            high = f.astype(jnp.bfloat16).astype(F32)
            highs.append(high)
            lows.append(f - high)
        high = jnp.concatenate(highs, axis=1)
        low = jnp.concatenate(lows, axis=1)
        both = jnp.concatenate([high, high, low], axis=0).astype(jnp.bfloat16)
        out = jnp.dot(w, both, preferred_element_type=F32)
        for e in range(2):
            h = h_ref[0, r + e : r + e + 1, :]
            o2[pl.ds(r + e, LEV, stride=8), :] = out[:, e * 128 : (e + 1) * 128] * h


def mix(info, w3, diag, hp, x):
    return pl.pallas_call(
        mix_kernel,
        out_shape=jax.ShapeDtypeStruct((LEV, QROWS, 128), F32),
        grid_spec=pltpu.PrefetchScalarGridSpec(
            num_scalar_prefetch=1,
            grid=(QROWS // 8,),
            in_specs=[
                pl.BlockSpec((LEV, 3 * LEV), lambda i, s: (0, 0)),
                pl.BlockSpec((LEV, 1), lambda i, s: (0, 0)),
                pl.BlockSpec((1, 8, 128), lambda i, s: (s[4], i, 0)),
                pl.BlockSpec((LEV, 8, 128), lambda i, s: (0, i, 0)),
            ],
            out_specs=pl.BlockSpec((LEV, 8, 128), lambda i, s: (0, i, 0)),
        ),
        name="mix",
    )(info, w3, diag, hp, x)


def last_kernel(tl, info, d_ref, ck_ref, hp_ref, live_ref, p_ref, q_ref, x_ref, y_ref, z_ref, m_ref, o_ref, s_ref, buf, acc):
    step = pl.program_id(0)

    @pl.when(step == 0)
    def _():
        acc[...] = jnp.zeros_like(acc)

    for l in range(tl):
        d = d_ref[info[4] * OWN + step * tl + l]
        for q in range(4):
            live = live_ref[q]
            v = p_ref[q, l] * live
            scale = 1.0 / (1.0 + hp_ref[q] * d)
            near = ck_ref[0, q] * q_ref[q, l] + ck_ref[1, q] * x_ref[q, l]
            near = near + ck_ref[2, q] * y_ref[q, l] + ck_ref[3, q] * z_ref[q, l]
            first = scale * v
            residual = v - (first + m_ref[q, l] + scale * near) * live
            buf[l, q * QROWS : (q + 1) * QROWS, :] = first + scale * residual
            acc[0] += jnp.sum((v * v).reshape(QROWS // 8, 8, 128), axis=0)
            acc[1] += jnp.sum((residual * residual).reshape(QROWS // 8, 8, 128), axis=0)
        for par in range(2):
            for t in range(TILES):
                at = (2 * t + par) * 20
                if t:
                    o_ref[l, at : at + 2 * t, :] = jnp.zeros((2 * t, 128), F32)
                n = 20 - 2 * t
                s = par * HALF + start_row(t)
                o_ref[l, at + 2 * t : at + 20, :] = buf[l, s : s + n, :]

    @pl.when(step == pl.num_programs(0) - 1)
    def _():
        row = lax.broadcasted_iota(jnp.int32, (8, 128), 0)
        s_ref[...] = jnp.where(row == 0, jnp.sum(acc[0]), jnp.sum(acc[1]))


def last(info, diag, ck, hp, live, p, q, x, y, z, m):
    tl = 3
    whole = lambda shape: pl.BlockSpec(shape, lambda i, s: (0,) * len(shape))
    block = pl.BlockSpec((4, tl, QROWS, 128), lambda i, s: (0, i, 0, 0))
    return pl.pallas_call(
        lambda *refs: last_kernel(tl, *refs),
        out_shape=(jax.ShapeDtypeStruct((OWN, 400, 128), F32), jax.ShapeDtypeStruct((8, 128), F32)),
        grid_spec=pltpu.PrefetchScalarGridSpec(
            num_scalar_prefetch=1,
            grid=(OWN // tl,),
            in_specs=[
                pl.BlockSpec(memory_space=pltpu.SMEM),
                whole((4, 4, QROWS, 128)),
                whole((4, QROWS, 128)),
                whole((4, QROWS, 128)),
            ]
            + [block] * 6,
            out_specs=[pl.BlockSpec((tl, 400, 128), lambda i, s: (i, 0, 0)), whole((8, 128))],
            scratch_shapes=[pltpu.VMEM((tl, 2 * HALF, 128), F32), pltpu.VMEM((2, 8, 128), F32)],
        ),
        name="last",
    )(info, diag, ck, hp, live, p, q, x, y, z, m)


def routes(owners):
    x, y = [], []
    for o in range(owners):
        down = o - 2 if o >= 2 else 1 - o
        up = o + 2 if o + 2 < owners else 2 * owners - 1 - (o + 2)
        x.append((o, down if o % 2 == 0 else up))
        y.append((o, up if o % 2 == 0 else down))
    return x, y, [(o, o ^ 1) for o in range(owners)]


def total(value, axes):
    n = lax.axis_size(axes)
    every = lax.all_to_all(jnp.broadcast_to(value[None], (n,) + value.shape), axes, 0, 0, tiled=True)
    return jnp.sum(every, axis=0)


def body(forcing, coupling, helmholtz, vertical):
    owner = lax.axis_index(MA).astype(jnp.int32)
    lev = lax.axis_index("lev").astype(jnp.int32)
    odd = owner % 2
    mode_x = jnp.where(owner == 0, 2, jnp.where(owner == OWNERS - 1, 1, 0))
    mode_y = jnp.where(owner == 1, 2, jnp.where(owner == OWNERS - 2, 1, 0))
    info = jnp.stack([mode_x, mode_y, owner, odd, lev]).astype(jnp.int32)
    native = forcing.reshape(OWN, 2, FOLDS, TILES, 128).transpose(0, 2, 3, 1, 4).reshape(OWN, 400, 128)
    crows = coupling.reshape(4, FOLDS, TILES, 128).transpose(1, 2, 0, 3).reshape(800, 128)
    p, px, py = pack(info, native)
    to_x, to_y, swap = routes(OWNERS)
    every = lax.all_to_all(p, "lev", 0, 0, tiled=True).reshape(LEV, QROWS, 128)
    x = lax.ppermute(px, MA, to_x)
    y = lax.ppermute(py, MA, to_y)
    q = lax.ppermute(p, MA, swap)
    ck, hp, live = prep(info, crows, helmholtz.reshape(TILES, 128))
    ck = ck.reshape(4, 4, QROWS, 128)
    hp = hp.reshape(4, QROWS, 128)
    live = live.reshape(4, QROWS, 128)
    diag = jnp.sum(vertical * jnp.eye(LEV, dtype=F32), axis=1)
    high = lax.reduce_precision(vertical, 8, 7)
    w3 = jnp.concatenate([high, vertical - high, high], axis=1)
    m = mix(info, w3, diag[:, None], hp, every).reshape(4, OWN, QROWS, 128)
    m = lax.all_to_all(m, "lev", 0, 0, tiled=True)
    z = lax.ppermute(x, MA, swap)
    rows, sums = last(info, diag, ck, hp, live, p, q, x, y, z, m)
    solution = rows.reshape(OWN, FOLDS, TILES, 2, 128).transpose(0, 3, 1, 2, 4).reshape(OWN, 2, FOLDS, WAVES)
    sums = total(total(sums, ("ma_1", "ma_2")), ("ma_0", "lev"))
    norms = jnp.sqrt(sums[:2, 0] / (LEV * WAVES * (WAVES + 1)))
    return (solution, norms)


def solution(mesh):
    split = Mesh(mesh.devices.reshape(4, 8, 2, mesh.shape["lev"]), ("ma_0", "ma_1", "ma_2", "lev"))
    return jax.shard_map(
        body,
        mesh=split,
        in_specs=(P("lev", None, MA, None), P(None, MA, None), P(), P()),
        out_specs=(P("lev", None, MA, None), P()),
        check_vma=False,
    )
```

time: 246 us -> 159 us (0.65)
  waiting for transfers between devices: 97.8 us -> 57.7 us
  matrix products: 27.1 us -> 0 us
  Pallas kernels: 0 us -> 25 us
  blocking collectives: 40.8 us -> 16.5 us
  between operations: 14.2 us -> 0.72 us
  local copies, waits for them, and re-layouts: 45.2 us -> 31.8 us
  starting transfers between devices: 14.3 us -> 24.8 us
  other arithmetic: 6.09 us -> 1.51 us
    ppermute x4, waiting for transfers between devices: 80.7 us -> 31.6 us  [the longest x1 31.6 us: body(): x = lax.ppermute(px, MA, to_x)]
    psum x4 -> x0, blocking collectives: 40.8 us -> none  [by_axis(): x = lax.psum(x, axis)]
    dot_general x1 -> x0, matrix products: 27.1 us -> none  [body(): jnp.einsum('kl,lcin->kcin', weights, lax.all_gather(first, 'lev', axis=0,...]
    all_to_all x0 -> x3, waiting for transfers between devices: none -> 26.1 us  [the longest x1 26.1 us: body(): m = lax.all_to_all(m, 'lev', 0, 0, tiled=True)]
    pallas_call x0 -> x4, Pallas kernels: none -> 25 us  [the longest x1 9.01 us: last(): pl.pallas_call(lambda *refs: last_kernel(tl, *refs), out_shape=(jax.Shape...]
    slice x4 -> x0, local copies, waits for them, and re-layouts: 21.1 us -> none  [the longest x3 20.8 us: next_row(): return jnp.concatenate([empty, block[:, :, :-1]], axis=2)]
    reshape x0 -> x4, local copies, waits for them, and re-layouts: none -> 19.2 us  [the longest x2 12.2 us: body(): rows.reshape(OWN, FOLDS, TILES, 2, 128).transpose(0, 3, 1, 2, 4)]
    all_gather x1 -> x0, waiting for transfers between devices: 17 us -> none  [body(): lax.all_gather(first, 'lev', axis=0, tiled=True)]
  transfers between devices with their start and end apart: 5 -> 7, of which waited for: 3 -> 2; matrix products, arithmetic and copies ran while one was open for 13% -> 9% of each run, Pallas kernels for 0% -> 6%
where the time goes in v1:
time: 159 us; the launch traced here: 158 us
  waiting for transfers between devices  57.7 us (36%)
  local copies, waits for them, and re-layouts  31.8 us (20%)
  Pallas kernels  25 us (16%)
  starting transfers between devices  24.8 us (16%)
  blocking collectives  16.5 us (10%)
    ppermute x1, waiting for transfers between devices, body(): x = lax.ppermute(px, MA, to_x)  31.6 us
    all_to_all x1, waiting for transfers between devices, body(): m = lax.all_to_all(m, 'lev', 0, 0, tiled=True)  26.1 us
    all_to_all x1, blocking collectives, total(): lax.all_to_all(jnp.broadcast_to(value[None], (n,) + value.shape), axes, 0...  16.5 us
    reshape x2, local copies, waits for them, and re-layouts, body(): rows.reshape(OWN, FOLDS, TILES, 2, 128).transpose(0, 3, 1, 2, 4)  12.2 us
    pallas_call x1, Pallas kernels, last(): pl.pallas_call(lambda *refs: last_kernel(tl, *refs), out_shape=(jax.Shape...  9.01 us
    ppermute x1, starting transfers between devices, body(): z = lax.ppermute(x, MA, swap)  7.39 us
    pallas_call x1, Pallas kernels, mix(): pl.pallas_call(mix_kernel, out_shape=jax.ShapeDtypeStruct((LEV, QROWS, 12...  7.06 us
    pallas_call x1, Pallas kernels, pack(): pl.pallas_call(lambda *refs: pack_kernel(tl, *refs), out_shape=(out, out,...  6.85 us
  transfers between devices with their start and end apart: 7, of which 2 were waited for; matrix products, arithmetic and copies ran while one was open for 9% of the time, Pallas kernels for 6%

profile of v1, /device:TPU:1, one launch (start us, length us, event | category | flops | bytes accessed | tf_op | source)
XLA Modules:
  0.0 157.9 jit_solution(16856685242774541228)
XLA Ops:
  0.7 6.8 %reshape.51 = f32[18,2,20,10,128]{4,3,1,2,0:T(8,128)} reshape(f32[18,2,20,1280]{3,1,2,0:T(2,128)} %param.4) | data formatting | bytes 7372800 | tf_op jit(solution)/shard_map/reshape | solution.py:273
  7.5 6.4 %copy.19 = f32[18,20,10,2,128]{4,3,2,1,0:T(2,128)} copy(f32[18,20,10,2,128]{4,2,3,1,0:T(8,128)} %bitcast.27) | data formatting | bytes 7372800 | tf_op jit(solution)/shard_map/transpose | solution.py:273
  13.9 0.6 stack.23.info.refs_0_
  14.6 6.9 %pack.1 = (f32[4,18,56,128]{3,2,1,0:T(8,128)}, f32[4,18,56,128]{3,2,1,0:T(8,128)}, f32[4,18,56,128]{3,2,1,0:T(8,128)}) custom-call(s32[5]{0:T(128)} %stack.23.info.refs_0_, f32[18,400,128]{2,1,0:T(8,128)} %bitcast.28), custom_call_target="tpu_custom_call" | custom-call | tf_op jit(solution)/shard_map/pack/pallas_call | solution.py:88
  21.4 2.5 %collective-permute-start.1 = (f32[4,18,56,128]{3,2,1,0:T(8,128)}, f32[4,18,56,128]{3,2,1,0:T(8,128)}, u32[]{:S(2)}, u32[]{:S(2)}) collective-permute-start(f32[4,18,56,128]{3,2,1,0:T(8,128)} %get-tuple-element.14), channel_id=1, source_target_pairs={{0,4},{4,12},{8,0},{12,20},{16,8},{20,28},{24,16},{28,36},{32,24},... | collective-permute-start | bytes 6193160 | tf_op jit(solution)/shard_map/ppermute | solution.py:278
  23.9 0.0 copy-start.3
  23.9 0.0 copy-start.2
  23.9 4.3 %all-to-all-start = ((f32[4,18,56,128]{3,2,1,0:T(8,128)}), f32[4,18,56,128]{3,2,1,0:T(8,128)S(1)}, u32[]{:S(2)}, u32[]{:S(2)}) async-start(f32[4,18,56,128]{3,2,1,0:T(8,128)} %get-tuple-element.13.refs_5_), calls=%async_computation | async-start | bytes 4128768 | tf_op jit(solution)/shard_map/all_to_all | solution.py:277
  28.2 0.3 collective-permute-start.2
  28.5 2.0 %collective-permute-start = (f32[4,18,56,128]{3,2,1,0:T(8,128)}, f32[4,18,56,128]{3,2,1,0:T(8,128)}, u32[]{:S(2)}, u32[]{:S(2)}) collective-permute-start(f32[4,18,56,128]{3,2,1,0:T(8,128)} %get-tuple-element.13.refs_5_), channel_id=1, source_target_pairs={{0,4},{4,0},{8,12},{12,8},{16,20},{20,16},{24,28},{28,24},{32,36},... | collective-permute-start | bytes 6193160 | tf_op jit(solution)/shard_map/ppermute | solution.py:280
  30.5 31.6 %collective-permute-done.1.refs_7_ = f32[4,18,56,128]{3,2,1,0:T(8,128)} collective-permute-done((f32[4,18,56,128]{3,2,1,0:T(8,128)}, f32[4,18,56,128]{3,2,1,0:T(8,128)}, u32[]{:S(2)}, u32[]{:S(2)}) %collective-permute-start.1) | collective-permute-done | bytes 2064416 | tf_op jit(solution)/shard_map/ppermute | solution.py:278
  62.1 7.4 %collective-permute-start.3 = (f32[4,18,56,128]{3,2,1,0:T(8,128)}, f32[4,18,56,128]{3,2,1,0:T(8,128)}, u32[]{:S(2)}, u32[]{:S(2)}) collective-permute-start(f32[4,18,56,128]{3,2,1,0:T(8,128)} %collective-permute-done.1.refs_7_), channel_id=1, source_target_pairs={{0,4},{4,0},{8,12},{12,8},{16,20},{20,16},{24,28},{28,24},{32,36},... | collective-permute-start | bytes 6193160 | tf_op jit(solution)/shard_map/ppermute | solution.py:290
  69.4 0.0 copy-done.3
  69.4 0.1 reduce-precision_subtract_fusion
  69.6 0.0 copy-start.4
  69.6 0.7 copy.20.d_ref
  70.3 0.0 copy-done.2
  70.3 0.2 reshape.45
  70.5 0.9 copy.18
  71.4 2.0 %prep.1 = (f32[4,224,128]{2,1,0:T(8,128)}, f32[224,128]{1,0:T(8,128)}, f32[224,128]{1,0:T(8,128)}) custom-call(s32[5]{0:T(128)} %stack.23.info.refs_0_, f32[800,128]{1,0:T(8,128)} %bitcast.33, f32[10,128]{1,0:T(8,128)} %bitcast.38), custom_call_target="tpu_custom_call" | custom-call | tf_op jit(solution)/shard_map/prep/pallas_call | solution.py:140
  73.4 0.7 pad_maximum_fusion.w_ref
  74.2 0.0 all-to-all-done
  74.2 0.0 copy-start
  74.2 1.3 copy-done
  75.5 7.1 %mix.1 = f32[72,56,128]{2,1,0:T(8,128)} custom-call(s32[5]{0:T(128)} %stack.23.info.refs_0_, f32[72,216]{1,0:T(8,128)} %pad_maximum_fusion.w_ref, f32[72,1]{1,0:T(8,128)} %copy.20.d_ref, f32[4,56,128]{2,1,0:T(8,128)} %bitcast.35, f32[72,56,128]{2,1,0:T(8,128)} %bitcast.29), custom_call_target="tpu_custom_call" | custom-call | tf_op jit(solution)/shard_map/mix/pallas_call | solution.py:173
  82.5 0.0 copy-done.4
  82.5 3.6 %all-to-all-start.1 = ((f32[4,18,56,128]{3,2,1,0:T(8,128)}), f32[4,18,56,128]{3,2,1,0:T(8,128)S(1)}, u32[]{:S(2)}, u32[]{:S(2)}) async-start(f32[4,18,56,128]{3,2,1,0:T(8,128)} %bitcast.30), calls=%async_computation.1 | async-start | bytes 4128768 | tf_op jit(solution)/shard_map/all_to_all | solution.py:289
  86.2 0.0 collective-permute-done.2.refs_8_
  86.2 0.0 collective-permute-done.refs_6_
  86.2 26.1 %all-to-all-done.1.refs_10_ = f32[4,18,56,128]{3,2,1,0:T(8,128)S(1)} async-done(((f32[4,18,56,128]{3,2,1,0:T(8,128)}), f32[4,18,56,128]{3,2,1,0:T(8,128)S(1)}, u32[]{:S(2)}, u32[]{:S(2)}) %all-to-all-start.1) | async-done | bytes 2064416 | tf_op jit(solution)/shard_map/all_to_all | solution.py:289
  112.3 0.0 copy-start.1
  112.3 0.0 collective-permute-done.3.refs_9_
  112.3 1.3 copy-done.1
  113.6 9.0 %last.1 = (f32[18,400,128]{2,1,0:T(8,128)}, f32[8,128]{1,0:T(8,128)}) custom-call(s32[5]{0:T(128)} %stack.23.info.refs_0_, f32[72]{0:T(128)} %copy-done.4, f32[4,4,56,128]{3,2,1,0:T(8,128)} %bitcast.34, f32[4,56,128]{2,1,0:T(8,128)} %bitcast.36, f32[4,56,128]{2,1,0:T(8,128)} %bitcast.37, f32[4,18,56,128]{3,2,1,0:T(8,128)} %get-tuple-element.13.refs_5_, ...), custom_call_target="tpu_custom_call" | custom-call | tf_op jit(solution)/shard_map/last/pallas_call | solution.py:230
  122.6 0.7 broadcast_in_dim.7
  123.3 16.5 %all_to_all.20 = f32[16,8,128]{2,1,0:T(8,128)S(1)} all-to-all(f32[16,8,128]{2,1,0:T(8,128)S(1)} %broadcast_in_dim.7), channel_id=1, replica_groups=mesh['ma_0'=4,'ma_1'=8,'ma_2'=2,'lev'=4] {'ma_1','ma_2'}, dimensions={0} | all-to-all | bytes 131072 | tf_op jit(solution)/shard_map/all_to_all | solution.py:262
  139.8 0.6 broadcast_in_dim.8
  140.4 4.7 %all-to-all-start.3 = ((f32[16,8,128]{2,1,0:T(8,128)}), f32[16,8,128]{2,1,0:T(8,128)S(1)}, u32[]{:S(2)}, u32[]{:S(2)}) async-start(f32[16,8,128]{2,1,0:T(8,128)} %broadcast_in_dim.8), calls=%async_computation.3 | async-start | bytes 131072 | tf_op jit(solution)/shard_map/all_to_all | solution.py:262
  145.1 5.4 %copy.23 = f32[18,20,10,2,128]{4,2,3,1,0:T(8,128)} copy(f32[18,20,10,2,128]{4,3,2,1,0:T(2,128)} %bitcast.31) | data formatting | bytes 7372800 | tf_op jit(solution)/shard_map/reshape | solution.py:292
  150.6 6.7 %reshape.56 = f32[18,2,20,1280]{3,1,2,0:T(2,128)} reshape(f32[18,2,20,10,128]{4,3,1,2,0:T(8,128)} %bitcast.26) | data formatting | bytes 7372800 | tf_op jit(solution)/shard_map/reshape | solution.py:292
  157.3 0.0 all-to-all-done.3
  157.3 0.6 sqrt_reduce_fusion
  (2 shorter events, 0.0 us)
Async XLA Ops:
  21.4 40.6 %collective-permute-start.1 = (f32[4,18,56,128]{3,2,1,0:T(8,128)}, f32[4,18,56,128]{3,2,1,0:T(8,128)}, u32[]{:S(2)}, u32[]{:S(2)}) collective-permute-start(f32[4,18,56,128]{3,2,1,0:T(8,128)} %get-tuple-element.14), channel_id=1, source_target_pairs={{0,4},{4,12},{8,0},{12,20},{16,8},{20,28},{24,16},{28,36},{32,24},... | collective-permute-start | bytes 6193160 | tf_op jit(solution)/shard_map/ppermute | solution.py:278
  23.9 45.6 %copy-start.3 = (f32[72,72]{1,0:T(8,128)S(1)}, f32[72,72]{1,0:T(8,128)}, u32[]{:S(2)}) copy-start(f32[72,72]{1,0:T(8,128)} %param.7) | copy-start | bytes 62212
  23.9 46.4 %copy-start.2 = (f32[4,20,1280]{2,0,1:T(4,128)S(1)}, f32[4,20,1280]{2,0,1:T(4,128)}, u32[]{:S(2)}) copy-start(f32[4,20,1280]{2,0,1:T(4,128)} %param.5) | copy-start | bytes 1228804
  23.9 50.3 %all-to-all-start = ((f32[4,18,56,128]{3,2,1,0:T(8,128)}), f32[4,18,56,128]{3,2,1,0:T(8,128)S(1)}, u32[]{:S(2)}, u32[]{:S(2)}) async-start(f32[4,18,56,128]{3,2,1,0:T(8,128)} %get-tuple-element.13.refs_5_), calls=%async_computation | async-start | bytes 4128768 | tf_op jit(solution)/shard_map/all_to_all | solution.py:277
  28.2 58.0 %collective-permute-start.2 = (f32[4,18,56,128]{3,2,1,0:T(8,128)}, f32[4,18,56,128]{3,2,1,0:T(8,128)}, u32[]{:S(2)}, u32[]{:S(2)}) collective-permute-start(f32[4,18,56,128]{3,2,1,0:T(8,128)} %get-tuple-element.15), channel_id=1, source_target_pairs={{0,8},{4,0},{8,16},{12,4},{16,24},{20,12},{24,32},{28,20},{32,40},... | collective-permute-start | bytes 6193160 | tf_op jit(solution)/shard_map/ppermute | solution.py:279
  28.5 57.7 %collective-permute-start = (f32[4,18,56,128]{3,2,1,0:T(8,128)}, f32[4,18,56,128]{3,2,1,0:T(8,128)}, u32[]{:S(2)}, u32[]{:S(2)}) collective-permute-start(f32[4,18,56,128]{3,2,1,0:T(8,128)} %get-tuple-element.13.refs_5_), channel_id=1, source_target_pairs={{0,4},{4,0},{8,12},{12,8},{16,20},{20,16},{24,28},{28,24},{32,36},... | collective-permute-start | bytes 6193160 | tf_op jit(solution)/shard_map/ppermute | solution.py:280
  62.1 50.2 %collective-permute-start.3 = (f32[4,18,56,128]{3,2,1,0:T(8,128)}, f32[4,18,56,128]{3,2,1,0:T(8,128)}, u32[]{:S(2)}, u32[]{:S(2)}) collective-permute-start(f32[4,18,56,128]{3,2,1,0:T(8,128)} %collective-permute-done.1.refs_7_), channel_id=1, source_target_pairs={{0,4},{4,0},{8,12},{12,8},{16,20},{20,16},{24,28},{28,24},{32,36},... | collective-permute-start | bytes 6193160 | tf_op jit(solution)/shard_map/ppermute | solution.py:290
  69.6 13.0 %copy-start.4 = (f32[72]{0:T(128)}, f32[72]{0:T(128)S(1)}, u32[]{:S(2)}) copy-start(f32[72]{0:T(128)S(1)} %get-tuple-element.19.refs_1_) | copy-start | bytes 868
  74.2 1.3 copy-start
  82.5 29.7 %all-to-all-start.1 = ((f32[4,18,56,128]{3,2,1,0:T(8,128)}), f32[4,18,56,128]{3,2,1,0:T(8,128)S(1)}, u32[]{:S(2)}, u32[]{:S(2)}) async-start(f32[4,18,56,128]{3,2,1,0:T(8,128)} %bitcast.30), calls=%async_computation.1 | async-start | bytes 4128768 | tf_op jit(solution)/shard_map/all_to_all | solution.py:289
  112.3 1.3 copy-start.1
  140.4 16.9 %all-to-all-start.3 = ((f32[16,8,128]{2,1,0:T(8,128)}), f32[16,8,128]{2,1,0:T(8,128)S(1)}, u32[]{:S(2)}, u32[]{:S(2)}) async-start(f32[16,8,128]{2,1,0:T(8,128)} %broadcast_in_dim.8), calls=%async_computation.3 | async-start | bytes 131072 | tf_op jit(solution)/shard_map/all_to_all | solution.py:262

commit v2 on v1

v2 whole, which is shorter than its diff:
```python
import jax
import jax.numpy as jnp
from jax import lax
from jax.experimental import pallas as pl
from jax.experimental.pallas import tpu as pltpu
from jax.sharding import Mesh
from jax.sharding import PartitionSpec as P

LEV = 72
WAVES = 1280
OWNERS = 64
FOLDS = 20
TILES = 10
HALF = 112
QROWS = 56
OWN = 18
MA = ("ma_0", "ma_1", "ma_2")
F32 = jnp.float32


def start_row(t):
    return 20 * t - t * (t - 1)


def cut(moves):
    out = []
    for s, d, n in moves:
        while n:
            step = min(n, QROWS - d % QROWS, QROWS - s % QROWS)
            out.append((s, d, step))
            s, d, n = s + step, d + step, n - step
    return out


LIVE = [
    (2 * t + par, j, par * HALF + start_row(t) + 2 * (j - t)) for par in range(2) for t in range(TILES) for j in range(t, TILES)
]
DOWN = cut(
    [(start_row(t + 1), HALF + start_row(t) + 2, 18 - 2 * t) for t in range(TILES - 1)]
    + [(HALF + start_row(t - 1) + 2, start_row(t), 20 - 2 * t) for t in range(1, TILES)]
)


def pack_kernel(x_ref, p_ref):
    for fold, j, row in LIVE:
        q, r = divmod(row, QROWS)
        p_ref[q, :, r : r + 2, :] = x_ref[:, fold, :, 128 * j : 128 * j + 128]
    for q in (1, 3):
        p_ref[q, :, QROWS - 2 :, :] = jnp.zeros((p_ref.shape[1], 2, 128), F32)


def pack(x):
    tl = 3
    return pl.pallas_call(
        pack_kernel,
        out_shape=jax.ShapeDtypeStruct((4, OWN, QROWS, 128), F32),
        grid=(OWN // tl,),
        in_specs=[pl.BlockSpec((tl, FOLDS, 2, WAVES), lambda i: (i, 0, 0, 0))],
        out_specs=pl.BlockSpec((4, tl, QROWS, 128), lambda i: (0, i, 0, 0)),
        name="pack",
    )(x)


BASES = (1, 2, -2, -1)
PLACE = {-2: 0, -1: 1, 1: 2, 2: 3}


def prep_kernel(info, c_ref, h_ref, ck_ref, hp_ref, live_ref):
    owner = info[0]
    odd = info[1]
    for par in range(2):
        for t in range(TILES):
            fold = 2 * t + par
            n = TILES - t
            at = par * HALF + start_row(t)
            wave = fold * OWNERS + (owner if par == 0 else OWNERS - 1 - owner)
            col = lax.broadcasted_iota(jnp.int32, (n, 128), 0) * 128 + lax.broadcasted_iota(jnp.int32, (n, 128), 1) + 128 * t
            live = jnp.where(col >= wave, 1.0, 0.0).astype(F32)
            h = h_ref[t:TILES, :]
            for part in range(2):
                live_ref[pl.ds(at + part, n, stride=2), :] = live
                hp_ref[pl.ds(at + part, n, stride=2), :] = h
            for a, base in enumerate(BASES):
                s_even = base * (1 if par == 0 else -1)
                shift = jnp.where(odd == 1, -s_even, s_even)
                place = jnp.where(odd == 1, PLACE[-s_even], PLACE[s_even])
                low = jnp.where(wave + shift < 0, 2 * WAVES, jnp.maximum(wave, wave + shift))
                c = c_ref[pl.ds((fold * TILES + t) * 4 + place, n, stride=4), :]
                c = jnp.where(col >= low, c, 0.0)
                for part in range(2):
                    ck_ref[a, pl.ds(at + part, n, stride=2), :] = c
        pad = pl.ds(par * HALF + 110, 2)
        zero = jnp.zeros((2, 128), F32)
        live_ref[pad, :] = zero
        hp_ref[pad, :] = zero
        for a in range(4):
            ck_ref[a, pad, :] = zero


def prep(info, c, h):
    rows = jax.ShapeDtypeStruct((2 * HALF, 128), F32)
    vmem = pl.BlockSpec(memory_space=pltpu.VMEM)
    return pl.pallas_call(
        prep_kernel,
        out_shape=(jax.ShapeDtypeStruct((4, 2 * HALF, 128), F32), rows, rows),
        in_specs=[pl.BlockSpec(memory_space=pltpu.SMEM), vmem, vmem],
        out_specs=(vmem, vmem, vmem),
        name="prep",
    )(info, c, h)


def mix_kernel(info, w_ref, d_ref, h_ref, x_ref, o_ref):
    w = w_ref[...].astype(jnp.bfloat16)
    d = d_ref[...]
    x2 = x_ref.reshape(LEV * 8, 128)
    o2 = o_ref.reshape(LEV * 8, 128)
    for r in range(0, 8, 2):
        h = h_ref[0, r : r + 1, :]
        scale = 1.0 / (1.0 + h * d)
        highs, lows = [], []
        for e in range(2):
            f = x2[pl.ds(r + e, LEV, stride=8), :] * scale
            high = f.astype(jnp.bfloat16).astype(F32)
            highs.append(high)
            lows.append(f - high)
        high = jnp.concatenate(highs, axis=1)
        low = jnp.concatenate(lows, axis=1)
        both = jnp.concatenate([high, high, low], axis=0).astype(jnp.bfloat16)
        out = jnp.dot(w, both, preferred_element_type=F32)
        for e in range(2):
            o2[pl.ds(r + e, LEV, stride=8), :] = out[:, e * 128 : (e + 1) * 128] * h


def mix(info, w3, diag, hp, x):
    return pl.pallas_call(
        mix_kernel,
        out_shape=jax.ShapeDtypeStruct((LEV, QROWS, 128), F32),
        grid_spec=pltpu.PrefetchScalarGridSpec(
            num_scalar_prefetch=1,
            grid=(QROWS // 8,),
            in_specs=[
                pl.BlockSpec((LEV, 3 * LEV), lambda i, s: (0, 0)),
                pl.BlockSpec((LEV, 1), lambda i, s: (0, 0)),
                pl.BlockSpec((1, 8, 128), lambda i, s: (s[2], i, 0)),
                pl.BlockSpec((LEV, 8, 128), lambda i, s: (0, i, 0)),
            ],
            out_specs=pl.BlockSpec((LEV, 8, 128), lambda i, s: (0, i, 0)),
        ),
        name="mix",
    )(info, w3, diag, hp, x)


def fold_sum(acc, slot, value):
    acc[slot] += jnp.sum((value * value).reshape(QROWS // 8, 8, 128), axis=0)


def near_kernel(tl, info, d_ref, ck_ref, hp_ref, live_ref, p_ref, q_ref, x_ref, y_ref, z_ref, o_ref, s_ref, fix):
    step = pl.program_id(0)
    received = (x_ref, y_ref, z_ref)

    @pl.when(step == 0)
    def _():
        s_ref[...] = jnp.zeros_like(s_ref)
        fix[...] = jnp.zeros_like(fix)

    def one(l, get):
        d = d_ref[info[2] * OWN + step * tl + l]
        for q in range(4):
            live = live_ref[q]
            v = p_ref[q, l] * live
            scale = 1.0 / (1.0 + hp_ref[q] * d)
            near = ck_ref[0, q] * q_ref[q, l] + v
            for a in range(3):
                near = near + ck_ref[a + 1, q] * get(a, q)
            o_ref[q, l] = v - scale * near * live
            fold_sum(s_ref, 0, v)

    @pl.when(info[0] > 1)
    def _():
        def level(l, _):
            one(l, lambda a, q: received[a][jnp.where(info[3 + a] == 1, q ^ 2, q), l])
            return 0

        lax.fori_loop(0, tl, level, 0)

    @pl.when(info[0] <= 1)
    def _():
        def level(l, _):
            for a in range(3):

                @pl.when(info[3 + a] == 2)
                def _():
                    for s, t, n in DOWN:
                        fix[a, t // QROWS, t % QROWS : t % QROWS + n, :] = received[a][s // QROWS, l, s % QROWS : s % QROWS + n, :]

                @pl.when(info[3 + a] != 2)
                def _():
                    fix[a] = received[a][:, l]

            one(l, lambda a, q: fix[a, q])
            return 0

        lax.fori_loop(0, tl, level, 0)


def whole(shape):
    return pl.BlockSpec(shape, lambda i, s: (0,) * len(shape))


def near(info, diag, ck, hp, live, p, q, x, y, z):
    tl = 3
    block = pl.BlockSpec((4, tl, QROWS, 128), lambda i, s: (0, i, 0, 0))
    return pl.pallas_call(
        lambda *refs: near_kernel(tl, *refs),
        out_shape=(jax.ShapeDtypeStruct((4, OWN, QROWS, 128), F32), jax.ShapeDtypeStruct((1, 8, 128), F32)),
        grid_spec=pltpu.PrefetchScalarGridSpec(
            num_scalar_prefetch=1,
            grid=(OWN // tl,),
            in_specs=[
                pl.BlockSpec(memory_space=pltpu.SMEM),
                whole((4, 4, QROWS, 128)),
                whole((4, QROWS, 128)),
                whole((4, QROWS, 128)),
            ]
            + [block] * 5,
            out_specs=[block, whole((1, 8, 128))],
            scratch_shapes=[pltpu.VMEM((3, 4, QROWS, 128), F32)],
        ),
        name="near",
    )(info, diag, ck, hp, live, p, q, x, y, z)


def last_kernel(tl, info, d_ref, v_sum, hp_ref, live_ref, p_ref, part_ref, m_ref, o_ref, s_ref, buf, acc):
    step = pl.program_id(0)

    @pl.when(step == 0)
    def _():
        acc[...] = jnp.zeros_like(acc)

    for l in range(tl):
        d = d_ref[info[2] * OWN + step * tl + l]
        for q in range(4):
            live = live_ref[q]
            scale = 1.0 / (1.0 + hp_ref[q] * d)
            residual = part_ref[q, l] - m_ref[q, l] * live
            buf[l, q * QROWS : (q + 1) * QROWS, :] = scale * (p_ref[q, l] * live + residual)
            fold_sum(acc, 0, residual)
    for t in range(1, TILES):
        for par in range(2):
            o_ref[:, 2 * t + par, :, : 128 * t] = jnp.zeros((tl, 2, 128 * t), F32)
    for fold, j, row in LIVE:
        o_ref[:, fold, :, 128 * j : 128 * j + 128] = buf[:, row : row + 2, :]

    @pl.when(step == pl.num_programs(0) - 1)
    def _():
        row = lax.broadcasted_iota(jnp.int32, (8, 128), 0)
        s_ref[...] = jnp.where(row == 0, jnp.sum(v_sum[0]), jnp.sum(acc[0]))


def last(info, diag, v_sum, hp, live, p, part, m):
    tl = 3
    block = pl.BlockSpec((4, tl, QROWS, 128), lambda i, s: (0, i, 0, 0))
    return pl.pallas_call(
        lambda *refs: last_kernel(tl, *refs),
        out_shape=(jax.ShapeDtypeStruct((OWN, FOLDS, 2, WAVES), F32), jax.ShapeDtypeStruct((8, 128), F32)),
        grid_spec=pltpu.PrefetchScalarGridSpec(
            num_scalar_prefetch=1,
            grid=(OWN // tl,),
            in_specs=[
                pl.BlockSpec(memory_space=pltpu.SMEM),
                whole((1, 8, 128)),
                whole((4, QROWS, 128)),
                whole((4, QROWS, 128)),
            ]
            + [block] * 3,
            out_specs=[pl.BlockSpec((tl, FOLDS, 2, WAVES), lambda i, s: (i, 0, 0, 0)), whole((8, 128))],
            scratch_shapes=[pltpu.VMEM((tl, 2 * HALF, 128), F32), pltpu.VMEM((1, 8, 128), F32)],
        ),
        name="last",
    )(info, diag, v_sum, hp, live, p, part, m)


def routes(owners):
    x, y = [], []
    for o in range(owners):
        down = o - 2 if o >= 2 else 1 - o
        up = o + 2 if o + 2 < owners else 2 * owners - 1 - (o + 2)
        x.append((o, down if o % 2 == 0 else up))
        y.append((o, up if o % 2 == 0 else down))
    return x, y, [(o, o ^ 1) for o in range(owners)]


def total(value, axes):
    n = lax.axis_size(axes)
    every = lax.all_to_all(jnp.broadcast_to(value[None], (n,) + value.shape), axes, 0, 0, tiled=True)
    return jnp.sum(every, axis=0)


def body(forcing, coupling, helmholtz, vertical):
    owner = lax.axis_index(MA).astype(jnp.int32)
    lev = lax.axis_index("lev").astype(jnp.int32)
    ends = {"x": (1, OWNERS - 2), "y": (0, OWNERS - 1), "z": (0, OWNERS - 1)}
    modes = [jnp.where(owner == low, 2, jnp.where(owner == high, 1, 0)) for low, high in ends.values()]
    info = jnp.stack([owner, owner & 1, lev] + modes).astype(jnp.int32)
    crows = coupling.reshape(4, FOLDS, TILES, 128).transpose(1, 2, 0, 3).reshape(800, 128)
    p = pack(forcing.transpose(0, 2, 1, 3))
    to_x, to_y, swap = routes(OWNERS)
    every = lax.all_to_all(p, "lev", 0, 0, tiled=True).reshape(LEV, QROWS, 128)
    x = lax.ppermute(p, MA, to_x)
    y = lax.ppermute(p, MA, to_y)
    q = lax.ppermute(p, MA, swap)
    ck, hp, live = prep(info, crows, helmholtz.reshape(TILES, 128))
    ck = ck.reshape(4, 4, QROWS, 128)
    hp = hp.reshape(4, QROWS, 128)
    live = live.reshape(4, QROWS, 128)
    diag = jnp.sum(vertical * jnp.eye(LEV, dtype=F32), axis=1)
    high = lax.reduce_precision(vertical, 8, 7)
    w3 = jnp.concatenate([high, vertical - high, high], axis=1)
    m = mix(info, w3, diag[:, None], hp, every).reshape(4, OWN, QROWS, 128)
    x, m = lax.optimization_barrier((x, m))
    m = lax.all_to_all(m, "lev", 0, 0, tiled=True)
    z = lax.ppermute(x, MA, swap)
    part, v_sum = near(info, diag, ck, hp, live, p, q, x, y, z)
    part, m = lax.optimization_barrier((part, m))
    rows, sums = last(info, diag, v_sum, hp, live, p, part, m)
    sums = total(total(sums, ("ma_1", "ma_2")), ("ma_0", "lev"))
    norms = jnp.sqrt(sums[:2, 0] / (LEV * WAVES * (WAVES + 1)))
    return (rows.transpose(0, 2, 1, 3), norms)


def solution(mesh):
    split = Mesh(mesh.devices.reshape(4, 8, 2, mesh.shape["lev"]), ("ma_0", "ma_1", "ma_2", "lev"))
    return jax.shard_map(
        body,
        mesh=split,
        in_specs=(P("lev", None, MA, None), P(None, MA, None), P(), P()),
        out_specs=(P("lev", None, MA, None), P()),
        check_vma=False,
    )
```

time: 159 us -> 121 us (0.76)
  local copies, waits for them, and re-layouts: 31.8 us -> 3.1 us
  waiting for transfers between devices: 57.7 us -> 35.7 us
  blocking collectives: 16.5 us -> 26.8 us
  Pallas kernels: 25 us -> 29.7 us
  starting transfers between devices: 24.8 us -> 22.3 us
    ppermute x2, waiting for transfers between devices: 31.6 us -> 1.05 us  [the longest x1 1.04 us: body(): x = lax.ppermute(p, MA, to_x)]
    reshape x3 -> x0, local copies, waits for them, and re-layouts: 19 us -> none  [the longest x2 12.2 us: body(): rows.reshape(OWN, FOLDS, TILES, 2, 128).transpose(0, 3, 1, 2, 4)]
    all_to_all x1, waiting for transfers between devices: 0.01 us -> 16.9 us  [body(): every = lax.all_to_all(p, 'lev', 0, 0, tiled=True).reshape(LEV, QROWS, 128)]
    all_to_all x1 -> x2, blocking collectives: 16.5 us -> 26.8 us  [total(): lax.all_to_all(jnp.broadcast_to(value[None], (n,) + value.shape), axes, 0...]
    all_to_all x1, waiting for transfers between devices: 26.1 us -> 17.7 us  [body(): m = lax.all_to_all(m, 'lev', 0, 0, tiled=True)]
    pallas_call x1 -> x2, Pallas kernels: 6.85 us -> 13.6 us  [the longest x1 8.43 us: near(): pl.pallas_call(lambda *refs: near_kernel(tl, *refs), out_shape=(jax.Shape...]
    transpose x1 -> x0, local copies, waits for them, and re-layouts: 6.43 us -> none  [body(): forcing.reshape(OWN, 2, FOLDS, TILES, 128).transpose(0, 2, 3, 1, 4)]
    all_to_all x1 -> x0, starting transfers between devices: 4.73 us -> none  [total(): lax.all_to_all(jnp.broadcast_to(value[None], (n,) + value.shape), axes, 0...]
  transfers between devices with their start and end apart: 7 -> 6, of which waited for: 2 -> 3; matrix products, arithmetic and copies ran while one was open for 9% -> 3% of each run, Pallas kernels for 6% -> 15%
where the time goes in v2:
time: 121 us; the launch traced here: 120 us
  waiting for transfers between devices  35.7 us (30%)
  Pallas kernels  29.7 us (25%)
  blocking collectives  26.8 us (22%)
  starting transfers between devices  22.3 us (18%)
  local copies, waits for them, and re-layouts  3.1 us (3%)
  other arithmetic  1.51 us (1%)
    all_to_all x2, blocking collectives, total(): lax.all_to_all(jnp.broadcast_to(value[None], (n,) + value.shape), axes, 0...  26.8 us
    all_to_all x1, waiting for transfers between devices, body(): m = lax.all_to_all(m, 'lev', 0, 0, tiled=True)  17.7 us
    all_to_all x1, waiting for transfers between devices, body(): every = lax.all_to_all(p, 'lev', 0, 0, tiled=True).reshape(LEV, QROWS, 128)  16.9 us
    pallas_call x1, Pallas kernels, near(): pl.pallas_call(lambda *refs: near_kernel(tl, *refs), out_shape=(jax.Shape...  8.43 us
    ppermute x1, starting transfers between devices, body(): z = lax.ppermute(x, MA, swap)  7.88 us
    pallas_call x1, Pallas kernels, last(): pl.pallas_call(lambda *refs: last_kernel(tl, *refs), out_shape=(jax.Shape...  7.18 us
    pallas_call x1, Pallas kernels, mix(): pl.pallas_call(mix_kernel, out_shape=jax.ShapeDtypeStruct((LEV, QROWS, 12...  6.95 us
    pallas_call x1, Pallas kernels, pack(): pl.pallas_call(pack_kernel, out_shape=jax.ShapeDtypeStruct((4, OWN, QROWS...  5.14 us
  transfers between devices with their start and end apart: 6, of which 3 were waited for; matrix products, arithmetic and copies ran while one was open for 3% of the time, Pallas kernels for 15%

profile of v2, /device:TPU:1, one launch (start us, length us, event | category | flops | bytes accessed | tf_op | source)
XLA Modules:
  0.0 119.9 jit_solution(4340985379082951257)
XLA Ops:
  0.6 5.1 %pack.1.refs_5_ = f32[4,18,56,128]{3,2,1,0:T(8,128)} custom-call(f32[18,20,2,1280]{3,2,1,0:T(2,128)} %bitcast.19), custom_call_target="tpu_custom_call" | custom-call | tf_op jit(solution)/shard_map/pack/pallas_call | solution.py:54
  5.8 0.0 copy-start
  5.8 0.0 copy-start.2
  5.8 0.0 copy-start.1
  5.8 2.5 %collective-permute-start.1 = (f32[4,18,56,128]{3,2,1,0:T(8,128)}, f32[4,18,56,128]{3,2,1,0:T(8,128)}, u32[]{:S(2)}, u32[]{:S(2)}) collective-permute-start(f32[4,18,56,128]{3,2,1,0:T(8,128)} %pack.1.refs_5_), channel_id=1, source_target_pairs={{0,4},{4,12},{8,0},{12,20},{16,8},{20,28},{24,16},{28,36},{32,24},... | collective-permute-start | bytes 6193160 | tf_op jit(solution)/shard_map/ppermute | solution.py:309
  8.3 4.5 %all-to-all-start = ((f32[4,18,56,128]{3,2,1,0:T(8,128)}), f32[4,18,56,128]{3,2,1,0:T(8,128)}, u32[]{:S(2)}, u32[]{:S(2)}) async-start(f32[4,18,56,128]{3,2,1,0:T(8,128)} %pack.1.refs_5_), calls=%async_computation | async-start | bytes 4128768 | tf_op jit(solution)/shard_map/all_to_all | solution.py:308
  12.8 0.0 copy-done
  12.8 1.0 collective-permute-start.2
  13.8 1.9 %collective-permute-start = (f32[4,18,56,128]{3,2,1,0:T(8,128)S(1)}, f32[4,18,56,128]{3,2,1,0:T(8,128)}, u32[]{:S(2)}, u32[]{:S(2)}) collective-permute-start(f32[4,18,56,128]{3,2,1,0:T(8,128)S(1)} %copy-done), channel_id=1, source_target_pairs={{0,4},{4,0},{8,12},{12,8},{16,20},{20,16},{24,28},{28,24},{32,36},... | collective-permute-start | bytes 6193160 | tf_op jit(solution)/shard_map/ppermute | solution.py:311
  15.7 0.0 copy-done.2
  15.7 0.1 reduce-precision_subtract_fusion
  15.8 0.0 copy-start.3
  15.8 0.7 copy.13.d_ref
  16.5 0.0 copy-done.1
  16.5 0.2 reshape.33
  16.7 0.9 copy.12
  17.7 0.6 stack.24.info.refs_0_
  18.2 2.1 %prep.1 = (f32[4,224,128]{2,1,0:T(8,128)}, f32[224,128]{1,0:T(8,128)}, f32[224,128]{1,0:T(8,128)}) custom-call(s32[6]{0:T(128)} %stack.24.info.refs_0_, f32[800,128]{1,0:T(8,128)} %bitcast.21, f32[10,128]{1,0:T(8,128)} %bitcast.29), custom_call_target="tpu_custom_call" | custom-call | tf_op jit(solution)/shard_map/prep/pallas_call | solution.py:103
  20.3 0.7 pad_maximum_fusion.w_ref
  21.0 16.9 %all-to-all-done = f32[4,18,56,128]{3,2,1,0:T(8,128)} async-done(((f32[4,18,56,128]{3,2,1,0:T(8,128)}), f32[4,18,56,128]{3,2,1,0:T(8,128)}, u32[]{:S(2)}, u32[]{:S(2)}) %all-to-all-start) | async-done | bytes 2064416 | tf_op jit(solution)/shard_map/all_to_all | solution.py:308
  38.0 6.9 %mix.1 = f32[72,56,128]{2,1,0:T(8,128)} custom-call(s32[6]{0:T(128)} %stack.24.info.refs_0_, f32[72,216]{1,0:T(8,128)} %pad_maximum_fusion.w_ref, f32[72,1]{1,0:T(8,128)} %copy.13.d_ref, f32[4,56,128]{2,1,0:T(8,128)} %bitcast.22, f32[72,56,128]{2,1,0:T(8,128)} %bitcast.13.x_ref), custom_call_target="tpu_custom_call" | custom-call | tf_op jit(solution)/shard_map/mix/pallas_call | solution.py:135
  44.9 0.0 copy-done.3
  44.9 1.0 collective-permute-done.1.refs_7_
  46.0 7.9 %collective-permute-start.3 = (f32[4,18,56,128]{3,2,1,0:T(8,128)}, f32[4,18,56,128]{3,2,1,0:T(8,128)}, u32[]{:S(2)}, u32[]{:S(2)}) collective-permute-start(f32[4,18,56,128]{3,2,1,0:T(8,128)} %collective-permute-done.1.refs_7_), channel_id=1, source_target_pairs={{0,4},{4,0},{8,12},{12,8},{16,20},{20,16},{24,28},{28,24},{32,36},... | collective-permute-start | bytes 6193160 | tf_op jit(solution)/shard_map/ppermute | solution.py:322
  53.8 4.5 %all-to-all-start.1 = ((f32[4,18,56,128]{3,2,1,0:T(8,128)}), f32[4,18,56,128]{3,2,1,0:T(8,128)}, u32[]{:S(2)}, u32[]{:S(2)}) async-start(f32[4,18,56,128]{3,2,1,0:T(8,128)} %bitcast.18), calls=%async_computation.1 | async-start | bytes 4128768 | tf_op jit(solution)/shard_map/all_to_all | solution.py:321
  58.3 0.0 collective-permute-done.2.refs_8_
  58.3 0.0 collective-permute-done.refs_6_
  58.4 0.0 collective-permute-done.3.refs_9_
  58.4 8.4 %near.1 = (f32[4,18,56,128]{3,2,1,0:T(8,128)}, f32[1,8,128]{2,1,0:T(8,128)}) custom-call(s32[6]{0:T(128)} %stack.24.info.refs_0_, f32[72]{0:T(128)} %copy-done.3, f32[4,4,56,128]{3,2,1,0:T(8,128)} %bitcast.27, f32[4,56,128]{2,1,0:T(8,128)} %bitcast.23, f32[4,56,128]{2,1,0:T(8,128)} %bitcast.25, f32[4,18,56,128]{3,2,1,0:T(8,128)} %pack.1.refs_5_, ...), custom_call_target="tpu_custom_call" | custom-call | tf_op jit(solution)/shard_map/near/pallas_call | solution.py:213
  66.8 17.7 %all-to-all-done.1.refs_7_ = f32[4,18,56,128]{3,2,1,0:T(8,128)} async-done(((f32[4,18,56,128]{3,2,1,0:T(8,128)}), f32[4,18,56,128]{3,2,1,0:T(8,128)}, u32[]{:S(2)}, u32[]{:S(2)}) %all-to-all-start.1) | async-done | bytes 2064416 | tf_op jit(solution)/shard_map/all_to_all | solution.py:321
  84.5 7.2 %last.1 = (f32[18,20,2,1280]{3,2,1,0:T(2,128)}, f32[8,128]{1,0:T(8,128)}) custom-call(s32[6]{0:T(128)} %stack.24.info.refs_0_, f32[72]{0:T(128)} %copy-done.3, f32[1,8,128]{2,1,0:T(8,128)} %get-tuple-element.17.refs_2_, f32[4,56,128]{2,1,0:T(8,128)} %bitcast.24, f32[4,56,128]{2,1,0:T(8,128)} %bitcast.26, f32[4,18,56,128]{3,2,1,0:T(8,128)} %pack.1.refs_5_, ...), custom_call_target="tpu_custom_call" | custom-call | tf_op jit(solution)/shard_map/last/pallas_call | solution.py:263
  91.7 0.7 broadcast_in_dim.7
  92.4 15.8 %all_to_all.20 = f32[16,8,128]{2,1,0:T(8,128)S(1)} all-to-all(f32[16,8,128]{2,1,0:T(8,128)S(1)} %broadcast_in_dim.7), channel_id=1, replica_groups=mesh['ma_0'=4,'ma_1'=8,'ma_2'=2,'lev'=4] {'ma_1','ma_2'}, dimensions={0} | all-to-all | bytes 131072 | tf_op jit(solution)/shard_map/all_to_all | solution.py:295
  108.2 11.0 %all_to_all.21 = f32[16,8,128]{2,1,0:T(8,128)S(1)} all-to-all(f32[16,8,128]{2,1,0:T(8,128)S(1)} %broadcast_in_dim.8), channel_id=1, replica_groups=mesh['ma_0'=4,'ma_1'=8,'ma_2'=2,'lev'=4] {'ma_0','lev'}, dimensions={0} | all-to-all | bytes 131072 | tf_op jit(solution)/shard_map/all_to_all | solution.py:295
  119.3 0.6 sqrt_reduce_fusion
  (3 shorter events, 0.0 us)
Async XLA Ops:
  5.8 7.0 %copy-start = (f32[4,18,56,128]{3,2,1,0:T(8,128)S(1)}, f32[4,18,56,128]{3,2,1,0:T(8,128)}, u32[]{:S(2)}) copy-start(f32[4,18,56,128]{3,2,1,0:T(8,128)} %pack.1.refs_5_) | copy-start | bytes 6193156
  5.8 9.9 %copy-start.2 = (f32[72,72]{1,0:T(8,128)S(1)}, f32[72,72]{1,0:T(8,128)}, u32[]{:S(2)}) copy-start(f32[72,72]{1,0:T(8,128)} %param.7) | copy-start | bytes 62212
  5.8 10.8 %copy-start.1 = (f32[4,20,1280]{2,0,1:T(4,128)S(1)}, f32[4,20,1280]{2,0,1:T(4,128)}, u32[]{:S(2)}) copy-start(f32[4,20,1280]{2,0,1:T(4,128)} %param.5) | copy-start | bytes 1228804
  5.8 40.2 %collective-permute-start.1 = (f32[4,18,56,128]{3,2,1,0:T(8,128)}, f32[4,18,56,128]{3,2,1,0:T(8,128)}, u32[]{:S(2)}, u32[]{:S(2)}) collective-permute-start(f32[4,18,56,128]{3,2,1,0:T(8,128)} %pack.1.refs_5_), channel_id=1, source_target_pairs={{0,4},{4,12},{8,0},{12,20},{16,8},{20,28},{24,16},{28,36},{32,24},... | collective-permute-start | bytes 6193160 | tf_op jit(solution)/shard_map/ppermute | solution.py:309
  8.3 29.6 %all-to-all-start = ((f32[4,18,56,128]{3,2,1,0:T(8,128)}), f32[4,18,56,128]{3,2,1,0:T(8,128)}, u32[]{:S(2)}, u32[]{:S(2)}) async-start(f32[4,18,56,128]{3,2,1,0:T(8,128)} %pack.1.refs_5_), calls=%async_computation | async-start | bytes 4128768 | tf_op jit(solution)/shard_map/all_to_all | solution.py:308
  12.8 45.5 %collective-permute-start.2 = (f32[4,18,56,128]{3,2,1,0:T(8,128)S(1)}, f32[4,18,56,128]{3,2,1,0:T(8,128)}, u32[]{:S(2)}, u32[]{:S(2)}) collective-permute-start(f32[4,18,56,128]{3,2,1,0:T(8,128)S(1)} %copy-done), channel_id=1, source_target_pairs={{0,8},{4,0},{8,16},{12,4},{16,24},{20,12},{24,32},{28,20},{32,40},... | collective-permute-start | bytes 6193160 | tf_op jit(solution)/shard_map/ppermute | solution.py:310
  13.8 44.5 %collective-permute-start = (f32[4,18,56,128]{3,2,1,0:T(8,128)S(1)}, f32[4,18,56,128]{3,2,1,0:T(8,128)}, u32[]{:S(2)}, u32[]{:S(2)}) collective-permute-start(f32[4,18,56,128]{3,2,1,0:T(8,128)S(1)} %copy-done), channel_id=1, source_target_pairs={{0,4},{4,0},{8,12},{12,8},{16,20},{20,16},{24,28},{28,24},{32,36},... | collective-permute-start | bytes 6193160 | tf_op jit(solution)/shard_map/ppermute | solution.py:311
  15.8 29.1 %copy-start.3 = (f32[72]{0:T(128)}, f32[72]{0:T(128)S(1)}, u32[]{:S(2)}) copy-start(f32[72]{0:T(128)S(1)} %get-tuple-element.25.refs_1_) | copy-start | bytes 868
  46.0 12.4 %collective-permute-start.3 = (f32[4,18,56,128]{3,2,1,0:T(8,128)}, f32[4,18,56,128]{3,2,1,0:T(8,128)}, u32[]{:S(2)}, u32[]{:S(2)}) collective-permute-start(f32[4,18,56,128]{3,2,1,0:T(8,128)} %collective-permute-done.1.refs_7_), channel_id=1, source_target_pairs={{0,4},{4,0},{8,12},{12,8},{16,20},{20,16},{24,28},{28,24},{32,36},... | collective-permute-start | bytes 6193160 | tf_op jit(solution)/shard_map/ppermute | solution.py:322
  53.8 30.7 %all-to-all-start.1 = ((f32[4,18,56,128]{3,2,1,0:T(8,128)}), f32[4,18,56,128]{3,2,1,0:T(8,128)}, u32[]{:S(2)}, u32[]{:S(2)}) async-start(f32[4,18,56,128]{3,2,1,0:T(8,128)} %bitcast.18), calls=%async_computation.1 | async-start | bytes 4128768 | tf_op jit(solution)/shard_map/all_to_all | solution.py:321

commit v3 on v2

--- a/solution.py
+++ b/solution.py
@@ -14,6 +14,7 @@
 HALF = 112
 QROWS = 56
 OWN = 18
+STEP = 3
 MA = ("ma_0", "ma_1", "ma_2")
 F32 = jnp.float32
 
@@ -50,13 +51,12 @@
 
 
 def pack(x):
-    tl = 3
     return pl.pallas_call(
         pack_kernel,
         out_shape=jax.ShapeDtypeStruct((4, OWN, QROWS, 128), F32),
-        grid=(OWN // tl,),
-        in_specs=[pl.BlockSpec((tl, FOLDS, 2, WAVES), lambda i: (i, 0, 0, 0))],
-        out_specs=pl.BlockSpec((4, tl, QROWS, 128), lambda i: (0, i, 0, 0)),
+        grid=(OWN // STEP,),
+        in_specs=[pl.BlockSpec((STEP, FOLDS, 2, WAVES), lambda i: (i, 0, 0, 0))],
+        out_specs=pl.BlockSpec((4, STEP, QROWS, 128), lambda i: (0, i, 0, 0)),
         name="pack",
     )(x)
 
@@ -154,7 +154,8 @@
     acc[slot] += jnp.sum((value * value).reshape(QROWS // 8, 8, 128), axis=0)
 
 
-def near_kernel(tl, info, d_ref, ck_ref, hp_ref, live_ref, p_ref, q_ref, x_ref, y_ref, z_ref, o_ref, s_ref, fix):
+def near_kernel(info, d_ref, ck_ref, hp_ref, live_ref, p_ref, q_ref, x_ref, y_ref, z_ref, o_ref, s_ref, fix):
+    tl = STEP
     step = pl.program_id(0)
     received = (x_ref, y_ref, z_ref)
 
@@ -207,77 +208,89 @@
     return pl.BlockSpec(shape, lambda i, s: (0,) * len(shape))
 
 
+BLOCK = pl.BlockSpec((4, STEP, QROWS, 128), lambda i, s: (0, i, 0, 0))
+SMEM = pl.BlockSpec(memory_space=pltpu.SMEM)
+SUM = jax.ShapeDtypeStruct((1, 8, 128), F32)
+
+
 def near(info, diag, ck, hp, live, p, q, x, y, z):
-    tl = 3
-    block = pl.BlockSpec((4, tl, QROWS, 128), lambda i, s: (0, i, 0, 0))
-    return pl.pallas_call(
-        lambda *refs: near_kernel(tl, *refs),
-        out_shape=(jax.ShapeDtypeStruct((4, OWN, QROWS, 128), F32), jax.ShapeDtypeStruct((1, 8, 128), F32)),
+    return pl.pallas_call(
+        near_kernel,
+        out_shape=(jax.ShapeDtypeStruct(p.shape, F32), SUM),
         grid_spec=pltpu.PrefetchScalarGridSpec(
             num_scalar_prefetch=1,
-            grid=(OWN // tl,),
-            in_specs=[
-                pl.BlockSpec(memory_space=pltpu.SMEM),
-                whole((4, 4, QROWS, 128)),
-                whole((4, QROWS, 128)),
-                whole((4, QROWS, 128)),
-            ]
-            + [block] * 5,
-            out_specs=[block, whole((1, 8, 128))],
+            grid=(OWN // STEP,),
+            in_specs=[SMEM, whole((4, 4, QROWS, 128)), whole((4, QROWS, 128)), whole((4, QROWS, 128))] + [BLOCK] * 5,
+            out_specs=[BLOCK, whole((1, 8, 128))],
             scratch_shapes=[pltpu.VMEM((3, 4, QROWS, 128), F32)],
         ),
         name="near",
     )(info, diag, ck, hp, live, p, q, x, y, z)
 
 
-def last_kernel(tl, info, d_ref, v_sum, hp_ref, live_ref, p_ref, part_ref, m_ref, o_ref, s_ref, buf, acc):
+def finish_kernel(info, d_ref, hp_ref, live_ref, p_ref, part_ref, m_ref, o_ref, buf):
     step = pl.program_id(0)
-
-    @pl.when(step == 0)
-    def _():
-        acc[...] = jnp.zeros_like(acc)
-
-    for l in range(tl):
-        d = d_ref[info[2] * OWN + step * tl + l]
+    for l in range(STEP):
+        d = d_ref[info[2] * OWN + step * STEP + l]
         for q in range(4):
             live = live_ref[q]
             scale = 1.0 / (1.0 + hp_ref[q] * d)
             residual = part_ref[q, l] - m_ref[q, l] * live
             buf[l, q * QROWS : (q + 1) * QROWS, :] = scale * (p_ref[q, l] * live + residual)
-            fold_sum(acc, 0, residual)
     for t in range(1, TILES):
         for par in range(2):
-            o_ref[:, 2 * t + par, :, : 128 * t] = jnp.zeros((tl, 2, 128 * t), F32)
+            o_ref[:, 2 * t + par, :, : 128 * t] = jnp.zeros((STEP, 2, 128 * t), F32)
     for fold, j, row in LIVE:
         o_ref[:, fold, :, 128 * j : 128 * j + 128] = buf[:, row : row + 2, :]
 
-    @pl.when(step == pl.num_programs(0) - 1)
-    def _():
-        row = lax.broadcasted_iota(jnp.int32, (8, 128), 0)
-        s_ref[...] = jnp.where(row == 0, jnp.sum(v_sum[0]), jnp.sum(acc[0]))
-
-
-def last(info, diag, v_sum, hp, live, p, part, m):
-    tl = 3
-    block = pl.BlockSpec((4, tl, QROWS, 128), lambda i, s: (0, i, 0, 0))
-    return pl.pallas_call(
-        lambda *refs: last_kernel(tl, *refs),
-        out_shape=(jax.ShapeDtypeStruct((OWN, FOLDS, 2, WAVES), F32), jax.ShapeDtypeStruct((8, 128), F32)),
+
+def finish(info, diag, hp, live, p, part, m):
+    return pl.pallas_call(
+        finish_kernel,
+        out_shape=jax.ShapeDtypeStruct((OWN, FOLDS, 2, WAVES), F32),
         grid_spec=pltpu.PrefetchScalarGridSpec(
             num_scalar_prefetch=1,
-            grid=(OWN // tl,),
-            in_specs=[
-                pl.BlockSpec(memory_space=pltpu.SMEM),
-                whole((1, 8, 128)),
-                whole((4, QROWS, 128)),
-                whole((4, QROWS, 128)),
-            ]
-            + [block] * 3,
-            out_specs=[pl.BlockSpec((tl, FOLDS, 2, WAVES), lambda i, s: (i, 0, 0, 0)), whole((8, 128))],
-            scratch_shapes=[pltpu.VMEM((tl, 2 * HALF, 128), F32), pltpu.VMEM((1, 8, 128), F32)],
+            grid=(OWN // STEP,),
+            in_specs=[SMEM, whole((4, QROWS, 128)), whole((4, QROWS, 128))] + [BLOCK] * 3,
+            out_specs=pl.BlockSpec((STEP, FOLDS, 2, WAVES), lambda i, s: (i, 0, 0, 0)),
+            scratch_shapes=[pltpu.VMEM((STEP, 2 * HALF, 128), F32)],
         ),
-        name="last",
-    )(info, diag, v_sum, hp, live, p, part, m)
+        name="finish",
+    )(info, diag, hp, live, p, part, m)
+
+
+def squares_kernel(v_ref, live_ref, part_ref, m_ref, o_ref, acc):
+    step = pl.program_id(0)
+
+    @pl.when(step == 0)
+    def _():
+        acc[...] = jnp.zeros_like(acc)
+
+    for l in range(SQUARES_STEP):
+        for q in range(4):
+            fold_sum(acc, 0, part_ref[q, l] - m_ref[q, l] * live_ref[q])
+
+    @pl.when(step == pl.num_programs(0) - 1)
+    def _():
+        row = lax.broadcasted_iota(jnp.int32, (8, 128), 0)
+        o_ref[...] = jnp.where(row == 0, jnp.sum(v_ref[0]), jnp.sum(acc[0]))
+
+
+SQUARES_STEP = 6
+
+
+def squares(v_sum, live, part, m):
+    full = lambda shape: pl.BlockSpec(shape, lambda i: (0,) * len(shape))
+    block = pl.BlockSpec((4, SQUARES_STEP, QROWS, 128), lambda i: (0, i, 0, 0))
+    return pl.pallas_call(
+        squares_kernel,
+        out_shape=jax.ShapeDtypeStruct((8, 128), F32),
+        grid=(OWN // SQUARES_STEP,),
+        in_specs=[full((1, 8, 128)), full((4, QROWS, 128)), block, block],
+        out_specs=full((8, 128)),
+        scratch_shapes=[pltpu.VMEM((1, 8, 128), F32)],
+        name="squares",
+    )(v_sum, live, part, m)
 
 
 def routes(owners):
@@ -307,8 +320,10 @@
     to_x, to_y, swap = routes(OWNERS)
     every = lax.all_to_all(p, "lev", 0, 0, tiled=True).reshape(LEV, QROWS, 128)
     x = lax.ppermute(p, MA, to_x)
-    y = lax.ppermute(p, MA, to_y)
     q = lax.ppermute(p, MA, swap)
+    x, p_after = lax.optimization_barrier((x, p))
+    y = lax.ppermute(p_after, MA, to_y)
+    z = lax.ppermute(x, MA, swap)
     ck, hp, live = prep(info, crows, helmholtz.reshape(TILES, 128))
     ck = ck.reshape(4, 4, QROWS, 128)
     hp = hp.reshape(4, QROWS, 128)
@@ -317,13 +332,13 @@
     high = lax.reduce_precision(vertical, 8, 7)
     w3 = jnp.concatenate([high, vertical - high, high], axis=1)
     m = mix(info, w3, diag[:, None], hp, every).reshape(4, OWN, QROWS, 128)
-    x, m = lax.optimization_barrier((x, m))
     m = lax.all_to_all(m, "lev", 0, 0, tiled=True)
-    z = lax.ppermute(x, MA, swap)
     part, v_sum = near(info, diag, ck, hp, live, p, q, x, y, z)
     part, m = lax.optimization_barrier((part, m))
-    rows, sums = last(info, diag, v_sum, hp, live, p, part, m)
-    sums = total(total(sums, ("ma_1", "ma_2")), ("ma_0", "lev"))
+    sums = total(squares(v_sum, live, part, m), ("ma_1", "ma_2"))
+    rows = finish(info, diag, hp, live, p, part, m)
+    sums, rows = lax.optimization_barrier((sums, rows))
+    sums = total(sums, ("ma_0", "lev"))
     norms = jnp.sqrt(sums[:2, 0] / (LEV * WAVES * (WAVES + 1)))
     return (rows.transpose(0, 2, 1, 3), norms)
 

time: 121 us -> 112 us (0.926)
  blocking collectives: 26.8 us -> 11 us
  Pallas kernels: 29.7 us -> 33.3 us
  starting transfers between devices: 22.3 us -> 25 us
    all_to_all x1, waiting for transfers between devices: 16.9 us -> 0.01 us  [body(): every = lax.all_to_all(p, 'lev', 0, 0, tiled=True).reshape(LEV, QROWS, 128)]
    ppermute x1, waiting for transfers between devices: 1.04 us -> 17.4 us  [body(): x = lax.ppermute(p, MA, to_x)]
    all_to_all x2 -> x1, blocking collectives: 26.8 us -> 11 us  [total(): lax.all_to_all(jnp.broadcast_to(value[None], (n,) + value.shape), axes, 0...]
    all_to_all x0 -> x1, starting transfers between devices: none -> 8.8 us  [total(): lax.all_to_all(jnp.broadcast_to(value[None], (n,) + value.shape), axes, 0...]
    all_to_all x1, waiting for transfers between devices: 17.7 us -> 9.4 us  [body(): m = lax.all_to_all(m, 'lev', 0, 0, tiled=True)]
    ppermute x1, waiting for transfers between devices: 0.01 us -> 8.08 us  [body(): y = lax.ppermute(p_after, MA, to_y)]
    ppermute x1, starting transfers between devices: 7.88 us -> 3.83 us  [body(): z = lax.ppermute(x, MA, swap)]
    pallas_call x2 -> x3, Pallas kernels: 15.6 us -> 19.1 us  [the longest x1 8.46 us: near(): pl.pallas_call(near_kernel, out_shape=(jax.ShapeDtypeStruct(p.shape, F32)...]
  transfers between devices with their start and end apart: 6 -> 7, of which waited for: 3 -> 4; matrix products, arithmetic and copies ran while one was open for 3% -> 3% of each run, Pallas kernels for 15% -> 22%
where the time goes in v3:
time: 112 us; the launch traced here: 111 us
  waiting for transfers between devices  35.7 us (32%)
  Pallas kernels  33.3 us (30%)
  starting transfers between devices  25 us (22%)
  blocking collectives  11 us (10%)
  local copies, waits for them, and re-layouts  3.82 us (3%)
  other arithmetic  1.53 us (1%)
    ppermute x1, waiting for transfers between devices, body(): x = lax.ppermute(p, MA, to_x)  17.4 us
    all_to_all x1, blocking collectives, total(): lax.all_to_all(jnp.broadcast_to(value[None], (n,) + value.shape), axes, 0...  11 us
    all_to_all x1, waiting for transfers between devices, body(): m = lax.all_to_all(m, 'lev', 0, 0, tiled=True)  9.4 us
    all_to_all x1, starting transfers between devices, total(): lax.all_to_all(jnp.broadcast_to(value[None], (n,) + value.shape), axes, 0...  8.8 us
    pallas_call x1, Pallas kernels, near(): pl.pallas_call(near_kernel, out_shape=(jax.ShapeDtypeStruct(p.shape, F32)...  8.46 us
    ppermute x1, waiting for transfers between devices, body(): y = lax.ppermute(p_after, MA, to_y)  8.08 us
    pallas_call x1, Pallas kernels, finish(): pl.pallas_call(finish_kernel, out_shape=jax.ShapeDtypeStruct((OWN, FOLDS,...  6.99 us
    pallas_call x1, Pallas kernels, mix(): pl.pallas_call(mix_kernel, out_shape=jax.ShapeDtypeStruct((LEV, QROWS, 12...  6.95 us
  transfers between devices with their start and end apart: 7, of which 4 were waited for; matrix products, arithmetic and copies ran while one was open for 3% of the time, Pallas kernels for 22%

profile of v3, /device:TPU:1, one launch (start us, length us, event | category | flops | bytes accessed | tf_op | source)
XLA Modules:
  0.0 111.2 jit_solution(8663881645138364348)
XLA Ops:
  0.6 5.2 %pack.1.p_ref = f32[4,18,56,128]{3,2,1,0:T(8,128)} custom-call(f32[18,20,2,1280]{3,2,1,0:T(2,128)} %bitcast.19), custom_call_target="tpu_custom_call" | custom-call | tf_op jit(solution)/shard_map/pack/pallas_call | solution.py:54
  5.8 0.0 copy-start
  5.8 0.0 copy-start.1
  5.8 2.5 %collective-permute-start.1 = (f32[4,18,56,128]{3,2,1,0:T(8,128)}, f32[4,18,56,128]{3,2,1,0:T(8,128)}, u32[]{:S(2)}, u32[]{:S(2)}) collective-permute-start(f32[4,18,56,128]{3,2,1,0:T(8,128)} %pack.1.p_ref), channel_id=1, source_target_pairs={{0,4},{4,12},{8,0},{12,20},{16,8},{20,28},{24,16},{28,36},{32,24},... | collective-permute-start | bytes 6193160 | tf_op jit(solution)/shard_map/ppermute | solution.py:322
  8.3 4.5 %all-to-all-start = ((f32[4,18,56,128]{3,2,1,0:T(8,128)}), f32[4,18,56,128]{3,2,1,0:T(8,128)}, u32[]{:S(2)}, u32[]{:S(2)}) async-start(f32[4,18,56,128]{3,2,1,0:T(8,128)} %pack.1.p_ref), calls=%async_computation | async-start | bytes 4128768 | tf_op jit(solution)/shard_map/all_to_all | solution.py:321
  12.8 0.0 copy-done
  12.8 0.0 copy-start.2
  12.8 1.0 collective-permute-start
  13.8 17.4 %collective-permute-done.1.x_ref = f32[4,18,56,128]{3,2,1,0:T(8,128)} collective-permute-done((f32[4,18,56,128]{3,2,1,0:T(8,128)}, f32[4,18,56,128]{3,2,1,0:T(8,128)}, u32[]{:S(2)}, u32[]{:S(2)}) %collective-permute-start.1) | collective-permute-done | bytes 2064416 | tf_op jit(solution)/shard_map/ppermute | solution.py:322
  31.2 3.8 %collective-permute-start.3 = (f32[4,18,56,128]{3,2,1,0:T(8,128)}, f32[4,18,56,128]{3,2,1,0:T(8,128)}, u32[]{:S(2)}, u32[]{:S(2)}) collective-permute-start(f32[4,18,56,128]{3,2,1,0:T(8,128)} %collective-permute-done.1.x_ref), channel_id=1, source_target_pairs={{0,4},{4,0},{8,12},{12,8},{16,20},{20,16},{24,28},{28,24},{32,36},... | collective-permute-start | bytes 6193160 | tf_op jit(solution)/shard_map/ppermute | solution.py:326
  35.1 0.0 collective-permute-start.2
  35.1 0.0 copy-done.1
  35.1 0.2 reshape.33
  35.3 0.9 copy.12
  36.2 0.0 copy-done.2
  36.2 0.1 reduce-precision_subtract_fusion
  36.3 0.0 copy-start.3
  36.3 0.7 copy.13.d_ref
  37.0 0.7 stack.24.info
  37.7 2.0 %prep.1 = (f32[4,224,128]{2,1,0:T(8,128)}, f32[224,128]{1,0:T(8,128)}, f32[224,128]{1,0:T(8,128)}) custom-call(s32[6]{0:T(128)} %stack.24.info, f32[800,128]{1,0:T(8,128)} %bitcast.22, f32[10,128]{1,0:T(8,128)} %bitcast.30), custom_call_target="tpu_custom_call" | custom-call | tf_op jit(solution)/shard_map/prep/pallas_call | solution.py:103
  39.7 0.8 pad_maximum_fusion.w_ref
  40.5 0.0 all-to-all-done
  40.5 6.9 %mix.1 = f32[72,56,128]{2,1,0:T(8,128)} custom-call(s32[6]{0:T(128)} %stack.24.info, f32[72,216]{1,0:T(8,128)} %pad_maximum_fusion.w_ref, f32[72,1]{1,0:T(8,128)} %copy.13.d_ref, f32[4,56,128]{2,1,0:T(8,128)} %bitcast.26, f32[72,56,128]{2,1,0:T(8,128)} %bitcast.13.x_ref), custom_call_target="tpu_custom_call" | custom-call | tf_op jit(solution)/shard_map/mix/pallas_call | solution.py:135
  47.4 0.0 copy-done.3
  47.4 4.5 %all-to-all-start.1 = ((f32[4,18,56,128]{3,2,1,0:T(8,128)}), f32[4,18,56,128]{3,2,1,0:T(8,128)}, u32[]{:S(2)}, u32[]{:S(2)}) async-start(f32[4,18,56,128]{3,2,1,0:T(8,128)} %bitcast.18), calls=%async_computation.1 | async-start | bytes 4128768 | tf_op jit(solution)/shard_map/all_to_all | solution.py:335
  51.9 0.0 collective-permute-done.q_ref
  51.9 0.0 collective-permute-done.3.z_ref
  51.9 8.1 %collective-permute-done.2.y_ref = f32[4,18,56,128]{3,2,1,0:T(8,128)} collective-permute-done((f32[4,18,56,128]{3,2,1,0:T(8,128)S(1)}, f32[4,18,56,128]{3,2,1,0:T(8,128)}, u32[]{:S(2)}, u32[]{:S(2)}) %collective-permute-start.2) | collective-permute-done | bytes 2064416 | tf_op jit(solution)/shard_map/ppermute | solution.py:325
  60.0 8.5 %near.1 = (f32[4,18,56,128]{3,2,1,0:T(8,128)}, f32[1,8,128]{2,1,0:T(8,128)}) custom-call(s32[6]{0:T(128)} %stack.24.info, f32[72]{0:T(128)} %copy-done.3, f32[4,4,56,128]{3,2,1,0:T(8,128)} %bitcast.29, f32[4,56,128]{2,1,0:T(8,128)} %bitcast.27, f32[4,56,128]{2,1,0:T(8,128)} %bitcast.23, f32[4,18,56,128]{3,2,1,0:T(8,128)} %pack.1.p_ref, ...), custom_call_target="tpu_custom_call" | custom-call | tf_op jit(solution)/shard_map/near/pallas_call | solution.py:217
  68.5 9.4 %all-to-all-done.1.m_ref = f32[4,18,56,128]{3,2,1,0:T(8,128)} async-done(((f32[4,18,56,128]{3,2,1,0:T(8,128)}), f32[4,18,56,128]{3,2,1,0:T(8,128)}, u32[]{:S(2)}, u32[]{:S(2)}) %all-to-all-start.1) | async-done | bytes 2064416 | tf_op jit(solution)/shard_map/all_to_all | solution.py:335
  77.9 3.6 %squares.1 = f32[8,128]{1,0:T(8,128)} custom-call(f32[1,8,128]{2,1,0:T(8,128)} %get-tuple-element.18.v_ref, f32[4,56,128]{2,1,0:T(8,128)} %bitcast.24, f32[4,18,56,128]{3,2,1,0:T(8,128)} %get-tuple-element.20.part_ref, f32[4,18,56,128]{3,2,1,0:T(8,128)} %all-to-all-done.1.m_ref), custom_call_target="tpu_custom_call" | custom-call | tf_op jit(solution)/shard_map/squares/pallas_call | solution.py:285
  81.5 1.3 %broadcast_in_dim.7 = f32[16,8,128]{2,1,0:T(8,128)} broadcast(f32[8,128]{1,0:T(8,128)} %squares.1), dimensions={1,2} | broadcast | bytes 69632 | tf_op jit(solution)/shard_map/broadcast_in_dim | solution.py:308
  82.8 8.8 %all-to-all-start.2 = ((f32[16,8,128]{2,1,0:T(8,128)}), f32[16,8,128]{2,1,0:T(8,128)S(1)}, u32[]{:S(2)}, u32[]{:S(2)}) async-start(f32[16,8,128]{2,1,0:T(8,128)} %broadcast_in_dim.7), calls=%async_computation.2 | async-start | bytes 131072 | tf_op jit(solution)/shard_map/all_to_all | solution.py:308
  91.6 7.0 %finish.1 = f32[18,20,2,1280]{3,2,1,0:T(2,128)} custom-call(s32[6]{0:T(128)} %stack.24.info, f32[72]{0:T(128)} %copy-done.3, f32[4,56,128]{2,1,0:T(8,128)} %bitcast.28, f32[4,56,128]{2,1,0:T(8,128)} %bitcast.25, f32[4,18,56,128]{3,2,1,0:T(8,128)} %pack.1.p_ref, f32[4,18,56,128]{3,2,1,0:T(8,128)} %get-tuple-element.20.part_ref, ...), custom_call_target="tpu_custom_call" | custom-call | tf_op jit(solution)/shard_map/finish/pallas_call | solution.py:248
  98.6 0.8 all-to-all-done.2
  99.5 11.0 %all_to_all.20 = f32[16,8,128]{2,1,0:T(8,128)S(1)} all-to-all(f32[16,8,128]{2,1,0:T(8,128)S(1)} %broadcast_in_dim.8), channel_id=1, replica_groups=mesh['ma_0'=4,'ma_1'=8,'ma_2'=2,'lev'=4] {'ma_0','lev'}, dimensions={0} | all-to-all | bytes 131072 | tf_op jit(solution)/shard_map/all_to_all | solution.py:308
  110.5 0.6 sqrt_reduce_fusion
  (3 shorter events, 0.0 us)
Async XLA Ops:
  5.8 6.9 %copy-start = (f32[4,18,56,128]{3,2,1,0:T(8,128)S(1)}, f32[4,18,56,128]{3,2,1,0:T(8,128)}, u32[]{:S(2)}) copy-start(f32[4,18,56,128]{3,2,1,0:T(8,128)} %pack.1.p_ref) | copy-start | bytes 6193156
  5.8 29.2 %copy-start.1 = (f32[4,20,1280]{2,0,1:T(4,128)S(1)}, f32[4,20,1280]{2,0,1:T(4,128)}, u32[]{:S(2)}) copy-start(f32[4,20,1280]{2,0,1:T(4,128)} %param.5) | copy-start | bytes 1228804
  5.8 25.4 %collective-permute-start.1 = (f32[4,18,56,128]{3,2,1,0:T(8,128)}, f32[4,18,56,128]{3,2,1,0:T(8,128)}, u32[]{:S(2)}, u32[]{:S(2)}) collective-permute-start(f32[4,18,56,128]{3,2,1,0:T(8,128)} %pack.1.p_ref), channel_id=1, source_target_pairs={{0,4},{4,12},{8,0},{12,20},{16,8},{20,28},{24,16},{28,36},{32,24},... | collective-permute-start | bytes 6193160 | tf_op jit(solution)/shard_map/ppermute | solution.py:322
  8.3 32.2 %all-to-all-start = ((f32[4,18,56,128]{3,2,1,0:T(8,128)}), f32[4,18,56,128]{3,2,1,0:T(8,128)}, u32[]{:S(2)}, u32[]{:S(2)}) async-start(f32[4,18,56,128]{3,2,1,0:T(8,128)} %pack.1.p_ref), calls=%async_computation | async-start | bytes 4128768 | tf_op jit(solution)/shard_map/all_to_all | solution.py:321
  12.8 23.4 %copy-start.2 = (f32[72,72]{1,0:T(8,128)S(1)}, f32[72,72]{1,0:T(8,128)}, u32[]{:S(2)}) copy-start(f32[72,72]{1,0:T(8,128)} %param.7) | copy-start | bytes 62212
  12.8 39.1 %collective-permute-start = (f32[4,18,56,128]{3,2,1,0:T(8,128)S(1)}, f32[4,18,56,128]{3,2,1,0:T(8,128)}, u32[]{:S(2)}, u32[]{:S(2)}) collective-permute-start(f32[4,18,56,128]{3,2,1,0:T(8,128)S(1)} %copy-done), channel_id=1, source_target_pairs={{0,4},{4,0},{8,12},{12,8},{16,20},{20,16},{24,28},{28,24},{32,36},... | collective-permute-start | bytes 6193160 | tf_op jit(solution)/shard_map/ppermute | solution.py:323
  31.2 20.7 %collective-permute-start.3 = (f32[4,18,56,128]{3,2,1,0:T(8,128)}, f32[4,18,56,128]{3,2,1,0:T(8,128)}, u32[]{:S(2)}, u32[]{:S(2)}) collective-permute-start(f32[4,18,56,128]{3,2,1,0:T(8,128)} %collective-permute-done.1.x_ref), channel_id=1, source_target_pairs={{0,4},{4,0},{8,12},{12,8},{16,20},{20,16},{24,28},{28,24},{32,36},... | collective-permute-start | bytes 6193160 | tf_op jit(solution)/shard_map/ppermute | solution.py:326
  35.1 24.9 %collective-permute-start.2 = (f32[4,18,56,128]{3,2,1,0:T(8,128)S(1)}, f32[4,18,56,128]{3,2,1,0:T(8,128)}, u32[]{:S(2)}, u32[]{:S(2)}) collective-permute-start(f32[4,18,56,128]{3,2,1,0:T(8,128)S(1)} %copy-done), channel_id=1, source_target_pairs={{0,8},{4,0},{8,16},{12,4},{16,24},{20,12},{24,32},{28,20},{32,40},... | collective-permute-start | bytes 6193160 | tf_op jit(solution)/shard_map/ppermute | solution.py:325
  36.3 11.1 %copy-start.3 = (f32[72]{0:T(128)}, f32[72]{0:T(128)S(1)}, u32[]{:S(2)}) copy-start(f32[72]{0:T(128)S(1)} %get-tuple-element.25.d_ref) | copy-start | bytes 868
  47.4 30.4 %all-to-all-start.1 = ((f32[4,18,56,128]{3,2,1,0:T(8,128)}), f32[4,18,56,128]{3,2,1,0:T(8,128)}, u32[]{:S(2)}, u32[]{:S(2)}) async-start(f32[4,18,56,128]{3,2,1,0:T(8,128)} %bitcast.18), calls=%async_computation.1 | async-start | bytes 4128768 | tf_op jit(solution)/shard_map/all_to_all | solution.py:335
  82.8 16.6 %all-to-all-start.2 = ((f32[16,8,128]{2,1,0:T(8,128)}), f32[16,8,128]{2,1,0:T(8,128)S(1)}, u32[]{:S(2)}, u32[]{:S(2)}) async-start(f32[16,8,128]{2,1,0:T(8,128)} %broadcast_in_dim.7), calls=%async_computation.2 | async-start | bytes 131072 | tf_op jit(solution)/shard_map/all_to_all | solution.py:308

commit v4 on v3

--- a/solution.py
+++ b/solution.py
@@ -14,7 +14,7 @@
 HALF = 112
 QROWS = 56
 OWN = 18
-STEP = 3
+STEP = 9
 MA = ("ma_0", "ma_1", "ma_2")
 F32 = jnp.float32
 
@@ -112,14 +112,14 @@
 def mix_kernel(info, w_ref, d_ref, h_ref, x_ref, o_ref):
     w = w_ref[...].astype(jnp.bfloat16)
     d = d_ref[...]
-    x2 = x_ref.reshape(LEV * 8, 128)
-    o2 = o_ref.reshape(LEV * 8, 128)
-    for r in range(0, 8, 2):
+    x2 = x_ref.reshape(LEV * QROWS, 128)
+    o2 = o_ref.reshape(LEV * QROWS, 128)
+    for r in range(0, QROWS, 2):
         h = h_ref[0, r : r + 1, :]
         scale = 1.0 / (1.0 + h * d)
         highs, lows = [], []
         for e in range(2):
-            f = x2[pl.ds(r + e, LEV, stride=8), :] * scale
+            f = x2[pl.ds(r + e, LEV, stride=QROWS), :] * scale
             high = f.astype(jnp.bfloat16).astype(F32)
             highs.append(high)
             lows.append(f - high)
@@ -128,7 +128,7 @@
         both = jnp.concatenate([high, high, low], axis=0).astype(jnp.bfloat16)
         out = jnp.dot(w, both, preferred_element_type=F32)
         for e in range(2):
-            o2[pl.ds(r + e, LEV, stride=8), :] = out[:, e * 128 : (e + 1) * 128] * h
+            o2[pl.ds(r + e, LEV, stride=QROWS), :] = out[:, e * 128 : (e + 1) * 128] * h
 
 
 def mix(info, w3, diag, hp, x):
@@ -137,14 +137,14 @@
         out_shape=jax.ShapeDtypeStruct((LEV, QROWS, 128), F32),
         grid_spec=pltpu.PrefetchScalarGridSpec(
             num_scalar_prefetch=1,
-            grid=(QROWS // 8,),
+            grid=(1,),
             in_specs=[
                 pl.BlockSpec((LEV, 3 * LEV), lambda i, s: (0, 0)),
                 pl.BlockSpec((LEV, 1), lambda i, s: (0, 0)),
-                pl.BlockSpec((1, 8, 128), lambda i, s: (s[2], i, 0)),
-                pl.BlockSpec((LEV, 8, 128), lambda i, s: (0, i, 0)),
+                pl.BlockSpec((1, QROWS, 128), lambda i, s: (s[2], 0, 0)),
+                pl.BlockSpec((LEV, QROWS, 128), lambda i, s: (0, 0, 0)),
             ],
-            out_specs=pl.BlockSpec((LEV, 8, 128), lambda i, s: (0, i, 0)),
+            out_specs=pl.BlockSpec((LEV, QROWS, 128), lambda i, s: (0, 0, 0)),
         ),
         name="mix",
     )(info, w3, diag, hp, x)
@@ -228,10 +228,11 @@
     )(info, diag, ck, hp, live, p, q, x, y, z)
 
 
-def finish_kernel(info, d_ref, hp_ref, live_ref, p_ref, part_ref, m_ref, o_ref, buf):
-    step = pl.program_id(0)
-    for l in range(STEP):
-        d = d_ref[info[2] * OWN + step * STEP + l]
+def finish_kernel(base, info, d_ref, hp_ref, live_ref, p_ref, part_ref, m_ref, *refs):
+    o_ref, buf = refs[-2:]
+    step = base // FINISH_STEP + pl.program_id(0)
+    for l in range(FINISH_STEP):
+        d = d_ref[info[2] * OWN + step * FINISH_STEP + l]
         for q in range(4):
             live = live_ref[q]
             scale = 1.0 / (1.0 + hp_ref[q] * d)
@@ -239,24 +240,30 @@
             buf[l, q * QROWS : (q + 1) * QROWS, :] = scale * (p_ref[q, l] * live + residual)
     for t in range(1, TILES):
         for par in range(2):
-            o_ref[:, 2 * t + par, :, : 128 * t] = jnp.zeros((STEP, 2, 128 * t), F32)
+            o_ref[:, 2 * t + par, :, : 128 * t] = jnp.zeros((FINISH_STEP, 2, 128 * t), F32)
     for fold, j, row in LIVE:
         o_ref[:, fold, :, 128 * j : 128 * j + 128] = buf[:, row : row + 2, :]
 
 
-def finish(info, diag, hp, live, p, part, m):
-    return pl.pallas_call(
-        finish_kernel,
+def finish(base, info, diag, hp, live, p, part, m, rows=None):
+    at = base // FINISH_STEP
+    block = pl.BlockSpec((4, FINISH_STEP, QROWS, 128), lambda i, s: (0, i + at, 0, 0))
+    before = [] if rows is None else [rows]
+    return pl.pallas_call(
+        lambda *refs: finish_kernel(base, *refs),
         out_shape=jax.ShapeDtypeStruct((OWN, FOLDS, 2, WAVES), F32),
         grid_spec=pltpu.PrefetchScalarGridSpec(
             num_scalar_prefetch=1,
-            grid=(OWN // STEP,),
-            in_specs=[SMEM, whole((4, QROWS, 128)), whole((4, QROWS, 128))] + [BLOCK] * 3,
-            out_specs=pl.BlockSpec((STEP, FOLDS, 2, WAVES), lambda i, s: (i, 0, 0, 0)),
-            scratch_shapes=[pltpu.VMEM((STEP, 2 * HALF, 128), F32)],
+            grid=(OWN // 2 // FINISH_STEP,),
+            in_specs=[SMEM, whole((4, QROWS, 128)), whole((4, QROWS, 128))]
+            + [block] * 3
+            + [pl.BlockSpec(memory_space=pl.ANY)] * len(before),
+            out_specs=pl.BlockSpec((FINISH_STEP, FOLDS, 2, WAVES), lambda i, s: (i + at, 0, 0, 0)),
+            scratch_shapes=[pltpu.VMEM((FINISH_STEP, 2 * HALF, 128), F32)],
         ),
+        input_output_aliases={7: 0} if before else {},
         name="finish",
-    )(info, diag, hp, live, p, part, m)
+    )(info, diag, hp, live, p, part, m, *before)
 
 
 def squares_kernel(v_ref, live_ref, part_ref, m_ref, o_ref, acc):
@@ -273,21 +280,23 @@
     @pl.when(step == pl.num_programs(0) - 1)
     def _():
         row = lax.broadcasted_iota(jnp.int32, (8, 128), 0)
-        o_ref[...] = jnp.where(row == 0, jnp.sum(v_ref[0]), jnp.sum(acc[0]))
-
-
-SQUARES_STEP = 6
-
-
-def squares(v_sum, live, part, m):
+        both = jnp.where(row == 0, jnp.sum(v_ref[0]), jnp.sum(acc[0]))
+        o_ref[...] = jnp.broadcast_to(both, o_ref.shape)
+
+
+SQUARES_STEP = 9
+FINISH_STEP = 9
+
+
+def squares(copies, v_sum, live, part, m):
     full = lambda shape: pl.BlockSpec(shape, lambda i: (0,) * len(shape))
     block = pl.BlockSpec((4, SQUARES_STEP, QROWS, 128), lambda i: (0, i, 0, 0))
     return pl.pallas_call(
         squares_kernel,
-        out_shape=jax.ShapeDtypeStruct((8, 128), F32),
+        out_shape=jax.ShapeDtypeStruct((copies, 8, 128), F32),
         grid=(OWN // SQUARES_STEP,),
         in_specs=[full((1, 8, 128)), full((4, QROWS, 128)), block, block],
-        out_specs=full((8, 128)),
+        out_specs=full((copies, 8, 128)),
         scratch_shapes=[pltpu.VMEM((1, 8, 128), F32)],
         name="squares",
     )(v_sum, live, part, m)
@@ -303,10 +312,8 @@
     return x, y, [(o, o ^ 1) for o in range(owners)]
 
 
-def total(value, axes):
-    n = lax.axis_size(axes)
-    every = lax.all_to_all(jnp.broadcast_to(value[None], (n,) + value.shape), axes, 0, 0, tiled=True)
-    return jnp.sum(every, axis=0)
+def total(copies, axes):
+    return jnp.sum(lax.all_to_all(copies, axes, 0, 0, tiled=True), axis=0)
 
 
 def body(forcing, coupling, helmholtz, vertical):
@@ -321,24 +328,27 @@
     every = lax.all_to_all(p, "lev", 0, 0, tiled=True).reshape(LEV, QROWS, 128)
     x = lax.ppermute(p, MA, to_x)
     q = lax.ppermute(p, MA, swap)
-    x, p_after = lax.optimization_barrier((x, p))
+    ck, hp, live = prep(info, crows, helmholtz.reshape(TILES, 128))
+    diag = jnp.sum(vertical * jnp.eye(LEV, dtype=F32), axis=1)
+    column = diag[:, None]
+    high = lax.reduce_precision(vertical, 8, 7)
+    w3 = jnp.concatenate([high, vertical - high, high], axis=1)
+    x, p_after, ck, hp, live, w3, column = lax.optimization_barrier((x, p, ck, hp, live, w3, column))
     y = lax.ppermute(p_after, MA, to_y)
     z = lax.ppermute(x, MA, swap)
-    ck, hp, live = prep(info, crows, helmholtz.reshape(TILES, 128))
     ck = ck.reshape(4, 4, QROWS, 128)
     hp = hp.reshape(4, QROWS, 128)
     live = live.reshape(4, QROWS, 128)
-    diag = jnp.sum(vertical * jnp.eye(LEV, dtype=F32), axis=1)
-    high = lax.reduce_precision(vertical, 8, 7)
-    w3 = jnp.concatenate([high, vertical - high, high], axis=1)
-    m = mix(info, w3, diag[:, None], hp, every).reshape(4, OWN, QROWS, 128)
+    m = mix(info, w3, column, hp, every).reshape(4, OWN, QROWS, 128)
     m = lax.all_to_all(m, "lev", 0, 0, tiled=True)
     part, v_sum = near(info, diag, ck, hp, live, p, q, x, y, z)
     part, m = lax.optimization_barrier((part, m))
-    sums = total(squares(v_sum, live, part, m), ("ma_1", "ma_2"))
-    rows = finish(info, diag, hp, live, p, part, m)
+    inner, outer = ("ma_1", "ma_2"), ("ma_0", "lev")
+    sums = total(squares(lax.axis_size(inner), v_sum, live, part, m), inner)
+    rows = finish(0, info, diag, hp, live, p, part, m)
     sums, rows = lax.optimization_barrier((sums, rows))
-    sums = total(sums, ("ma_0", "lev"))
+    sums = total(jnp.broadcast_to(sums[None], (lax.axis_size(outer), 8, 128)), outer)
+    rows = finish(OWN // 2, info, diag, hp, live, p, part, m, rows)
     norms = jnp.sqrt(sums[:2, 0] / (LEV * WAVES * (WAVES + 1)))
     return (rows.transpose(0, 2, 1, 3), norms)
 

time: 112 us -> 105 us (0.938)
  blocking collectives: 11 us -> 0 us
  starting transfers between devices: 25 us -> 32.5 us
  Pallas kernels: 33.3 us -> 28.8 us
  waiting for transfers between devices: 35.7 us -> 37.5 us
    all_to_all x1 -> x0, blocking collectives: 11 us -> none  [total(): lax.all_to_all(jnp.broadcast_to(value[None], (n,) + value.shape), axes, 0...]
    all_to_all x1 -> x2, starting transfers between devices: 8.8 us -> 16.2 us  [total(): return jnp.sum(lax.all_to_all(copies, axes, 0, 0, tiled=True), axis=0)]
    all_to_all x1 -> x2, waiting for transfers between devices: 0.81 us -> 5.72 us  [total(): return jnp.sum(lax.all_to_all(copies, axes, 0, 0, tiled=True), axis=0)]
    ppermute x1, waiting for transfers between devices: 17.4 us -> 12.8 us  [body(): x = lax.ppermute(p, MA, to_x)]
    ppermute x1, starting transfers between devices: 0.01 us -> 3.83 us  [body(): y = lax.ppermute(p_after, MA, to_y)]
    ppermute x1, starting transfers between devices: 3.83 us -> 0.18 us  [body(): z = lax.ppermute(x, MA, swap)]
    pallas_call x1, Pallas kernels: 6.95 us -> 4.81 us  [mix(): pl.pallas_call(mix_kernel, out_shape=jax.ShapeDtypeStruct((LEV, QROWS, 12...]
    pallas_call x1, Pallas kernels: 5.19 us -> 3.13 us  [pack(): pl.pallas_call(pack_kernel, out_shape=jax.ShapeDtypeStruct((4, OWN, QROWS...]
  transfers between devices with their start and end apart: 7 -> 8, of which waited for: 4 -> 6; matrix products, arithmetic and copies ran while one was open for 3% -> 3% of each run, Pallas kernels for 22% -> 22%
where the time goes in v4:
time: 105 us; the launch traced here: 104 us
  waiting for transfers between devices  37.5 us (36%)
  starting transfers between devices  32.5 us (31%)
  Pallas kernels  28.8 us (27%)
  local copies, waits for them, and re-layouts  3.14 us (3%)
  other arithmetic  1.52 us (1%)
    all_to_all x2, starting transfers between devices, total(): return jnp.sum(lax.all_to_all(copies, axes, 0, 0, tiled=True), axis=0)  16.2 us
    ppermute x1, waiting for transfers between devices, body(): x = lax.ppermute(p, MA, to_x)  12.8 us
    ppermute x1, waiting for transfers between devices, body(): y = lax.ppermute(p_after, MA, to_y)  9.72 us
    pallas_call x2, Pallas kernels, finish(): pl.pallas_call(lambda *refs: finish_kernel(base, *refs), out_shape=jax.Sh...  8.61 us
    all_to_all x1, waiting for transfers between devices, body(): m = lax.all_to_all(m, 'lev', 0, 0, tiled=True)  7.34 us
    pallas_call x1, Pallas kernels, near(): pl.pallas_call(near_kernel, out_shape=(jax.ShapeDtypeStruct(p.shape, F32)...  7.16 us
    all_to_all x2, waiting for transfers between devices, total(): return jnp.sum(lax.all_to_all(copies, axes, 0, 0, tiled=True), axis=0)  5.72 us
    pallas_call x1, Pallas kernels, mix(): pl.pallas_call(mix_kernel, out_shape=jax.ShapeDtypeStruct((LEV, QROWS, 12...  4.81 us
  transfers between devices with their start and end apart: 8, of which 6 were waited for; matrix products, arithmetic and copies ran while one was open for 3% of the time, Pallas kernels for 22%

profile of v4, /device:TPU:1, one launch (start us, length us, event | category | flops | bytes accessed | tf_op | source)
XLA Modules:
  0.0 104.2 jit_solution(13049891617316236958)
XLA Ops:
  0.6 3.1 %pack.1.p_ref.refs_4_ = f32[4,18,56,128]{3,2,1,0:T(8,128)} custom-call(f32[18,20,2,1280]{3,2,1,0:T(2,128)} %bitcast.20), custom_call_target="tpu_custom_call" | custom-call | tf_op jit(solution)/shard_map/pack/pallas_call | solution.py:54
  3.8 0.0 copy-start
  3.8 0.0 copy-start.1
  3.8 2.5 %collective-permute-start = (f32[4,18,56,128]{3,2,1,0:T(8,128)}, f32[4,18,56,128]{3,2,1,0:T(8,128)}, u32[]{:S(2)}, u32[]{:S(2)}) collective-permute-start(f32[4,18,56,128]{3,2,1,0:T(8,128)} %pack.1.p_ref.refs_4_), channel_id=1, source_target_pairs={{0,4},{4,12},{8,0},{12,20},{16,8},{20,28},{24,16},{28,36},{32,24},... | collective-permute-start | bytes 6193160 | tf_op jit(solution)/shard_map/ppermute | solution.py:329
  6.2 4.4 %all-to-all-start = ((f32[4,18,56,128]{3,2,1,0:T(8,128)}), f32[4,18,56,128]{3,2,1,0:T(8,128)}, u32[]{:S(2)}, u32[]{:S(2)}) async-start(f32[4,18,56,128]{3,2,1,0:T(8,128)} %pack.1.p_ref.refs_4_), calls=%async_computation | async-start | bytes 4128768 | tf_op jit(solution)/shard_map/all_to_all | solution.py:328
  10.7 0.0 copy-done
  10.7 0.0 copy-start.2
  10.7 1.0 collective-permute-start.1
  11.7 0.0 copy-done.1
  11.7 0.2 reshape.32
  11.9 0.9 copy.13
  12.8 0.7 stack.24.info.refs_0_
  13.5 2.0 %prep.1 = (f32[4,224,128]{2,1,0:T(8,128)}, f32[224,128]{1,0:T(8,128)}, f32[224,128]{1,0:T(8,128)}) custom-call(s32[6]{0:T(128)} %stack.24.info.refs_0_, f32[800,128]{1,0:T(8,128)} %bitcast.30, f32[10,128]{1,0:T(8,128)} %bitcast.33), custom_call_target="tpu_custom_call" | custom-call | tf_op jit(solution)/shard_map/prep/pallas_call | solution.py:103
  15.5 0.0 copy-done.2
  15.5 0.1 reduce-precision_subtract_fusion
  15.7 0.0 copy-start.3
  15.7 0.7 pad_maximum_fusion.w_ref
  16.4 12.8 %collective-permute-done.x_ref = f32[4,18,56,128]{3,2,1,0:T(8,128)} collective-permute-done((f32[4,18,56,128]{3,2,1,0:T(8,128)}, f32[4,18,56,128]{3,2,1,0:T(8,128)}, u32[]{:S(2)}, u32[]{:S(2)}) %collective-permute-start) | collective-permute-done | bytes 2064416 | tf_op jit(solution)/shard_map/ppermute | solution.py:329
  29.2 3.8 %collective-permute-start.2 = (f32[4,18,56,128]{3,2,1,0:T(8,128)S(1)}, f32[4,18,56,128]{3,2,1,0:T(8,128)}, u32[]{:S(2)}, u32[]{:S(2)}) collective-permute-start(f32[4,18,56,128]{3,2,1,0:T(8,128)S(1)} %copy-done), channel_id=1, source_target_pairs={{0,8},{4,0},{8,16},{12,4},{16,24},{20,12},{24,32},{28,20},{32,40},... | collective-permute-start | bytes 6193160 | tf_op jit(solution)/shard_map/ppermute | solution.py:337
  33.0 0.2 collective-permute-start.3
  33.2 0.7 copy.14.d_ref
  33.9 1.9 %all-to-all-done = f32[4,18,56,128]{3,2,1,0:T(8,128)} async-done(((f32[4,18,56,128]{3,2,1,0:T(8,128)}), f32[4,18,56,128]{3,2,1,0:T(8,128)}, u32[]{:S(2)}, u32[]{:S(2)}) %all-to-all-start) | async-done | bytes 2064416 | tf_op jit(solution)/shard_map/all_to_all | solution.py:328
  35.8 4.8 %mix.1 = f32[72,56,128]{2,1,0:T(8,128)} custom-call(s32[6]{0:T(128)} %stack.24.info.refs_0_, f32[72,216]{1,0:T(8,128)} %pad_maximum_fusion.w_ref, f32[72,1]{1,0:T(8,128)} %copy.14.d_ref, f32[4,56,128]{2,1,0:T(8,128)} %bitcast.26, f32[72,56,128]{2,1,0:T(8,128)} %bitcast.13.x_ref), custom_call_target="tpu_custom_call" | custom-call | tf_op jit(solution)/shard_map/mix/pallas_call | solution.py:135
  40.7 0.0 copy-done.3
  40.7 4.4 %all-to-all-start.1 = ((f32[4,18,56,128]{3,2,1,0:T(8,128)}), f32[4,18,56,128]{3,2,1,0:T(8,128)}, u32[]{:S(2)}, u32[]{:S(2)}) async-start(f32[4,18,56,128]{3,2,1,0:T(8,128)} %bitcast.19), calls=%async_computation.1 | async-start | bytes 4128768 | tf_op jit(solution)/shard_map/all_to_all | solution.py:343
  45.1 0.0 collective-permute-done.1.q_ref
  45.1 9.7 %collective-permute-done.2.y_ref = f32[4,18,56,128]{3,2,1,0:T(8,128)} collective-permute-done((f32[4,18,56,128]{3,2,1,0:T(8,128)S(1)}, f32[4,18,56,128]{3,2,1,0:T(8,128)}, u32[]{:S(2)}, u32[]{:S(2)}) %collective-permute-start.2) | collective-permute-done | bytes 2064416 | tf_op jit(solution)/shard_map/ppermute | solution.py:337
  54.8 0.0 collective-permute-done.3.z_ref
  54.8 7.2 %near.1 = (f32[4,18,56,128]{3,2,1,0:T(8,128)}, f32[1,8,128]{2,1,0:T(8,128)}) custom-call(s32[6]{0:T(128)} %stack.24.info.refs_0_, f32[72]{0:T(128)} %copy-done.3, f32[4,4,56,128]{3,2,1,0:T(8,128)} %bitcast.31, f32[4,56,128]{2,1,0:T(8,128)} %bitcast.27, f32[4,56,128]{2,1,0:T(8,128)} %bitcast.22, f32[4,18,56,128]{3,2,1,0:T(8,128)} %pack.1.p_ref.refs_4_, ...), custom_call_target="tpu_custom_call" | custom-call | tf_op jit(solution)/shard_map/near/pallas_call | solution.py:217
  62.0 7.3 %all-to-all-done.1.m_ref.refs_6_ = f32[4,18,56,128]{3,2,1,0:T(8,128)} async-done(((f32[4,18,56,128]{3,2,1,0:T(8,128)}), f32[4,18,56,128]{3,2,1,0:T(8,128)}, u32[]{:S(2)}, u32[]{:S(2)}) %all-to-all-start.1) | async-done | bytes 2064416 | tf_op jit(solution)/shard_map/all_to_all | solution.py:343
  69.3 3.1 %squares.1 = f32[16,8,128]{2,1,0:T(8,128)} custom-call(f32[1,8,128]{2,1,0:T(8,128)} %get-tuple-element.31.v_ref, f32[4,56,128]{2,1,0:T(8,128)} %bitcast.23, f32[4,18,56,128]{3,2,1,0:T(8,128)} %get-tuple-element.29.part_ref.refs_5_, f32[4,18,56,128]{3,2,1,0:T(8,128)} %all-to-all-done.1.m_ref.refs_6_), custom_call_target="tpu_custom_call" | custom-call | tf_op jit(solution)/shard_map/squares/pallas_call | solution.py:294
  72.4 11.4 %all-to-all-start.2 = ((f32[16,8,128]{2,1,0:T(8,128)}), f32[16,8,128]{2,1,0:T(8,128)S(1)}, u32[]{:S(2)}, u32[]{:S(2)}) async-start(f32[16,8,128]{2,1,0:T(8,128)} %squares.1), calls=%async_computation.2 | async-start | bytes 131072 | tf_op jit(solution)/shard_map/all_to_all | solution.py:316
  83.9 4.3 %finish.2.refs_7_ = f32[18,20,2,1280]{3,2,1,0:T(2,128)} custom-call(s32[6]{0:T(128)} %stack.24.info.refs_0_, f32[72]{0:T(128)} %copy-done.3, f32[4,56,128]{2,1,0:T(8,128)} %bitcast.28, f32[4,56,128]{2,1,0:T(8,128)} %bitcast.24, f32[4,18,56,128]{3,2,1,0:T(8,128)} %pack.1.p_ref.refs_4_, f32[4,18,56,128]{3,2,1,0:T(8,128)} %get-tuple-element.29.part_ref.refs_5_, ...), custom_call_target="tpu_custom_call" | custom-call | tf_op jit(solution)/shard_map/finish/pallas_call | solution.py:252
  88.2 3.5 %all-to-all-done.2 = f32[16,8,128]{2,1,0:T(8,128)S(1)} async-done(((f32[16,8,128]{2,1,0:T(8,128)}), f32[16,8,128]{2,1,0:T(8,128)S(1)}, u32[]{:S(2)}, u32[]{:S(2)}) %all-to-all-start.2) | async-done | bytes 65568 | tf_op jit(solution)/shard_map/all_to_all | solution.py:316
  91.7 0.6 broadcast_in_dim.10
  92.3 4.7 %all-to-all-start.3 = ((f32[16,8,128]{2,1,0:T(8,128)}), f32[16,8,128]{2,1,0:T(8,128)S(1)}, u32[]{:S(2)}, u32[]{:S(2)}) async-start(f32[16,8,128]{2,1,0:T(8,128)} %broadcast_in_dim.10), calls=%async_computation.3 | async-start | bytes 131072 | tf_op jit(solution)/shard_map/all_to_all | solution.py:316
  97.1 4.3 %finish.3 = f32[18,20,2,1280]{3,2,1,0:T(2,128)} custom-call(s32[6]{0:T(128)} %stack.24.info.refs_0_, f32[72]{0:T(128)} %copy-done.3, f32[4,56,128]{2,1,0:T(8,128)} %bitcast.29, f32[4,56,128]{2,1,0:T(8,128)} %bitcast.25, f32[4,18,56,128]{3,2,1,0:T(8,128)} %pack.1.p_ref.refs_4_, ...), custom_call_target="tpu_custom_call", output_to_operand_aliasing={{}: (7, {})} | custom-call | tf_op jit(solution)/shard_map/finish/pallas_call | solution.py:252
  101.4 2.2 %all-to-all-done.3 = f32[16,8,128]{2,1,0:T(8,128)S(1)} async-done(((f32[16,8,128]{2,1,0:T(8,128)}), f32[16,8,128]{2,1,0:T(8,128)S(1)}, u32[]{:S(2)}, u32[]{:S(2)}) %all-to-all-start.3) | async-done | bytes 65568 | tf_op jit(solution)/shard_map/all_to_all | solution.py:316
  103.6 0.6 sqrt_reduce_fusion
  (2 shorter events, 0.0 us)
Async XLA Ops:
  3.8 6.9 %copy-start = (f32[4,18,56,128]{3,2,1,0:T(8,128)S(1)}, f32[4,18,56,128]{3,2,1,0:T(8,128)}, u32[]{:S(2)}) copy-start(f32[4,18,56,128]{3,2,1,0:T(8,128)} %pack.1.p_ref.refs_4_) | copy-start | bytes 6193156
  3.8 8.0 %copy-start.1 = (f32[4,20,1280]{2,0,1:T(4,128)S(1)}, f32[4,20,1280]{2,0,1:T(4,128)}, u32[]{:S(2)}) copy-start(f32[4,20,1280]{2,0,1:T(4,128)} %param.5) | copy-start | bytes 1228804
  3.8 25.4 %collective-permute-start = (f32[4,18,56,128]{3,2,1,0:T(8,128)}, f32[4,18,56,128]{3,2,1,0:T(8,128)}, u32[]{:S(2)}, u32[]{:S(2)}) collective-permute-start(f32[4,18,56,128]{3,2,1,0:T(8,128)} %pack.1.p_ref.refs_4_), channel_id=1, source_target_pairs={{0,4},{4,12},{8,0},{12,20},{16,8},{20,28},{24,16},{28,36},{32,24},... | collective-permute-start | bytes 6193160 | tf_op jit(solution)/shard_map/ppermute | solution.py:329
  6.2 29.6 %all-to-all-start = ((f32[4,18,56,128]{3,2,1,0:T(8,128)}), f32[4,18,56,128]{3,2,1,0:T(8,128)}, u32[]{:S(2)}, u32[]{:S(2)}) async-start(f32[4,18,56,128]{3,2,1,0:T(8,128)} %pack.1.p_ref.refs_4_), calls=%async_computation | async-start | bytes 4128768 | tf_op jit(solution)/shard_map/all_to_all | solution.py:328
  10.7 4.9 %copy-start.2 = (f32[72,72]{1,0:T(8,128)S(1)}, f32[72,72]{1,0:T(8,128)}, u32[]{:S(2)}) copy-start(f32[72,72]{1,0:T(8,128)} %param.7) | copy-start | bytes 62212
  10.7 34.4 %collective-permute-start.1 = (f32[4,18,56,128]{3,2,1,0:T(8,128)S(1)}, f32[4,18,56,128]{3,2,1,0:T(8,128)}, u32[]{:S(2)}, u32[]{:S(2)}) collective-permute-start(f32[4,18,56,128]{3,2,1,0:T(8,128)S(1)} %copy-done), channel_id=1, source_target_pairs={{0,4},{4,0},{8,12},{12,8},{16,20},{20,16},{24,28},{28,24},{32,36},... | collective-permute-start | bytes 6193160 | tf_op jit(solution)/shard_map/ppermute | solution.py:330
  15.7 25.0 %copy-start.3 = (f32[72]{0:T(128)}, f32[72]{0:T(128)S(1)}, u32[]{:S(2)}) copy-start(f32[72]{0:T(128)S(1)} %get-tuple-element.35.d_ref.refs_1_) | copy-start | bytes 868
  29.2 25.7 %collective-permute-start.2 = (f32[4,18,56,128]{3,2,1,0:T(8,128)S(1)}, f32[4,18,56,128]{3,2,1,0:T(8,128)}, u32[]{:S(2)}, u32[]{:S(2)}) collective-permute-start(f32[4,18,56,128]{3,2,1,0:T(8,128)S(1)} %copy-done), channel_id=1, source_target_pairs={{0,8},{4,0},{8,16},{12,4},{16,24},{20,12},{24,32},{28,20},{32,40},... | collective-permute-start | bytes 6193160 | tf_op jit(solution)/shard_map/ppermute | solution.py:337
  33.0 21.8 %collective-permute-start.3 = (f32[4,18,56,128]{3,2,1,0:T(8,128)}, f32[4,18,56,128]{3,2,1,0:T(8,128)}, u32[]{:S(2)}, u32[]{:S(2)}) collective-permute-start(f32[4,18,56,128]{3,2,1,0:T(8,128)} %collective-permute-done.x_ref), channel_id=1, source_target_pairs={{0,4},{4,0},{8,12},{12,8},{16,20},{20,16},{24,28},{28,24},{32,36},... | collective-permute-start | bytes 6193160 | tf_op jit(solution)/shard_map/ppermute | solution.py:338
  40.7 28.7 %all-to-all-start.1 = ((f32[4,18,56,128]{3,2,1,0:T(8,128)}), f32[4,18,56,128]{3,2,1,0:T(8,128)}, u32[]{:S(2)}, u32[]{:S(2)}) async-start(f32[4,18,56,128]{3,2,1,0:T(8,128)} %bitcast.19), calls=%async_computation.1 | async-start | bytes 4128768 | tf_op jit(solution)/shard_map/all_to_all | solution.py:343
  72.4 19.3 %all-to-all-start.2 = ((f32[16,8,128]{2,1,0:T(8,128)}), f32[16,8,128]{2,1,0:T(8,128)S(1)}, u32[]{:S(2)}, u32[]{:S(2)}) async-start(f32[16,8,128]{2,1,0:T(8,128)} %squares.1), calls=%async_computation.2 | async-start | bytes 131072 | tf_op jit(solution)/shard_map/all_to_all | solution.py:316
  92.3 11.3 %all-to-all-start.3 = ((f32[16,8,128]{2,1,0:T(8,128)}), f32[16,8,128]{2,1,0:T(8,128)S(1)}, u32[]{:S(2)}, u32[]{:S(2)}) async-start(f32[16,8,128]{2,1,0:T(8,128)} %broadcast_in_dim.10), calls=%async_computation.3 | async-start | bytes 131072 | tf_op jit(solution)/shard_map/all_to_all | solution.py:316

commit v5 on v4

--- a/solution.py
+++ b/solution.py
@@ -17,6 +17,13 @@
 STEP = 9
 MA = ("ma_0", "ma_1", "ma_2")
 F32 = jnp.float32
+VMEM = pl.BlockSpec(memory_space=pltpu.VMEM)
+SMEM = pl.BlockSpec(memory_space=pltpu.SMEM)
+QUARTER = jax.ShapeDtypeStruct((OWN, QROWS, 128), F32)
+
+
+def in_vmem(x):
+    return pltpu.with_memory_space_constraint(x, pltpu.VMEM)
 
 
 def start_row(t):
@@ -109,11 +116,14 @@
     )(info, c, h)
 
 
-def mix_kernel(info, w_ref, d_ref, h_ref, x_ref, o_ref):
-    w = w_ref[...].astype(jnp.bfloat16)
-    d = d_ref[...]
+ROWS = 24
+
+
+def mix_kernel(info, w_ref, h_ref, *refs):
+    x_ref, *outs = refs
+    w = w_ref[:, : 3 * LEV].astype(jnp.bfloat16)
+    d = w_ref[:LEV, 3 * LEV :]
     x2 = x_ref.reshape(LEV * QROWS, 128)
-    o2 = o_ref.reshape(LEV * QROWS, 128)
     for r in range(0, QROWS, 2):
         h = h_ref[0, r : r + 1, :]
         scale = 1.0 / (1.0 + h * d)
@@ -127,81 +137,94 @@
         low = jnp.concatenate(lows, axis=1)
         both = jnp.concatenate([high, high, low], axis=0).astype(jnp.bfloat16)
         out = jnp.dot(w, both, preferred_element_type=F32)
-        for e in range(2):
-            o2[pl.ds(r + e, LEV, stride=QROWS), :] = out[:, e * 128 : (e + 1) * 128] * h
-
-
-def mix(info, w3, diag, hp, x):
+        for away, ref in enumerate(outs):
+            o2 = ref.reshape(OWN * QROWS, 128)
+            for e in range(2):
+                part = out[away * ROWS : away * ROWS + OWN, e * 128 : (e + 1) * 128]
+                o2[pl.ds(r + e, OWN, stride=QROWS), :] = part * h
+
+
+def mix(info, w3, hp, x):
+    held = pl.BlockSpec((OWN, QROWS, 128), lambda i, s: (0, 0, 0))
     return pl.pallas_call(
         mix_kernel,
-        out_shape=jax.ShapeDtypeStruct((LEV, QROWS, 128), F32),
+        out_shape=[QUARTER] * 4,
         grid_spec=pltpu.PrefetchScalarGridSpec(
             num_scalar_prefetch=1,
             grid=(1,),
             in_specs=[
-                pl.BlockSpec((LEV, 3 * LEV), lambda i, s: (0, 0)),
-                pl.BlockSpec((LEV, 1), lambda i, s: (0, 0)),
+                pl.BlockSpec((4 * ROWS, 3 * LEV + 1), lambda i, s: (0, 0)),
                 pl.BlockSpec((1, QROWS, 128), lambda i, s: (s[2], 0, 0)),
-                pl.BlockSpec((LEV, QROWS, 128), lambda i, s: (0, 0, 0)),
+                VMEM,
             ],
-            out_specs=pl.BlockSpec((LEV, QROWS, 128), lambda i, s: (0, 0, 0)),
+            out_specs=[held] * 4,
         ),
         name="mix",
-    )(info, w3, diag, hp, x)
+    )(info, w3, hp, in_vmem(x))
+
+
+def mix_table(vertical, lev):
+    diag = jnp.sum(vertical * jnp.eye(LEV, dtype=F32), axis=1)
+    padded = jnp.pad(vertical.reshape(4, OWN, LEV), ((0, 0), (0, ROWS - OWN), (0, 0))).reshape(4 * ROWS, LEV)
+    turned = lax.dynamic_slice_in_dim(jnp.concatenate([padded, padded], axis=0), lev * ROWS, 4 * ROWS, 0)
+    high = lax.reduce_precision(turned, 8, 7)
+    column = jnp.pad(diag[:, None], ((0, 4 * ROWS - LEV), (0, 0)))
+    return diag, jnp.concatenate([high, turned - high, high, column], axis=1)
 
 
 def fold_sum(acc, slot, value):
     acc[slot] += jnp.sum((value * value).reshape(QROWS // 8, 8, 128), axis=0)
 
 
-def near_kernel(info, d_ref, ck_ref, hp_ref, live_ref, p_ref, q_ref, x_ref, y_ref, z_ref, o_ref, s_ref, fix):
-    tl = STEP
+def near_kernel(info, d_ref, ck_ref, hp_ref, live_ref, p_ref, q_ref, x_ref, y_ref, z_ref, o_ref, kept_ref, s_ref, fix):
     step = pl.program_id(0)
     received = (x_ref, y_ref, z_ref)
 
     @pl.when(step == 0)
     def _():
         s_ref[...] = jnp.zeros_like(s_ref)
-        fix[...] = jnp.zeros_like(fix)
-
-    def one(l, get):
-        d = d_ref[info[2] * OWN + step * tl + l]
-        for q in range(4):
-            live = live_ref[q]
-            v = p_ref[q, l] * live
-            scale = 1.0 / (1.0 + hp_ref[q] * d)
-            near = ck_ref[0, q] * q_ref[q, l] + v
-            for a in range(3):
-                near = near + ck_ref[a + 1, q] * get(a, q)
-            o_ref[q, l] = v - scale * near * live
-            fold_sum(s_ref, 0, v)
+
+    def every(get):
+        def chunk(c, _):
+            rows = pl.ds(pl.multiple_of(c * 8, 8), 8)
+            for q in range(4):
+                live, hp = live_ref[q, rows, :], hp_ref[q, rows, :]
+                ck = [ck_ref[a, q, rows, :] for a in range(4)]
+                squares = jnp.zeros((8, 128), F32)
+                for l in range(STEP):
+                    scale = 1.0 / (1.0 + hp * d_ref[info[2] * OWN + step * STEP + l])
+                    v = p_ref[q, l, rows, :] * live
+                    near = ck[0] * q_ref[q, l, rows, :] + v
+                    for a in range(3):
+                        near = near + ck[a + 1] * get(a, q, l, rows)
+                    left = v - scale * near * live
+                    o_ref[q, l, rows, :] = left
+                    kept_ref[q, step * STEP + l, rows, :] = left
+                    squares = squares + v * v
+                s_ref[0] += squares
+            return 0
+
+        lax.fori_loop(0, QROWS // 8, chunk, 0)
 
     @pl.when(info[0] > 1)
     def _():
-        def level(l, _):
-            one(l, lambda a, q: received[a][jnp.where(info[3 + a] == 1, q ^ 2, q), l])
-            return 0
-
-        lax.fori_loop(0, tl, level, 0)
+        every(lambda a, q, l, rows: received[a][jnp.where(info[3 + a] == 1, q ^ 2, q), l, rows, :])
 
     @pl.when(info[0] <= 1)
     def _():
-        def level(l, _):
-            for a in range(3):
-
-                @pl.when(info[3 + a] == 2)
-                def _():
-                    for s, t, n in DOWN:
-                        fix[a, t // QROWS, t % QROWS : t % QROWS + n, :] = received[a][s // QROWS, l, s % QROWS : s % QROWS + n, :]
-
-                @pl.when(info[3 + a] != 2)
-                def _():
-                    fix[a] = received[a][:, l]
-
-            one(l, lambda a, q: fix[a, q])
-            return 0
-
-        lax.fori_loop(0, tl, level, 0)
+        for a in range(3):
+
+            @pl.when(info[3 + a] == 2)
+            def _():
+                fix[a] = jnp.zeros(fix.shape[1:], F32)
+                for s, t, n in DOWN:
+                    fix[a, t // QROWS, :, t % QROWS : t % QROWS + n, :] = received[a][s // QROWS, :, s % QROWS : s % QROWS + n, :]
+
+            @pl.when(info[3 + a] != 2)
+            def _():
+                fix[a] = received[a][...]
+
+        every(lambda a, q, l, rows: fix[a, q, l, rows, :])
 
 
 def whole(shape):
@@ -209,35 +232,35 @@
 
 
 BLOCK = pl.BlockSpec((4, STEP, QROWS, 128), lambda i, s: (0, i, 0, 0))
-SMEM = pl.BlockSpec(memory_space=pltpu.SMEM)
 SUM = jax.ShapeDtypeStruct((1, 8, 128), F32)
 
 
 def near(info, diag, ck, hp, live, p, q, x, y, z):
     return pl.pallas_call(
         near_kernel,
-        out_shape=(jax.ShapeDtypeStruct(p.shape, F32), SUM),
+        out_shape=(jax.ShapeDtypeStruct(p.shape, F32), pltpu.VMEM(p.shape, F32), SUM),
         grid_spec=pltpu.PrefetchScalarGridSpec(
             num_scalar_prefetch=1,
             grid=(OWN // STEP,),
             in_specs=[SMEM, whole((4, 4, QROWS, 128)), whole((4, QROWS, 128)), whole((4, QROWS, 128))] + [BLOCK] * 5,
-            out_specs=[BLOCK, whole((1, 8, 128))],
-            scratch_shapes=[pltpu.VMEM((3, 4, QROWS, 128), F32)],
+            out_specs=[BLOCK, VMEM, whole((1, 8, 128))],
+            scratch_shapes=[pltpu.VMEM((3, 4, STEP, QROWS, 128), F32)],
         ),
         name="near",
     )(info, diag, ck, hp, live, p, q, x, y, z)
 
 
-def finish_kernel(base, info, d_ref, hp_ref, live_ref, p_ref, part_ref, m_ref, *refs):
+def finish_kernel(base, info, d_ref, hp_ref, live_ref, p_ref, part_ref, *refs):
     o_ref, buf = refs[-2:]
     step = base // FINISH_STEP + pl.program_id(0)
     for l in range(FINISH_STEP):
         d = d_ref[info[2] * OWN + step * FINISH_STEP + l]
-        for q in range(4):
+        for away in range(4):
+            q = (info[2] - away) & 3
             live = live_ref[q]
             scale = 1.0 / (1.0 + hp_ref[q] * d)
-            residual = part_ref[q, l] - m_ref[q, l] * live
-            buf[l, q * QROWS : (q + 1) * QROWS, :] = scale * (p_ref[q, l] * live + residual)
+            residual = part_ref[q, l] - refs[away][l] * live
+            buf[l, pl.ds(pl.multiple_of(q * QROWS, 8), QROWS), :] = scale * (p_ref[q, l] * live + residual)
     for t in range(1, TILES):
         for par in range(2):
             o_ref[:, 2 * t + par, :, : 128 * t] = jnp.zeros((FINISH_STEP, 2, 128 * t), F32)
@@ -245,10 +268,10 @@
         o_ref[:, fold, :, 128 * j : 128 * j + 128] = buf[:, row : row + 2, :]
 
 
-def finish(base, info, diag, hp, live, p, part, m, rows=None):
+def finish(base, info, diag, hp, live, p, part, m, *before):
     at = base // FINISH_STEP
     block = pl.BlockSpec((4, FINISH_STEP, QROWS, 128), lambda i, s: (0, i + at, 0, 0))
-    before = [] if rows is None else [rows]
+    piece = pl.BlockSpec((FINISH_STEP, QROWS, 128), lambda i, s: (i + at, 0, 0))
     return pl.pallas_call(
         lambda *refs: finish_kernel(base, *refs),
         out_shape=jax.ShapeDtypeStruct((OWN, FOLDS, 2, WAVES), F32),
@@ -256,26 +279,40 @@
             num_scalar_prefetch=1,
             grid=(OWN // 2 // FINISH_STEP,),
             in_specs=[SMEM, whole((4, QROWS, 128)), whole((4, QROWS, 128))]
-            + [block] * 3
+            + [block] * 2
+            + [piece] * 4
             + [pl.BlockSpec(memory_space=pl.ANY)] * len(before),
             out_specs=pl.BlockSpec((FINISH_STEP, FOLDS, 2, WAVES), lambda i, s: (i + at, 0, 0, 0)),
             scratch_shapes=[pltpu.VMEM((FINISH_STEP, 2 * HALF, 128), F32)],
         ),
-        input_output_aliases={7: 0} if before else {},
+        input_output_aliases={10: 0} if before else {},
         name="finish",
-    )(info, diag, hp, live, p, part, m, *before)
-
-
-def squares_kernel(v_ref, live_ref, part_ref, m_ref, o_ref, acc):
+    )(info, diag, hp, live, p, part, *m, *before)
+
+
+def squares_kernel(info, v_ref, live_ref, part_ref, *refs):
+    o_ref, acc = refs[-2:]
     step = pl.program_id(0)
 
     @pl.when(step == 0)
     def _():
         acc[...] = jnp.zeros_like(acc)
 
-    for l in range(SQUARES_STEP):
-        for q in range(4):
-            fold_sum(acc, 0, part_ref[q, l] - m_ref[q, l] * live_ref[q])
+    def chunk(c, _):
+        rows = pl.ds(pl.multiple_of(c * 8, 8), 8)
+        sums = [jnp.zeros((8, 128), F32) for _ in range(8)]
+        for away in range(4):
+            q = (info[2] - away) & 3
+            live = live_ref[q, rows, :]
+            for l in range(SQUARES_STEP):
+                residual = part_ref[q, step * SQUARES_STEP + l, rows, :] - refs[away][l, rows, :] * live
+                sums[2 * away + l % 2] += residual * residual
+        while len(sums) > 1:
+            sums = [a + b for a, b in zip(sums[::2], sums[1::2])]
+        acc[0] += sums[0]
+        return 0
+
+    lax.fori_loop(0, QROWS // 8, chunk, 0)
 
     @pl.when(step == pl.num_programs(0) - 1)
     def _():
@@ -288,18 +325,20 @@
 FINISH_STEP = 9
 
 
-def squares(copies, v_sum, live, part, m):
-    full = lambda shape: pl.BlockSpec(shape, lambda i: (0,) * len(shape))
-    block = pl.BlockSpec((4, SQUARES_STEP, QROWS, 128), lambda i: (0, i, 0, 0))
+def squares(copies, info, v_sum, live, part, m):
+    piece = pl.BlockSpec((SQUARES_STEP, QROWS, 128), lambda i, s: (i, 0, 0))
     return pl.pallas_call(
         squares_kernel,
         out_shape=jax.ShapeDtypeStruct((copies, 8, 128), F32),
-        grid=(OWN // SQUARES_STEP,),
-        in_specs=[full((1, 8, 128)), full((4, QROWS, 128)), block, block],
-        out_specs=full((copies, 8, 128)),
-        scratch_shapes=[pltpu.VMEM((1, 8, 128), F32)],
+        grid_spec=pltpu.PrefetchScalarGridSpec(
+            num_scalar_prefetch=1,
+            grid=(OWN // SQUARES_STEP,),
+            in_specs=[whole((1, 8, 128)), whole((4, QROWS, 128)), VMEM] + [piece] * 4,
+            out_specs=whole((copies, 8, 128)),
+            scratch_shapes=[pltpu.VMEM((1, 8, 128), F32)],
+        ),
         name="squares",
-    )(v_sum, live, part, m)
+    )(info, v_sum, live, in_vmem(part), *m)
 
 
 def routes(owners):
@@ -325,26 +364,24 @@
     crows = coupling.reshape(4, FOLDS, TILES, 128).transpose(1, 2, 0, 3).reshape(800, 128)
     p = pack(forcing.transpose(0, 2, 1, 3))
     to_x, to_y, swap = routes(OWNERS)
+    along = lambda v, away: lax.ppermute(v, "lev", [(i, (i + away) % 4) for i in range(4)])
     every = lax.all_to_all(p, "lev", 0, 0, tiled=True).reshape(LEV, QROWS, 128)
     x = lax.ppermute(p, MA, to_x)
     q = lax.ppermute(p, MA, swap)
     ck, hp, live = prep(info, crows, helmholtz.reshape(TILES, 128))
-    diag = jnp.sum(vertical * jnp.eye(LEV, dtype=F32), axis=1)
-    column = diag[:, None]
-    high = lax.reduce_precision(vertical, 8, 7)
-    w3 = jnp.concatenate([high, vertical - high, high], axis=1)
-    x, p_after, ck, hp, live, w3, column = lax.optimization_barrier((x, p, ck, hp, live, w3, column))
+    diag, w3 = mix_table(vertical, lev)
+    x, p_after, ck, hp, live, w3 = lax.optimization_barrier((x, p, ck, hp, live, w3))
     y = lax.ppermute(p_after, MA, to_y)
     z = lax.ppermute(x, MA, swap)
     ck = ck.reshape(4, 4, QROWS, 128)
     hp = hp.reshape(4, QROWS, 128)
     live = live.reshape(4, QROWS, 128)
-    m = mix(info, w3, column, hp, every).reshape(4, OWN, QROWS, 128)
-    m = lax.all_to_all(m, "lev", 0, 0, tiled=True)
-    part, v_sum = near(info, diag, ck, hp, live, p, q, x, y, z)
-    part, m = lax.optimization_barrier((part, m))
+    mixed = mix(info, w3, hp, every)
+    m = [mixed[0]] + [along(v, away) for v, away in zip(mixed[1:], (1, 2, 3))]
+    part, kept, v_sum = near(info, diag, ck, hp, live, p, q, x, y, z)
+    part, *m = lax.optimization_barrier((part, *m))
     inner, outer = ("ma_1", "ma_2"), ("ma_0", "lev")
-    sums = total(squares(lax.axis_size(inner), v_sum, live, part, m), inner)
+    sums = total(squares(lax.axis_size(inner), info, v_sum, live, kept, m), inner)
     rows = finish(0, info, diag, hp, live, p, part, m)
     sums, rows = lax.optimization_barrier((sums, rows))
     sums = total(jnp.broadcast_to(sums[None], (lax.axis_size(outer), 8, 128)), outer)

time: 105 us -> 101 us (0.962)
  starting transfers between devices: 32.5 us -> 30.2 us
    all_to_all x1 -> x0, waiting for transfers between devices: 7.34 us -> none  [body(): m = lax.all_to_all(m, 'lev', 0, 0, tiled=True)]
    all_to_all x1 -> x0, starting transfers between devices: 4.45 us -> none  [body(): m = lax.all_to_all(m, 'lev', 0, 0, tiled=True)]
    ppermute x0 -> x3, waiting for transfers between devices: none -> 3.38 us  [body(): lax.ppermute(v, 'lev', [(i, (i + away) % 4) for i in range(4)])]
    ppermute x0 -> x3, starting transfers between devices: none -> 2.69 us  [body(): lax.ppermute(v, 'lev', [(i, (i + away) % 4) for i in range(4)])]
    ppermute x1, waiting for transfers between devices: 9.72 us -> 12.2 us  [body(): y = lax.ppermute(p_after, MA, to_y)]
  transfers between devices with their start and end apart: 8 -> 10, of which waited for: 6 -> 7; matrix products, arithmetic and copies ran while one was open for 3% -> 3% of each run, Pallas kernels for 22% -> 22%
where the time goes in v5:
time: 101 us
  waiting for transfers between devices  37.6 us (37%)
  starting transfers between devices  30.2 us (30%)
  Pallas kernels  28.3 us (28%)
  local copies, waits for them, and re-layouts  2.57 us (3%)
  other arithmetic  1.58 us (2%)
    all_to_all x2, starting transfers between devices, total(): return jnp.sum(lax.all_to_all(copies, axes, 0, 0, tiled=True), axis=0)  16.6 us
    ppermute x1, waiting for transfers between devices, body(): x = lax.ppermute(p, MA, to_x)  13.6 us
    ppermute x1, waiting for transfers between devices, body(): y = lax.ppermute(p_after, MA, to_y)  12.2 us
    pallas_call x2, Pallas kernels, finish(): pl.pallas_call(lambda *refs: finish_kernel(base, *refs), out_shape=jax.Sh...  8.77 us
    pallas_call x1, Pallas kernels, near(): pl.pallas_call(near_kernel, out_shape=(jax.ShapeDtypeStruct(p.shape, F32)...  6.91 us
    all_to_all x2, waiting for transfers between devices, total(): return jnp.sum(lax.all_to_all(copies, axes, 0, 0, tiled=True), axis=0)  5.55 us
    pallas_call x1, Pallas kernels, mix(): pl.pallas_call(mix_kernel, out_shape=[QUARTER] * 4, grid_spec=pltpu.Prefe...  4.05 us
    ppermute x1, starting transfers between devices, body(): y = lax.ppermute(p_after, MA, to_y)  3.83 us
  transfers between devices with their start and end apart: 10, of which 7 were waited for; matrix products, arithmetic and copies ran while one was open for 3% of the time, Pallas kernels for 22%

profile of v5, /device:TPU:1, one launch (start us, length us, event | category | flops | bytes accessed | tf_op | source)
XLA Modules:
  0.0 100.9 jit_solution(7055884982440566286)
XLA Ops:
  0.6 3.1 %pack.1.p_ref.refs_4_ = f32[4,18,56,128]{3,2,1,0:T(8,128)} custom-call(f32[18,20,2,1280]{3,2,1,0:T(2,128)} %bitcast.20), custom_call_target="tpu_custom_call" | custom-call | tf_op jit(solution)/shard_map/pack/pallas_call | solution.py:61
  3.8 0.0 copy-start.2
  3.8 2.5 %collective-permute-start = (f32[4,18,56,128]{3,2,1,0:T(8,128)}, f32[4,18,56,128]{3,2,1,0:T(8,128)}, u32[]{:S(2)}, u32[]{:S(2)}) collective-permute-start(f32[4,18,56,128]{3,2,1,0:T(8,128)} %pack.1.p_ref.refs_4_), channel_id=1, source_target_pairs={{0,4},{4,12},{8,0},{12,20},{16,8},{20,28},{24,16},{28,36},{32,24},... | collective-permute-start | bytes 6193160 | tf_op jit(solution)/shard_map/ppermute | solution.py:369
  6.2 0.8 collective-permute-start.1
  7.0 3.6 %all-to-all-start = ((f32[4,18,56,128]{3,2,1,0:T(8,128)}), f32[4,18,56,128]{3,2,1,0:T(8,128)S(1)}, u32[]{:S(2)}, u32[]{:S(2)}) async-start(f32[4,18,56,128]{3,2,1,0:T(8,128)} %pack.1.p_ref.refs_4_), calls=%async_computation | async-start | bytes 4128768 | tf_op jit(solution)/shard_map/all_to_all | solution.py:368
  10.6 0.0 copy-start.3
  10.7 0.0 copy-done.2
  10.7 0.2 reshape.35
  10.9 0.9 copy.13
  11.8 0.0 copy-done.3
  11.8 0.1 select_reduce_fusion.d_ref.refs_1_
  11.9 0.0 copy-start.4
  11.9 0.1 copy.14
  12.1 0.7 stack.24.info.refs_0_
  12.7 2.1 %prep.1 = (f32[4,224,128]{2,1,0:T(8,128)}, f32[224,128]{1,0:T(8,128)}, f32[224,128]{1,0:T(8,128)}) custom-call(s32[6]{0:T(128)} %stack.24.info.refs_0_, f32[800,128]{1,0:T(8,128)} %bitcast.30, f32[10,128]{1,0:T(8,128)} %bitcast.34), custom_call_target="tpu_custom_call" | custom-call | tf_op jit(solution)/shard_map/prep/pallas_call | solution.py:110
  14.8 0.8 select_maximum_fusion.w_ref
  15.6 13.6 %collective-permute-done.x_ref = f32[4,18,56,128]{3,2,1,0:T(8,128)} collective-permute-done((f32[4,18,56,128]{3,2,1,0:T(8,128)}, f32[4,18,56,128]{3,2,1,0:T(8,128)}, u32[]{:S(2)}, u32[]{:S(2)}) %collective-permute-start) | collective-permute-done | bytes 2064416 | tf_op jit(solution)/shard_map/ppermute | solution.py:369
  29.2 3.8 %collective-permute-start.2 = (f32[4,18,56,128]{3,2,1,0:T(8,128)}, f32[4,18,56,128]{3,2,1,0:T(8,128)}, u32[]{:S(2)}, u32[]{:S(2)}) collective-permute-start(f32[4,18,56,128]{3,2,1,0:T(8,128)} %pack.1.p_ref.refs_4_), channel_id=1, source_target_pairs={{0,8},{4,0},{8,16},{12,4},{16,24},{20,12},{24,32},{28,20},{32,40},... | collective-permute-start | bytes 6193160 | tf_op jit(solution)/shard_map/ppermute | solution.py:374
  33.0 0.2 collective-permute-start.3
  33.2 2.8 %all-to-all-done = f32[4,18,56,128]{3,2,1,0:T(8,128)S(1)} async-done(((f32[4,18,56,128]{3,2,1,0:T(8,128)}), f32[4,18,56,128]{3,2,1,0:T(8,128)S(1)}, u32[]{:S(2)}, u32[]{:S(2)}) %all-to-all-start) | async-done | bytes 2064416 | tf_op jit(solution)/shard_map/all_to_all | solution.py:368
  36.0 4.1 %mix.1 = (f32[18,56,128]{2,1,0:T(8,128)}, f32[18,56,128]{2,1,0:T(8,128)}, f32[18,56,128]{2,1,0:T(8,128)}, f32[18,56,128]{2,1,0:T(8,128)}) custom-call(s32[6]{0:T(128)} %stack.24.info.refs_0_, f32[96,217]{1,0:T(8,128)} %select_maximum_fusion.w_ref, f32[4,56,128]{2,1,0:T(8,128)} %bitcast.22, f32[72,56,128]{2,1,0:T(8,128)S(1)} %bitcast.18), custom_call_target="tpu_custom_call" | custom-call | tf_op jit(solution)/shard_map/mix/pallas_call | solution.py:149
  40.1 0.3 collective-permute-start.4
  40.4 1.8 %collective-permute-start.5 = (f32[18,56,128]{2,1,0:T(8,128)}, f32[18,56,128]{2,1,0:T(8,128)S(1)}, u32[]{:S(2)}, u32[]{:S(2)}) collective-permute-start(f32[18,56,128]{2,1,0:T(8,128)} %get-tuple-element.37), channel_id=1, source_target_pairs={{0,2},{1,3},{2,0},{3,1},{4,6},{5,7},{6,4},{7,5},{8,10},{9,11},{10,... | collective-permute-start | bytes 1548296 | tf_op jit(solution)/shard_map/ppermute | solution.py:367
  42.2 0.0 collective-permute-done.1.q_ref
  42.2 0.6 collective-permute-start.6
  42.8 12.2 %collective-permute-done.2.y_ref = f32[4,18,56,128]{3,2,1,0:T(8,128)} collective-permute-done((f32[4,18,56,128]{3,2,1,0:T(8,128)}, f32[4,18,56,128]{3,2,1,0:T(8,128)}, u32[]{:S(2)}, u32[]{:S(2)}) %collective-permute-start.2) | collective-permute-done | bytes 2064416 | tf_op jit(solution)/shard_map/ppermute | solution.py:374
  55.0 0.0 collective-permute-done.3.z_ref
  55.0 0.0 copy-done.4
  55.0 6.9 %near.1 = (f32[4,18,56,128]{3,2,1,0:T(8,128)}, f32[4,18,56,128]{3,2,1,0:T(8,128)S(1)}, f32[1,8,128]{2,1,0:T(8,128)}) custom-call(s32[6]{0:T(128)} %stack.24.info.refs_0_, f32[72]{0:T(128)} %copy-done.4, f32[4,4,56,128]{3,2,1,0:T(8,128)} %bitcast.31, f32[4,56,128]{2,1,0:T(8,128)} %bitcast.23, f32[4,56,128]{2,1,0:T(8,128)} %bitcast.26, ...), custom_call_target="tpu_custom_call" | custom-call | tf_op jit(solution)/shard_map/near/pallas_call | solution.py:239
  61.9 0.0 collective-permute-done.4.refs_1_.refs_7_
  61.9 0.0 copy-start
  61.9 1.9 %collective-permute-done.5.refs_2_.refs_8_ = f32[18,56,128]{2,1,0:T(8,128)S(1)} collective-permute-done((f32[18,56,128]{2,1,0:T(8,128)}, f32[18,56,128]{2,1,0:T(8,128)S(1)}, u32[]{:S(2)}, u32[]{:S(2)}) %collective-permute-start.5) | collective-permute-done | bytes 516128 | tf_op jit(solution)/shard_map/ppermute | solution.py:367
  63.8 0.0 copy-start.1
  63.8 1.5 %collective-permute-done.6.refs_3_.refs_9_ = f32[18,56,128]{2,1,0:T(8,128)} collective-permute-done((f32[18,56,128]{2,1,0:T(8,128)}, f32[18,56,128]{2,1,0:T(8,128)}, u32[]{:S(2)}, u32[]{:S(2)}) %collective-permute-start.6) | collective-permute-done | bytes 516128 | tf_op jit(solution)/shard_map/ppermute | solution.py:367
  65.3 0.0 copy-done
  65.3 0.0 copy-done.1
  65.3 3.3 %squares.1 = f32[16,8,128]{2,1,0:T(8,128)} custom-call(s32[6]{0:T(128)} %stack.24.info.refs_0_, f32[1,8,128]{2,1,0:T(8,128)} %get-tuple-element.44.v_ref, f32[4,56,128]{2,1,0:T(8,128)} %bitcast.27, f32[4,18,56,128]{3,2,1,0:T(8,128)S(1)} %get-tuple-element.45.part_ref, f32[18,56,128]{2,1,0:T(8,128)} %get-tuple-element.40.refs_0_.refs_6_, ...), custom_call_target="tpu_custom_call" | custom-call | tf_op jit(solution)/shard_map/squares/pallas_call | solution.py:330
  68.6 10.7 %all-to-all-start.1 = ((f32[16,8,128]{2,1,0:T(8,128)}), f32[16,8,128]{2,1,0:T(8,128)S(1)}, u32[]{:S(2)}, u32[]{:S(2)}) async-start(f32[16,8,128]{2,1,0:T(8,128)} %squares.1), calls=%async_computation.1 | async-start | bytes 131072 | tf_op jit(solution)/shard_map/all_to_all | solution.py:355
  79.4 4.4 %finish.2.refs_10_ = f32[18,20,2,1280]{3,2,1,0:T(2,128)} custom-call(s32[6]{0:T(128)} %stack.24.info.refs_0_, f32[72]{0:T(128)} %copy-done.4, f32[4,56,128]{2,1,0:T(8,128)} %bitcast.24, f32[4,56,128]{2,1,0:T(8,128)} %bitcast.28, f32[4,18,56,128]{3,2,1,0:T(8,128)} %pack.1.p_ref.refs_4_, f32[4,18,56,128]{3,2,1,0:T(8,128)} %get-tuple-element.39.refs_5_, ...), custom_call_target="tpu_custom_call" | custom-call | tf_op jit(solution)/shard_map/finish/pallas_call | solution.py:275
  83.8 3.4 %all-to-all-done.1 = f32[16,8,128]{2,1,0:T(8,128)S(1)} async-done(((f32[16,8,128]{2,1,0:T(8,128)}), f32[16,8,128]{2,1,0:T(8,128)S(1)}, u32[]{:S(2)}, u32[]{:S(2)}) %all-to-all-start.1) | async-done | bytes 65568 | tf_op jit(solution)/shard_map/all_to_all | solution.py:355
  87.2 0.6 broadcast_in_dim.10
  87.8 5.9 %all-to-all-start.2 = ((f32[16,8,128]{2,1,0:T(8,128)}), f32[16,8,128]{2,1,0:T(8,128)S(1)}, u32[]{:S(2)}, u32[]{:S(2)}) async-start(f32[16,8,128]{2,1,0:T(8,128)} %broadcast_in_dim.10), calls=%async_computation.2 | async-start | bytes 131072 | tf_op jit(solution)/shard_map/all_to_all | solution.py:355
  93.7 4.4 %finish.3 = f32[18,20,2,1280]{3,2,1,0:T(2,128)} custom-call(s32[6]{0:T(128)} %stack.24.info.refs_0_, f32[72]{0:T(128)} %copy-done.4, f32[4,56,128]{2,1,0:T(8,128)} %bitcast.25, f32[4,56,128]{2,1,0:T(8,128)} %bitcast.29, f32[4,18,56,128]{3,2,1,0:T(8,128)} %pack.1.p_ref.refs_4_, ...), custom_call_target="tpu_custom_call", output_to_operand_aliasing={{}: (10, {})} | custom-call | tf_op jit(solution)/shard_map/finish/pallas_call | solution.py:275
  98.1 2.1 %all-to-all-done.2 = f32[16,8,128]{2,1,0:T(8,128)S(1)} async-done(((f32[16,8,128]{2,1,0:T(8,128)}), f32[16,8,128]{2,1,0:T(8,128)S(1)}, u32[]{:S(2)}, u32[]{:S(2)}) %all-to-all-start.2) | async-done | bytes 65568 | tf_op jit(solution)/shard_map/all_to_all | solution.py:355
  100.3 0.6 sqrt_reduce_fusion
  (5 shorter events, 0.1 us)
Async XLA Ops:
  3.8 6.9 %copy-start.2 = (f32[4,20,1280]{2,0,1:T(4,128)S(1)}, f32[4,20,1280]{2,0,1:T(4,128)}, u32[]{:S(2)}) copy-start(f32[4,20,1280]{2,0,1:T(4,128)} %param.5) | copy-start | bytes 1228804
  3.8 25.4 %collective-permute-start = (f32[4,18,56,128]{3,2,1,0:T(8,128)}, f32[4,18,56,128]{3,2,1,0:T(8,128)}, u32[]{:S(2)}, u32[]{:S(2)}) collective-permute-start(f32[4,18,56,128]{3,2,1,0:T(8,128)} %pack.1.p_ref.refs_4_), channel_id=1, source_target_pairs={{0,4},{4,12},{8,0},{12,20},{16,8},{20,28},{24,16},{28,36},{32,24},... | collective-permute-start | bytes 6193160 | tf_op jit(solution)/shard_map/ppermute | solution.py:369
  6.2 35.9 %collective-permute-start.1 = (f32[4,18,56,128]{3,2,1,0:T(8,128)}, f32[4,18,56,128]{3,2,1,0:T(8,128)}, u32[]{:S(2)}, u32[]{:S(2)}) collective-permute-start(f32[4,18,56,128]{3,2,1,0:T(8,128)} %pack.1.p_ref.refs_4_), channel_id=1, source_target_pairs={{0,4},{4,0},{8,12},{12,8},{16,20},{20,16},{24,28},{28,24},{32,36},... | collective-permute-start | bytes 6193160 | tf_op jit(solution)/shard_map/ppermute | solution.py:370
  7.0 29.0 %all-to-all-start = ((f32[4,18,56,128]{3,2,1,0:T(8,128)}), f32[4,18,56,128]{3,2,1,0:T(8,128)S(1)}, u32[]{:S(2)}, u32[]{:S(2)}) async-start(f32[4,18,56,128]{3,2,1,0:T(8,128)} %pack.1.p_ref.refs_4_), calls=%async_computation | async-start | bytes 4128768 | tf_op jit(solution)/shard_map/all_to_all | solution.py:368
  10.6 1.2 %copy-start.3 = (f32[72,72]{1,0:T(8,128)S(1)}, f32[72,72]{1,0:T(8,128)}, u32[]{:S(2)}) copy-start(f32[72,72]{1,0:T(8,128)} %param.7) | copy-start | bytes 62212
  11.9 43.0 %copy-start.4 = (f32[72]{0:T(128)}, f32[72]{0:T(128)S(1)}, u32[]{:S(2)}) copy-start(f32[72]{0:T(128)S(1)} %select_reduce_fusion.d_ref.refs_1_) | copy-start | bytes 868
  29.2 25.8 %collective-permute-start.2 = (f32[4,18,56,128]{3,2,1,0:T(8,128)}, f32[4,18,56,128]{3,2,1,0:T(8,128)}, u32[]{:S(2)}, u32[]{:S(2)}) collective-permute-start(f32[4,18,56,128]{3,2,1,0:T(8,128)} %pack.1.p_ref.refs_4_), channel_id=1, source_target_pairs={{0,8},{4,0},{8,16},{12,4},{16,24},{20,12},{24,32},{28,20},{32,40},... | collective-permute-start | bytes 6193160 | tf_op jit(solution)/shard_map/ppermute | solution.py:374
  33.0 22.0 %collective-permute-start.3 = (f32[4,18,56,128]{3,2,1,0:T(8,128)}, f32[4,18,56,128]{3,2,1,0:T(8,128)}, u32[]{:S(2)}, u32[]{:S(2)}) collective-permute-start(f32[4,18,56,128]{3,2,1,0:T(8,128)} %collective-permute-done.x_ref), channel_id=1, source_target_pairs={{0,4},{4,0},{8,12},{12,8},{16,20},{20,16},{24,28},{28,24},{32,36},... | collective-permute-start | bytes 6193160 | tf_op jit(solution)/shard_map/ppermute | solution.py:375
  40.1 21.8 %collective-permute-start.4 = (f32[18,56,128]{2,1,0:T(8,128)}, f32[18,56,128]{2,1,0:T(8,128)S(1)}, u32[]{:S(2)}, u32[]{:S(2)}) collective-permute-start(f32[18,56,128]{2,1,0:T(8,128)} %get-tuple-element.36), channel_id=1, source_target_pairs={{0,1},{1,2},{2,3},{3,0},{4,5},{5,6},{6,7},{7,4},{8,9},{9,10},{10,1... | collective-permute-start | bytes 1548296 | tf_op jit(solution)/shard_map/ppermute | solution.py:367
  40.4 23.4 %collective-permute-start.5 = (f32[18,56,128]{2,1,0:T(8,128)}, f32[18,56,128]{2,1,0:T(8,128)S(1)}, u32[]{:S(2)}, u32[]{:S(2)}) collective-permute-start(f32[18,56,128]{2,1,0:T(8,128)} %get-tuple-element.37), channel_id=1, source_target_pairs={{0,2},{1,3},{2,0},{3,1},{4,6},{5,7},{6,4},{7,5},{8,10},{9,11},{10,... | collective-permute-start | bytes 1548296 | tf_op jit(solution)/shard_map/ppermute | solution.py:367
  42.2 23.1 %collective-permute-start.6 = (f32[18,56,128]{2,1,0:T(8,128)}, f32[18,56,128]{2,1,0:T(8,128)}, u32[]{:S(2)}, u32[]{:S(2)}) collective-permute-start(f32[18,56,128]{2,1,0:T(8,128)} %get-tuple-element.38), channel_id=1, source_target_pairs={{0,3},{1,0},{2,1},{3,2},{4,7},{5,4},{6,5},{7,6},{8,11},{9,8},{10,9... | collective-permute-start | bytes 1548296 | tf_op jit(solution)/shard_map/ppermute | solution.py:367
  61.9 3.4 %copy-start = (f32[18,56,128]{2,1,0:T(8,128)}, f32[18,56,128]{2,1,0:T(8,128)S(1)}, u32[]{:S(2)}) copy-start(f32[18,56,128]{2,1,0:T(8,128)S(1)} %collective-permute-done.4.refs_1_.refs_7_) | copy-start | bytes 1548292
  63.8 1.5 %copy-start.1 = (f32[18,56,128]{2,1,0:T(8,128)}, f32[18,56,128]{2,1,0:T(8,128)S(1)}, u32[]{:S(2)}) copy-start(f32[18,56,128]{2,1,0:T(8,128)S(1)} %collective-permute-done.5.refs_2_.refs_8_) | copy-start | bytes 1548292
  68.6 18.5 %all-to-all-start.1 = ((f32[16,8,128]{2,1,0:T(8,128)}), f32[16,8,128]{2,1,0:T(8,128)S(1)}, u32[]{:S(2)}, u32[]{:S(2)}) async-start(f32[16,8,128]{2,1,0:T(8,128)} %squares.1), calls=%async_computation.1 | async-start | bytes 131072 | tf_op jit(solution)/shard_map/all_to_all | solution.py:355
  87.8 12.4 %all-to-all-start.2 = ((f32[16,8,128]{2,1,0:T(8,128)}), f32[16,8,128]{2,1,0:T(8,128)S(1)}, u32[]{:S(2)}, u32[]{:S(2)}) async-start(f32[16,8,128]{2,1,0:T(8,128)} %broadcast_in_dim.10), calls=%async_computation.2 | async-start | bytes 131072 | tf_op jit(solution)/shard_map/all_to_all | solution.py:355

commit v6 on v5

--- a/solution.py
+++ b/solution.py
@@ -3,6 +3,7 @@
 from jax import lax
 from jax.experimental import pallas as pl
 from jax.experimental.pallas import tpu as pltpu
+from jax.experimental.layout import Layout, with_layout_constraint
 from jax.sharding import Mesh
 from jax.sharding import PartitionSpec as P
 
@@ -19,6 +20,7 @@
 F32 = jnp.float32
 VMEM = pl.BlockSpec(memory_space=pltpu.VMEM)
 SMEM = pl.BlockSpec(memory_space=pltpu.SMEM)
+FAR = pl.BlockSpec(memory_space=pl.ANY)
 QUARTER = jax.ShapeDtypeStruct((OWN, QROWS, 128), F32)
 
 
@@ -40,32 +42,71 @@
     return out
 
 
-LIVE = [
-    (2 * t + par, j, par * HALF + start_row(t) + 2 * (j - t)) for par in range(2) for t in range(TILES) for j in range(t, TILES)
-]
+def quarters(moves):
+    out = []
+    for s, d, n in moves:
+        while n:
+            step = min(n, QROWS - d % QROWS)
+            out.append((s, d, step))
+            s, d, n = s + step, d + step, n - step
+    return out
+
+
+LIVE = [((2 * t + par) * 20 + 2 * t, par * HALF + start_row(t), 20 - 2 * t) for par in range(2) for t in range(TILES)]
 DOWN = cut(
     [(start_row(t + 1), HALF + start_row(t) + 2, 18 - 2 * t) for t in range(TILES - 1)]
     + [(HALF + start_row(t - 1) + 2, start_row(t), 20 - 2 * t) for t in range(1, TILES)]
 )
 
 
-def pack_kernel(x_ref, p_ref):
-    for fold, j, row in LIVE:
-        q, r = divmod(row, QROWS)
-        p_ref[q, :, r : r + 2, :] = x_ref[:, fold, :, 128 * j : 128 * j + 128]
-    for q in (1, 3):
-        p_ref[q, :, QROWS - 2 :, :] = jnp.zeros((p_ref.shape[1], 2, 128), F32)
+PART = 3
+PARTS = OWN // PART
+
+
+def pack_kernel(x_ref, p_ref, x_buf, p_buf, in_sem, out_sem):
+    own = [pl.ds(c * PART, PART) for c in range(PARTS)]
+    loads = [pltpu.make_async_copy(x_ref.at[o], x_buf.at[o], in_sem.at[c]) for c, o in enumerate(own)]
+    stores = [pltpu.make_async_copy(p_buf.at[:, o], p_ref.at[:, o], out_sem.at[c]) for c, o in enumerate(own)]
+    for load in loads:
+        load.start()
+    for load, store, o in zip(loads, stores, own):
+        load.wait()
+        for s, d, n in quarters(LIVE):
+            q, r = divmod(d, QROWS)
+            p_buf[q, o, r : r + n, :] = x_buf[o, s : s + n, :]
+        for q in (1, 3):
+            p_buf[q, o, QROWS - 2 :, :] = jnp.zeros((PART, 2, 128), F32)
+        store.start()
+    for store in stores:
+        store.wait()
 
 
 def pack(x):
+    packed = (4, OWN, QROWS, 128)
     return pl.pallas_call(
         pack_kernel,
-        out_shape=jax.ShapeDtypeStruct((4, OWN, QROWS, 128), F32),
-        grid=(OWN // STEP,),
-        in_specs=[pl.BlockSpec((STEP, FOLDS, 2, WAVES), lambda i: (i, 0, 0, 0))],
-        out_specs=pl.BlockSpec((4, STEP, QROWS, 128), lambda i: (0, i, 0, 0)),
+        out_shape=jax.ShapeDtypeStruct(packed, F32),
+        in_specs=[FAR],
+        out_specs=FAR,
+        scratch_shapes=[
+            pltpu.VMEM(x.shape, F32),
+            pltpu.VMEM(packed, F32),
+            pltpu.SemaphoreType.DMA((PARTS,)),
+            pltpu.SemaphoreType.DMA((PARTS,)),
+        ],
         name="pack",
     )(x)
+
+
+def as_rows(x):
+    tiles = with_layout_constraint(x.reshape(OWN, 2, FOLDS, TILES, 128), Layout(major_to_minor=(0, 2, 3, 1, 4)))
+    return tiles.transpose(0, 2, 3, 1, 4).reshape(OWN, 400, 128)
+
+
+def from_rows(rows):
+    tiles = rows.reshape(OWN, FOLDS, TILES, 2, 128).transpose(0, 3, 1, 2, 4)
+    tiles = with_layout_constraint(tiles, Layout(major_to_minor=(0, 2, 3, 1, 4)))
+    return tiles.reshape(OWN, 2, FOLDS, WAVES)
 
 
 BASES = (1, 2, -2, -1)
@@ -261,11 +302,10 @@
             scale = 1.0 / (1.0 + hp_ref[q] * d)
             residual = part_ref[q, l] - refs[away][l] * live
             buf[l, pl.ds(pl.multiple_of(q * QROWS, 8), QROWS), :] = scale * (p_ref[q, l] * live + residual)
-    for t in range(1, TILES):
-        for par in range(2):
-            o_ref[:, 2 * t + par, :, : 128 * t] = jnp.zeros((FINISH_STEP, 2, 128 * t), F32)
-    for fold, j, row in LIVE:
-        o_ref[:, fold, :, 128 * j : 128 * j + 128] = buf[:, row : row + 2, :]
+    for s, d, n in LIVE:
+        if n < 20:
+            o_ref[:, s + n - 20 : s, :] = jnp.zeros((FINISH_STEP, 20 - n, 128), F32)
+        o_ref[:, s : s + n, :] = buf[:, d : d + n, :]
 
 
 def finish(base, info, diag, hp, live, p, part, m, *before):
@@ -274,7 +314,7 @@
     piece = pl.BlockSpec((FINISH_STEP, QROWS, 128), lambda i, s: (i + at, 0, 0))
     return pl.pallas_call(
         lambda *refs: finish_kernel(base, *refs),
-        out_shape=jax.ShapeDtypeStruct((OWN, FOLDS, 2, WAVES), F32),
+        out_shape=jax.ShapeDtypeStruct((OWN, 400, 128), F32),
         grid_spec=pltpu.PrefetchScalarGridSpec(
             num_scalar_prefetch=1,
             grid=(OWN // 2 // FINISH_STEP,),
@@ -282,7 +322,7 @@
             + [block] * 2
             + [piece] * 4
             + [pl.BlockSpec(memory_space=pl.ANY)] * len(before),
-            out_specs=pl.BlockSpec((FINISH_STEP, FOLDS, 2, WAVES), lambda i, s: (i + at, 0, 0, 0)),
+            out_specs=pl.BlockSpec((FINISH_STEP, 400, 128), lambda i, s: (i + at, 0, 0)),
             scratch_shapes=[pltpu.VMEM((FINISH_STEP, 2 * HALF, 128), F32)],
         ),
         input_output_aliases={10: 0} if before else {},
@@ -362,7 +402,7 @@
     modes = [jnp.where(owner == low, 2, jnp.where(owner == high, 1, 0)) for low, high in ends.values()]
     info = jnp.stack([owner, owner & 1, lev] + modes).astype(jnp.int32)
     crows = coupling.reshape(4, FOLDS, TILES, 128).transpose(1, 2, 0, 3).reshape(800, 128)
-    p = pack(forcing.transpose(0, 2, 1, 3))
+    p = pack(as_rows(forcing))
     to_x, to_y, swap = routes(OWNERS)
     along = lambda v, away: lax.ppermute(v, "lev", [(i, (i + away) % 4) for i in range(4)])
     every = lax.all_to_all(p, "lev", 0, 0, tiled=True).reshape(LEV, QROWS, 128)
@@ -387,7 +427,7 @@
     sums = total(jnp.broadcast_to(sums[None], (lax.axis_size(outer), 8, 128)), outer)
     rows = finish(OWN // 2, info, diag, hp, live, p, part, m, rows)
     norms = jnp.sqrt(sums[:2, 0] / (LEV * WAVES * (WAVES + 1)))
-    return (rows.transpose(0, 2, 1, 3), norms)
+    return (from_rows(rows), norms)
 
 
 def solution(mesh):

time: 101 us -> 101 us (level)
  no operation moved by 1% of the time
where the time goes in v6:
time: 101 us
  waiting for transfers between devices  37.7 us (37%)
  starting transfers between devices  30.1 us (30%)
  Pallas kernels  27.9 us (28%)
  local copies, waits for them, and re-layouts  2.57 us (3%)
  other arithmetic  1.58 us (2%)
    all_to_all x2, starting transfers between devices, total(): return jnp.sum(lax.all_to_all(copies, axes, 0, 0, tiled=True), axis=0)  16.4 us
    ppermute x1, waiting for transfers between devices, body(): x = lax.ppermute(p, MA, to_x)  13.5 us
    ppermute x1, waiting for transfers between devices, body(): y = lax.ppermute(p_after, MA, to_y)  12 us
    pallas_call x2, Pallas kernels, finish(): pl.pallas_call(lambda *refs: finish_kernel(base, *refs), out_shape=jax.Sh...  8.71 us
    pallas_call x1, Pallas kernels, near(): pl.pallas_call(near_kernel, out_shape=(jax.ShapeDtypeStruct(p.shape, F32)...  6.91 us
    all_to_all x2, waiting for transfers between devices, total(): return jnp.sum(lax.all_to_all(copies, axes, 0, 0, tiled=True), axis=0)  5.61 us
    pallas_call x1, Pallas kernels, mix(): pl.pallas_call(mix_kernel, out_shape=[QUARTER] * 4, grid_spec=pltpu.Prefe...  4.05 us
    ppermute x1, starting transfers between devices, body(): y = lax.ppermute(p_after, MA, to_y)  3.83 us
  transfers between devices with their start and end apart: 10, of which 7 were waited for; matrix products, arithmetic and copies ran while one was open for 3% of the time, Pallas kernels for 22%

profile of v6, /device:TPU:1, one launch (start us, length us, event | category | flops | bytes accessed | tf_op | source)
XLA Modules:
  0.0 100.7 jit_solution(16295721585518434109)
XLA Ops:
  0.6 2.9 %pack.1.p_ref.refs_4_ = f32[4,18,56,128]{3,2,1,0:T(8,128)} custom-call(f32[18,400,128]{2,1,0:T(8,128)} %bitcast.28), custom_call_target="tpu_custom_call" | custom-call | tf_op jit(solution)/shard_map/pack/pallas_call | solution.py:86
  3.5 0.0 copy-start.2
  3.5 2.5 %collective-permute-start = (f32[4,18,56,128]{3,2,1,0:T(8,128)}, f32[4,18,56,128]{3,2,1,0:T(8,128)}, u32[]{:S(2)}, u32[]{:S(2)}) collective-permute-start(f32[4,18,56,128]{3,2,1,0:T(8,128)} %pack.1.p_ref.refs_4_), channel_id=1, source_target_pairs={{0,4},{4,12},{8,0},{12,20},{16,8},{20,28},{24,16},{28,36},{32,24},... | collective-permute-start | bytes 6193160 | tf_op jit(solution)/shard_map/ppermute | solution.py:409
  6.1 0.9 collective-permute-start.1
  7.0 3.6 %all-to-all-start = ((f32[4,18,56,128]{3,2,1,0:T(8,128)}), f32[4,18,56,128]{3,2,1,0:T(8,128)S(1)}, u32[]{:S(2)}, u32[]{:S(2)}) async-start(f32[4,18,56,128]{3,2,1,0:T(8,128)} %pack.1.p_ref.refs_4_), calls=%async_computation | async-start | bytes 4128768 | tf_op jit(solution)/shard_map/all_to_all | solution.py:408
  10.6 0.0 copy-start.3
  10.6 0.0 copy-done.2
  10.6 0.2 reshape.49
  10.8 0.9 copy.13
  11.7 0.0 copy-done.3
  11.8 0.1 select_reduce_fusion.d_ref.refs_1_
  11.9 0.0 copy-start.4
  11.9 0.1 copy.14
  12.0 0.7 stack.24.info.refs_0_
  12.7 2.1 %prep.1 = (f32[4,224,128]{2,1,0:T(8,128)}, f32[224,128]{1,0:T(8,128)}, f32[224,128]{1,0:T(8,128)}) custom-call(s32[6]{0:T(128)} %stack.24.info.refs_0_, f32[800,128]{1,0:T(8,128)} %bitcast.38, f32[10,128]{1,0:T(8,128)} %bitcast.42), custom_call_target="tpu_custom_call" | custom-call | tf_op jit(solution)/shard_map/prep/pallas_call | solution.py:151
  14.8 0.8 select_maximum_fusion.w_ref
  15.5 13.5 %collective-permute-done.x_ref = f32[4,18,56,128]{3,2,1,0:T(8,128)} collective-permute-done((f32[4,18,56,128]{3,2,1,0:T(8,128)}, f32[4,18,56,128]{3,2,1,0:T(8,128)}, u32[]{:S(2)}, u32[]{:S(2)}) %collective-permute-start) | collective-permute-done | bytes 2064416 | tf_op jit(solution)/shard_map/ppermute | solution.py:409
  29.0 3.8 %collective-permute-start.2 = (f32[4,18,56,128]{3,2,1,0:T(8,128)}, f32[4,18,56,128]{3,2,1,0:T(8,128)}, u32[]{:S(2)}, u32[]{:S(2)}) collective-permute-start(f32[4,18,56,128]{3,2,1,0:T(8,128)} %pack.1.p_ref.refs_4_), channel_id=1, source_target_pairs={{0,8},{4,0},{8,16},{12,4},{16,24},{20,12},{24,32},{28,20},{32,40},... | collective-permute-start | bytes 6193160 | tf_op jit(solution)/shard_map/ppermute | solution.py:414
  32.9 0.2 collective-permute-start.3
  33.0 3.1 %all-to-all-done = f32[4,18,56,128]{3,2,1,0:T(8,128)S(1)} async-done(((f32[4,18,56,128]{3,2,1,0:T(8,128)}), f32[4,18,56,128]{3,2,1,0:T(8,128)S(1)}, u32[]{:S(2)}, u32[]{:S(2)}) %all-to-all-start) | async-done | bytes 2064416 | tf_op jit(solution)/shard_map/all_to_all | solution.py:408
  36.1 4.1 %mix.1 = (f32[18,56,128]{2,1,0:T(8,128)}, f32[18,56,128]{2,1,0:T(8,128)}, f32[18,56,128]{2,1,0:T(8,128)}, f32[18,56,128]{2,1,0:T(8,128)}) custom-call(s32[6]{0:T(128)} %stack.24.info.refs_0_, f32[96,217]{1,0:T(8,128)} %select_maximum_fusion.w_ref, f32[4,56,128]{2,1,0:T(8,128)} %bitcast.30, f32[72,56,128]{2,1,0:T(8,128)S(1)} %bitcast.26), custom_call_target="tpu_custom_call" | custom-call | tf_op jit(solution)/shard_map/mix/pallas_call | solution.py:190
  40.1 0.3 collective-permute-start.4
  40.4 1.8 %collective-permute-start.5 = (f32[18,56,128]{2,1,0:T(8,128)}, f32[18,56,128]{2,1,0:T(8,128)S(1)}, u32[]{:S(2)}, u32[]{:S(2)}) collective-permute-start(f32[18,56,128]{2,1,0:T(8,128)} %get-tuple-element.37), channel_id=1, source_target_pairs={{0,2},{1,3},{2,0},{3,1},{4,6},{5,7},{6,4},{7,5},{8,10},{9,11},{10,... | collective-permute-start | bytes 1548296 | tf_op jit(solution)/shard_map/ppermute | solution.py:407
  42.2 0.0 collective-permute-done.1.q_ref
  42.2 0.6 collective-permute-start.6
  42.8 12.0 %collective-permute-done.2.y_ref = f32[4,18,56,128]{3,2,1,0:T(8,128)} collective-permute-done((f32[4,18,56,128]{3,2,1,0:T(8,128)}, f32[4,18,56,128]{3,2,1,0:T(8,128)}, u32[]{:S(2)}, u32[]{:S(2)}) %collective-permute-start.2) | collective-permute-done | bytes 2064416 | tf_op jit(solution)/shard_map/ppermute | solution.py:414
  54.8 0.0 collective-permute-done.3.z_ref
  54.8 0.0 copy-done.4
  54.8 6.9 %near.1 = (f32[4,18,56,128]{3,2,1,0:T(8,128)}, f32[4,18,56,128]{3,2,1,0:T(8,128)S(1)}, f32[1,8,128]{2,1,0:T(8,128)}) custom-call(s32[6]{0:T(128)} %stack.24.info.refs_0_, f32[72]{0:T(128)} %copy-done.4, f32[4,4,56,128]{3,2,1,0:T(8,128)} %bitcast.39, f32[4,56,128]{2,1,0:T(8,128)} %bitcast.31, f32[4,56,128]{2,1,0:T(8,128)} %bitcast.34, ...), custom_call_target="tpu_custom_call" | custom-call | tf_op jit(solution)/shard_map/near/pallas_call | solution.py:280
  61.7 0.0 collective-permute-done.4.refs_1_.refs_7_
  61.7 0.0 copy-start
  61.7 2.2 %collective-permute-done.5.refs_2_.refs_8_ = f32[18,56,128]{2,1,0:T(8,128)S(1)} collective-permute-done((f32[18,56,128]{2,1,0:T(8,128)}, f32[18,56,128]{2,1,0:T(8,128)S(1)}, u32[]{:S(2)}, u32[]{:S(2)}) %collective-permute-start.5) | collective-permute-done | bytes 516128 | tf_op jit(solution)/shard_map/ppermute | solution.py:407
  63.9 0.0 copy-start.1
  63.9 1.4 %collective-permute-done.6.refs_3_.refs_9_ = f32[18,56,128]{2,1,0:T(8,128)} collective-permute-done((f32[18,56,128]{2,1,0:T(8,128)}, f32[18,56,128]{2,1,0:T(8,128)}, u32[]{:S(2)}, u32[]{:S(2)}) %collective-permute-start.6) | collective-permute-done | bytes 516128 | tf_op jit(solution)/shard_map/ppermute | solution.py:407
  65.3 0.0 copy-done
  65.3 0.0 copy-done.1
  65.3 3.3 %squares.1 = f32[16,8,128]{2,1,0:T(8,128)} custom-call(s32[6]{0:T(128)} %stack.24.info.refs_0_, f32[1,8,128]{2,1,0:T(8,128)} %get-tuple-element.44.v_ref, f32[4,56,128]{2,1,0:T(8,128)} %bitcast.35, f32[4,18,56,128]{3,2,1,0:T(8,128)S(1)} %get-tuple-element.45.part_ref, f32[18,56,128]{2,1,0:T(8,128)} %get-tuple-element.40.refs_0_.refs_6_, ...), custom_call_target="tpu_custom_call" | custom-call | tf_op jit(solution)/shard_map/squares/pallas_call | solution.py:370
  68.7 10.5 %all-to-all-start.1 = ((f32[16,8,128]{2,1,0:T(8,128)}), f32[16,8,128]{2,1,0:T(8,128)S(1)}, u32[]{:S(2)}, u32[]{:S(2)}) async-start(f32[16,8,128]{2,1,0:T(8,128)} %squares.1), calls=%async_computation.1 | async-start | bytes 131072 | tf_op jit(solution)/shard_map/all_to_all | solution.py:395
  79.2 4.3 %finish.2.refs_10_ = f32[18,400,128]{2,1,0:T(8,128)} custom-call(s32[6]{0:T(128)} %stack.24.info.refs_0_, f32[72]{0:T(128)} %copy-done.4, f32[4,56,128]{2,1,0:T(8,128)} %bitcast.32, f32[4,56,128]{2,1,0:T(8,128)} %bitcast.36, f32[4,18,56,128]{3,2,1,0:T(8,128)} %pack.1.p_ref.refs_4_, f32[4,18,56,128]{3,2,1,0:T(8,128)} %get-tuple-element.39.refs_5_, ...), custom_call_target="tpu_custom_call" | custom-call | tf_op jit(solution)/shard_map/finish/pallas_call | solution.py:315
  83.5 3.5 %all-to-all-done.1 = f32[16,8,128]{2,1,0:T(8,128)S(1)} async-done(((f32[16,8,128]{2,1,0:T(8,128)}), f32[16,8,128]{2,1,0:T(8,128)S(1)}, u32[]{:S(2)}, u32[]{:S(2)}) %all-to-all-start.1) | async-done | bytes 65568 | tf_op jit(solution)/shard_map/all_to_all | solution.py:395
  87.0 0.6 broadcast_in_dim.10
  87.6 5.9 %all-to-all-start.2 = ((f32[16,8,128]{2,1,0:T(8,128)}), f32[16,8,128]{2,1,0:T(8,128)S(1)}, u32[]{:S(2)}, u32[]{:S(2)}) async-start(f32[16,8,128]{2,1,0:T(8,128)} %broadcast_in_dim.10), calls=%async_computation.2 | async-start | bytes 131072 | tf_op jit(solution)/shard_map/all_to_all | solution.py:395
  93.5 4.4 %finish.3 = f32[18,400,128]{2,1,0:T(8,128)} custom-call(s32[6]{0:T(128)} %stack.24.info.refs_0_, f32[72]{0:T(128)} %copy-done.4, f32[4,56,128]{2,1,0:T(8,128)} %bitcast.33, f32[4,56,128]{2,1,0:T(8,128)} %bitcast.37, f32[4,18,56,128]{3,2,1,0:T(8,128)} %pack.1.p_ref.refs_4_, ...), custom_call_target="tpu_custom_call", output_to_operand_aliasing={{}: (10, {})} | custom-call | tf_op jit(solution)/shard_map/finish/pallas_call | solution.py:315
  97.9 2.2 %all-to-all-done.2 = f32[16,8,128]{2,1,0:T(8,128)S(1)} async-done(((f32[16,8,128]{2,1,0:T(8,128)}), f32[16,8,128]{2,1,0:T(8,128)S(1)}, u32[]{:S(2)}, u32[]{:S(2)}) %all-to-all-start.2) | async-done | bytes 65568 | tf_op jit(solution)/shard_map/all_to_all | solution.py:395
  100.1 0.6 sqrt_reduce_fusion
  (5 shorter events, 0.1 us)
Async XLA Ops:
  3.5 7.1 %copy-start.2 = (f32[4,20,1280]{2,0,1:T(4,128)S(1)}, f32[4,20,1280]{2,0,1:T(4,128)}, u32[]{:S(2)}) copy-start(f32[4,20,1280]{2,0,1:T(4,128)} %param.5) | copy-start | bytes 1228804
  3.5 25.5 %collective-permute-start = (f32[4,18,56,128]{3,2,1,0:T(8,128)}, f32[4,18,56,128]{3,2,1,0:T(8,128)}, u32[]{:S(2)}, u32[]{:S(2)}) collective-permute-start(f32[4,18,56,128]{3,2,1,0:T(8,128)} %pack.1.p_ref.refs_4_), channel_id=1, source_target_pairs={{0,4},{4,12},{8,0},{12,20},{16,8},{20,28},{24,16},{28,36},{32,24},... | collective-permute-start | bytes 6193160 | tf_op jit(solution)/shard_map/ppermute | solution.py:409
  6.1 36.1 %collective-permute-start.1 = (f32[4,18,56,128]{3,2,1,0:T(8,128)}, f32[4,18,56,128]{3,2,1,0:T(8,128)}, u32[]{:S(2)}, u32[]{:S(2)}) collective-permute-start(f32[4,18,56,128]{3,2,1,0:T(8,128)} %pack.1.p_ref.refs_4_), channel_id=1, source_target_pairs={{0,4},{4,0},{8,12},{12,8},{16,20},{20,16},{24,28},{28,24},{32,36},... | collective-permute-start | bytes 6193160 | tf_op jit(solution)/shard_map/ppermute | solution.py:410
  7.0 29.1 %all-to-all-start = ((f32[4,18,56,128]{3,2,1,0:T(8,128)}), f32[4,18,56,128]{3,2,1,0:T(8,128)S(1)}, u32[]{:S(2)}, u32[]{:S(2)}) async-start(f32[4,18,56,128]{3,2,1,0:T(8,128)} %pack.1.p_ref.refs_4_), calls=%async_computation | async-start | bytes 4128768 | tf_op jit(solution)/shard_map/all_to_all | solution.py:408
  10.6 1.2 %copy-start.3 = (f32[72,72]{1,0:T(8,128)S(1)}, f32[72,72]{1,0:T(8,128)}, u32[]{:S(2)}) copy-start(f32[72,72]{1,0:T(8,128)} %param.7) | copy-start | bytes 62212
  11.9 42.9 %copy-start.4 = (f32[72]{0:T(128)}, f32[72]{0:T(128)S(1)}, u32[]{:S(2)}) copy-start(f32[72]{0:T(128)S(1)} %select_reduce_fusion.d_ref.refs_1_) | copy-start | bytes 868
  29.0 25.8 %collective-permute-start.2 = (f32[4,18,56,128]{3,2,1,0:T(8,128)}, f32[4,18,56,128]{3,2,1,0:T(8,128)}, u32[]{:S(2)}, u32[]{:S(2)}) collective-permute-start(f32[4,18,56,128]{3,2,1,0:T(8,128)} %pack.1.p_ref.refs_4_), channel_id=1, source_target_pairs={{0,8},{4,0},{8,16},{12,4},{16,24},{20,12},{24,32},{28,20},{32,40},... | collective-permute-start | bytes 6193160 | tf_op jit(solution)/shard_map/ppermute | solution.py:414
  32.9 21.9 %collective-permute-start.3 = (f32[4,18,56,128]{3,2,1,0:T(8,128)}, f32[4,18,56,128]{3,2,1,0:T(8,128)}, u32[]{:S(2)}, u32[]{:S(2)}) collective-permute-start(f32[4,18,56,128]{3,2,1,0:T(8,128)} %collective-permute-done.x_ref), channel_id=1, source_target_pairs={{0,4},{4,0},{8,12},{12,8},{16,20},{20,16},{24,28},{28,24},{32,36},... | collective-permute-start | bytes 6193160 | tf_op jit(solution)/shard_map/ppermute | solution.py:415
  40.1 21.6 %collective-permute-start.4 = (f32[18,56,128]{2,1,0:T(8,128)}, f32[18,56,128]{2,1,0:T(8,128)S(1)}, u32[]{:S(2)}, u32[]{:S(2)}) collective-permute-start(f32[18,56,128]{2,1,0:T(8,128)} %get-tuple-element.36), channel_id=1, source_target_pairs={{0,1},{1,2},{2,3},{3,0},{4,5},{5,6},{6,7},{7,4},{8,9},{9,10},{10,1... | collective-permute-start | bytes 1548296 | tf_op jit(solution)/shard_map/ppermute | solution.py:407
  40.4 23.5 %collective-permute-start.5 = (f32[18,56,128]{2,1,0:T(8,128)}, f32[18,56,128]{2,1,0:T(8,128)S(1)}, u32[]{:S(2)}, u32[]{:S(2)}) collective-permute-start(f32[18,56,128]{2,1,0:T(8,128)} %get-tuple-element.37), channel_id=1, source_target_pairs={{0,2},{1,3},{2,0},{3,1},{4,6},{5,7},{6,4},{7,5},{8,10},{9,11},{10,... | collective-permute-start | bytes 1548296 | tf_op jit(solution)/shard_map/ppermute | solution.py:407
  42.2 23.1 %collective-permute-start.6 = (f32[18,56,128]{2,1,0:T(8,128)}, f32[18,56,128]{2,1,0:T(8,128)}, u32[]{:S(2)}, u32[]{:S(2)}) collective-permute-start(f32[18,56,128]{2,1,0:T(8,128)} %get-tuple-element.38), channel_id=1, source_target_pairs={{0,3},{1,0},{2,1},{3,2},{4,7},{5,4},{6,5},{7,6},{8,11},{9,8},{10,9... | collective-permute-start | bytes 1548296 | tf_op jit(solution)/shard_map/ppermute | solution.py:407
  61.7 3.6 %copy-start = (f32[18,56,128]{2,1,0:T(8,128)}, f32[18,56,128]{2,1,0:T(8,128)S(1)}, u32[]{:S(2)}) copy-start(f32[18,56,128]{2,1,0:T(8,128)S(1)} %collective-permute-done.4.refs_1_.refs_7_) | copy-start | bytes 1548292
  63.9 1.4 %copy-start.1 = (f32[18,56,128]{2,1,0:T(8,128)}, f32[18,56,128]{2,1,0:T(8,128)S(1)}, u32[]{:S(2)}) copy-start(f32[18,56,128]{2,1,0:T(8,128)S(1)} %collective-permute-done.5.refs_2_.refs_8_) | copy-start | bytes 1548292
  68.7 18.3 %all-to-all-start.1 = ((f32[16,8,128]{2,1,0:T(8,128)}), f32[16,8,128]{2,1,0:T(8,128)S(1)}, u32[]{:S(2)}, u32[]{:S(2)}) async-start(f32[16,8,128]{2,1,0:T(8,128)} %squares.1), calls=%async_computation.1 | async-start | bytes 131072 | tf_op jit(solution)/shard_map/all_to_all | solution.py:395
  87.6 12.4 %all-to-all-start.2 = ((f32[16,8,128]{2,1,0:T(8,128)}), f32[16,8,128]{2,1,0:T(8,128)S(1)}, u32[]{:S(2)}, u32[]{:S(2)}) async-start(f32[16,8,128]{2,1,0:T(8,128)} %broadcast_in_dim.10), calls=%async_computation.2 | async-start | bytes 131072 | tf_op jit(solution)/shard_map/all_to_all | solution.py:395

commit v7 on v6

--- a/solution.py
+++ b/solution.py
@@ -161,7 +161,12 @@
 
 
 def mix_kernel(info, w_ref, h_ref, *refs):
-    x_ref, *outs = refs
+    x_ref, far_outs, outs, sem = refs[0], refs[1:5], refs[5:9], refs[9]
+    ends = (0, 32, QROWS)
+    stores = [
+        [pltpu.make_async_copy(o.at[:, a:b], far.at[:, a:b], sem.at[i, k]) for i, (o, far) in enumerate(zip(outs, far_outs))]
+        for k, (a, b) in enumerate(zip(ends, ends[1:]))
+    ]
     w = w_ref[:, : 3 * LEV].astype(jnp.bfloat16)
     d = w_ref[:LEV, 3 * LEV :]
     x2 = x_ref.reshape(LEV * QROWS, 128)
@@ -183,10 +188,14 @@
             for e in range(2):
                 part = out[away * ROWS : away * ROWS + OWN, e * 128 : (e + 1) * 128]
                 o2[pl.ds(r + e, OWN, stride=QROWS), :] = part * h
+        if r + 2 in ends:
+            for store in stores[ends.index(r + 2) - 1]:
+                store.start()
+    for store in stores[0] + stores[1]:
+        store.wait()
 
 
 def mix(info, w3, hp, x):
-    held = pl.BlockSpec((OWN, QROWS, 128), lambda i, s: (0, 0, 0))
     return pl.pallas_call(
         mix_kernel,
         out_shape=[QUARTER] * 4,
@@ -198,7 +207,8 @@
                 pl.BlockSpec((1, QROWS, 128), lambda i, s: (s[2], 0, 0)),
                 VMEM,
             ],
-            out_specs=[held] * 4,
+            out_specs=[FAR] * 4,
+            scratch_shapes=[pltpu.VMEM((OWN, QROWS, 128), F32)] * 4 + [pltpu.SemaphoreType.DMA((4, 2))],
         ),
         name="mix",
     )(info, w3, hp, in_vmem(x))
@@ -356,8 +366,8 @@
 
     @pl.when(step == pl.num_programs(0) - 1)
     def _():
-        row = lax.broadcasted_iota(jnp.int32, (8, 128), 0)
-        both = jnp.where(row == 0, jnp.sum(v_ref[0]), jnp.sum(acc[0]))
+        lane = lax.broadcasted_iota(jnp.int32, (1, 128), 1)
+        both = jnp.where(lane < 64, jnp.sum(v_ref[0]), jnp.sum(acc[0]))
         o_ref[...] = jnp.broadcast_to(both, o_ref.shape)
 
 
@@ -369,12 +379,12 @@
     piece = pl.BlockSpec((SQUARES_STEP, QROWS, 128), lambda i, s: (i, 0, 0))
     return pl.pallas_call(
         squares_kernel,
-        out_shape=jax.ShapeDtypeStruct((copies, 8, 128), F32),
+        out_shape=jax.ShapeDtypeStruct((copies, 1, 128), F32),
         grid_spec=pltpu.PrefetchScalarGridSpec(
             num_scalar_prefetch=1,
             grid=(OWN // SQUARES_STEP,),
             in_specs=[whole((1, 8, 128)), whole((4, QROWS, 128)), VMEM] + [piece] * 4,
-            out_specs=whole((copies, 8, 128)),
+            out_specs=whole((copies, 1, 128)),
             scratch_shapes=[pltpu.VMEM((1, 8, 128), F32)],
         ),
         name="squares",
@@ -424,9 +434,9 @@
     sums = total(squares(lax.axis_size(inner), info, v_sum, live, kept, m), inner)
     rows = finish(0, info, diag, hp, live, p, part, m)
     sums, rows = lax.optimization_barrier((sums, rows))
-    sums = total(jnp.broadcast_to(sums[None], (lax.axis_size(outer), 8, 128)), outer)
+    sums = total(jnp.broadcast_to(sums[None], (lax.axis_size(outer), 1, 128)), outer)
     rows = finish(OWN // 2, info, diag, hp, live, p, part, m, rows)
-    norms = jnp.sqrt(sums[:2, 0] / (LEV * WAVES * (WAVES + 1)))
+    norms = jnp.sqrt(sums[0, ::64] / (LEV * WAVES * (WAVES + 1)))
     return (from_rows(rows), norms)
 
 

time: 101 us -> 100 us (0.990)
  no operation moved by 1% of the time
where the time goes in v7:
time: 100 us; the launch traced here: 99.6 us
  waiting for transfers between devices  37.2 us (37%)
  starting transfers between devices  30 us (30%)
  Pallas kernels  27.6 us (28%)
  local copies, waits for them, and re-layouts  2.56 us (3%)
  other arithmetic  1.48 us (1%)
    all_to_all x2, starting transfers between devices, total(): return jnp.sum(lax.all_to_all(copies, axes, 0, 0, tiled=True), axis=0)  16.1 us
    ppermute x1, waiting for transfers between devices, body(): x = lax.ppermute(p, MA, to_x)  13.6 us
    ppermute x1, waiting for transfers between devices, body(): y = lax.ppermute(p_after, MA, to_y)  12 us
    pallas_call x2, Pallas kernels, finish(): pl.pallas_call(lambda *refs: finish_kernel(base, *refs), out_shape=jax.Sh...  8.71 us
    pallas_call x1, Pallas kernels, near(): pl.pallas_call(near_kernel, out_shape=(jax.ShapeDtypeStruct(p.shape, F32)...  6.89 us
    all_to_all x2, waiting for transfers between devices, total(): return jnp.sum(lax.all_to_all(copies, axes, 0, 0, tiled=True), axis=0)  4.73 us
    ppermute x1, starting transfers between devices, body(): y = lax.ppermute(p_after, MA, to_y)  3.83 us
    pallas_call x1, Pallas kernels, mix(): pl.pallas_call(mix_kernel, out_shape=[QUARTER] * 4, grid_spec=pltpu.Prefe...  3.81 us
  transfers between devices with their start and end apart: 10, of which 7 were waited for; matrix products, arithmetic and copies ran while one was open for 3% of the time, Pallas kernels for 22%

profile of v7, /device:TPU:1, one launch (start us, length us, event | category | flops | bytes accessed | tf_op | source)
XLA Modules:
  0.0 99.6 jit_solution(4565410869260967838)
XLA Ops:
  0.6 2.9 %pack.1.p_ref.refs_4_ = f32[4,18,56,128]{3,2,1,0:T(8,128)} custom-call(f32[18,400,128]{2,1,0:T(8,128)} %bitcast.34), custom_call_target="tpu_custom_call" | custom-call | tf_op jit(solution)/shard_map/pack/pallas_call | solution.py:86
  3.5 0.0 copy-start.2
  3.5 2.5 %collective-permute-start = (f32[4,18,56,128]{3,2,1,0:T(8,128)}, f32[4,18,56,128]{3,2,1,0:T(8,128)}, u32[]{:S(2)}, u32[]{:S(2)}) collective-permute-start(f32[4,18,56,128]{3,2,1,0:T(8,128)} %pack.1.p_ref.refs_4_), channel_id=1, source_target_pairs={{0,4},{4,12},{8,0},{12,20},{16,8},{20,28},{24,16},{28,36},{32,24},... | collective-permute-start | bytes 6193160 | tf_op jit(solution)/shard_map/ppermute | solution.py:419
  6.1 0.9 collective-permute-start.1
  7.0 3.6 %all-to-all-start = ((f32[4,18,56,128]{3,2,1,0:T(8,128)}), f32[4,18,56,128]{3,2,1,0:T(8,128)S(1)}, u32[]{:S(2)}, u32[]{:S(2)}) async-start(f32[4,18,56,128]{3,2,1,0:T(8,128)} %pack.1.p_ref.refs_4_), calls=%async_computation | async-start | bytes 4128768 | tf_op jit(solution)/shard_map/all_to_all | solution.py:418
  10.6 0.0 copy-start.3
  10.6 0.0 copy-done.2
  10.6 0.2 reshape.53
  10.8 0.9 copy.13
  11.7 0.0 copy-done.3
  11.8 0.1 select_reduce_fusion.d_ref.refs_1_
  11.9 0.0 copy-start.4
  11.9 0.1 copy.14
  12.0 0.6 stack.24.info.refs_0_
  12.6 2.0 %prep.1 = (f32[4,224,128]{2,1,0:T(8,128)}, f32[224,128]{1,0:T(8,128)}, f32[224,128]{1,0:T(8,128)}) custom-call(s32[6]{0:T(128)} %stack.24.info.refs_0_, f32[800,128]{1,0:T(8,128)} %bitcast.44, f32[10,128]{1,0:T(8,128)} %bitcast.49), custom_call_target="tpu_custom_call" | custom-call | tf_op jit(solution)/shard_map/prep/pallas_call | solution.py:151
  14.6 0.8 select_maximum_fusion.w_ref
  15.4 13.6 %collective-permute-done.x_ref = f32[4,18,56,128]{3,2,1,0:T(8,128)} collective-permute-done((f32[4,18,56,128]{3,2,1,0:T(8,128)}, f32[4,18,56,128]{3,2,1,0:T(8,128)}, u32[]{:S(2)}, u32[]{:S(2)}) %collective-permute-start) | collective-permute-done | bytes 2064416 | tf_op jit(solution)/shard_map/ppermute | solution.py:419
  29.0 3.8 %collective-permute-start.2 = (f32[4,18,56,128]{3,2,1,0:T(8,128)}, f32[4,18,56,128]{3,2,1,0:T(8,128)}, u32[]{:S(2)}, u32[]{:S(2)}) collective-permute-start(f32[4,18,56,128]{3,2,1,0:T(8,128)} %pack.1.p_ref.refs_4_), channel_id=1, source_target_pairs={{0,8},{4,0},{8,16},{12,4},{16,24},{20,12},{24,32},{28,20},{32,40},... | collective-permute-start | bytes 6193160 | tf_op jit(solution)/shard_map/ppermute | solution.py:424
  32.9 0.2 collective-permute-start.3
  33.0 3.1 %all-to-all-done = f32[4,18,56,128]{3,2,1,0:T(8,128)S(1)} async-done(((f32[4,18,56,128]{3,2,1,0:T(8,128)}), f32[4,18,56,128]{3,2,1,0:T(8,128)S(1)}, u32[]{:S(2)}, u32[]{:S(2)}) %all-to-all-start) | async-done | bytes 2064416 | tf_op jit(solution)/shard_map/all_to_all | solution.py:418
  36.1 3.8 %mix.1 = (f32[18,56,128]{2,1,0:T(8,128)}, f32[18,56,128]{2,1,0:T(8,128)}, f32[18,56,128]{2,1,0:T(8,128)}, f32[18,56,128]{2,1,0:T(8,128)}) custom-call(s32[6]{0:T(128)} %stack.24.info.refs_0_, f32[96,217]{1,0:T(8,128)} %select_maximum_fusion.w_ref, f32[4,56,128]{2,1,0:T(8,128)} %bitcast.36, f32[72,56,128]{2,1,0:T(8,128)S(1)} %bitcast.32), custom_call_target="tpu_custom_call" | custom-call | tf_op jit(solution)/shard_map/mix/pallas_call | solution.py:199
  39.9 0.4 collective-permute-start.4
  40.3 1.8 %collective-permute-start.5 = (f32[18,56,128]{2,1,0:T(8,128)}, f32[18,56,128]{2,1,0:T(8,128)S(1)}, u32[]{:S(2)}, u32[]{:S(2)}) collective-permute-start(f32[18,56,128]{2,1,0:T(8,128)} %get-tuple-element.37), channel_id=1, source_target_pairs={{0,2},{1,3},{2,0},{3,1},{4,6},{5,7},{6,4},{7,5},{8,10},{9,11},{10,... | collective-permute-start | bytes 1548296 | tf_op jit(solution)/shard_map/ppermute | solution.py:417
  42.1 0.0 collective-permute-done.1.q_ref
  42.1 0.7 collective-permute-start.6
  42.8 12.0 %collective-permute-done.2.y_ref = f32[4,18,56,128]{3,2,1,0:T(8,128)} collective-permute-done((f32[4,18,56,128]{3,2,1,0:T(8,128)}, f32[4,18,56,128]{3,2,1,0:T(8,128)}, u32[]{:S(2)}, u32[]{:S(2)}) %collective-permute-start.2) | collective-permute-done | bytes 2064416 | tf_op jit(solution)/shard_map/ppermute | solution.py:424
  54.8 0.0 collective-permute-done.3.z_ref
  54.8 0.0 copy-done.4
  54.8 6.9 %near.1 = (f32[4,18,56,128]{3,2,1,0:T(8,128)}, f32[4,18,56,128]{3,2,1,0:T(8,128)S(1)}, f32[1,8,128]{2,1,0:T(8,128)}) custom-call(s32[6]{0:T(128)} %stack.24.info.refs_0_, f32[72]{0:T(128)} %copy-done.4, f32[4,4,56,128]{3,2,1,0:T(8,128)} %bitcast.45, f32[4,56,128]{2,1,0:T(8,128)} %bitcast.37, f32[4,56,128]{2,1,0:T(8,128)} %bitcast.40, ...), custom_call_target="tpu_custom_call" | custom-call | tf_op jit(solution)/shard_map/near/pallas_call | solution.py:290
  61.7 0.0 collective-permute-done.4.refs_1_.refs_7_
  61.7 0.0 copy-start
  61.7 2.1 %collective-permute-done.5.refs_2_.refs_8_ = f32[18,56,128]{2,1,0:T(8,128)S(1)} collective-permute-done((f32[18,56,128]{2,1,0:T(8,128)}, f32[18,56,128]{2,1,0:T(8,128)S(1)}, u32[]{:S(2)}, u32[]{:S(2)}) %collective-permute-start.5) | collective-permute-done | bytes 516128 | tf_op jit(solution)/shard_map/ppermute | solution.py:417
  63.8 0.0 copy-start.1
  63.8 1.6 %collective-permute-done.6.refs_3_.refs_9_ = f32[18,56,128]{2,1,0:T(8,128)} collective-permute-done((f32[18,56,128]{2,1,0:T(8,128)}, f32[18,56,128]{2,1,0:T(8,128)}, u32[]{:S(2)}, u32[]{:S(2)}) %collective-permute-start.6) | collective-permute-done | bytes 516128 | tf_op jit(solution)/shard_map/ppermute | solution.py:417
  65.4 0.0 copy-done
  65.4 0.0 copy-done.1
  65.4 3.3 %squares.1 = f32[16,1,128]{2,1,0:T(1,128)} custom-call(s32[6]{0:T(128)} %stack.24.info.refs_0_, f32[1,8,128]{2,1,0:T(8,128)} %get-tuple-element.44.v_ref, f32[4,56,128]{2,1,0:T(8,128)} %bitcast.41, f32[4,18,56,128]{3,2,1,0:T(8,128)S(1)} %get-tuple-element.45.part_ref, f32[18,56,128]{2,1,0:T(8,128)} %get-tuple-element.40.refs_0_.refs_6_, ...), custom_call_target="tpu_custom_call" | custom-call | tf_op jit(solution)/shard_map/squares/pallas_call | solution.py:380
  68.8 10.3 %all-to-all-start.1 = ((f32[16,1,128]{2,1,0:T(1,128)}), f32[16,1,128]{2,1,0:T(1,128)S(1)}, u32[]{:S(2)}, u32[]{:S(2)}) async-start(f32[16,1,128]{2,1,0:T(1,128)} %squares.1), calls=%async_computation.1 | async-start | bytes 16384 | tf_op jit(solution)/shard_map/all_to_all | solution.py:405
  79.0 4.3 %finish.2.refs_10_ = f32[18,400,128]{2,1,0:T(8,128)} custom-call(s32[6]{0:T(128)} %stack.24.info.refs_0_, f32[72]{0:T(128)} %copy-done.4, f32[4,56,128]{2,1,0:T(8,128)} %bitcast.38, f32[4,56,128]{2,1,0:T(8,128)} %bitcast.42, f32[4,18,56,128]{3,2,1,0:T(8,128)} %pack.1.p_ref.refs_4_, f32[4,18,56,128]{3,2,1,0:T(8,128)} %get-tuple-element.39.refs_5_, ...), custom_call_target="tpu_custom_call" | custom-call | tf_op jit(solution)/shard_map/finish/pallas_call | solution.py:325
  83.4 2.7 %all-to-all-done.1 = f32[16,1,128]{2,1,0:T(1,128)S(1)} async-done(((f32[16,1,128]{2,1,0:T(1,128)}), f32[16,1,128]{2,1,0:T(1,128)S(1)}, u32[]{:S(2)}, u32[]{:S(2)}) %all-to-all-start.1) | async-done | bytes 8224 | tf_op jit(solution)/shard_map/all_to_all | solution.py:405
  86.1 0.6 broadcast_in_dim.13
  86.7 5.8 %all-to-all-start.2 = ((f32[16,1,128]{2,1,0:T(1,128)}), f32[16,1,128]{2,1,0:T(1,128)S(1)}, u32[]{:S(2)}, u32[]{:S(2)}) async-start(f32[16,1,128]{2,1,0:T(1,128)} %broadcast_in_dim.13), calls=%async_computation.2 | async-start | bytes 16384 | tf_op jit(solution)/shard_map/all_to_all | solution.py:405
  92.5 4.4 %finish.3 = f32[18,400,128]{2,1,0:T(8,128)} custom-call(s32[6]{0:T(128)} %stack.24.info.refs_0_, f32[72]{0:T(128)} %copy-done.4, f32[4,56,128]{2,1,0:T(8,128)} %bitcast.39, f32[4,56,128]{2,1,0:T(8,128)} %bitcast.43, f32[4,18,56,128]{3,2,1,0:T(8,128)} %pack.1.p_ref.refs_4_, ...), custom_call_target="tpu_custom_call", output_to_operand_aliasing={{}: (10, {})} | custom-call | tf_op jit(solution)/shard_map/finish/pallas_call | solution.py:325
  96.9 2.1 %all-to-all-done.2 = f32[16,1,128]{2,1,0:T(1,128)S(1)} async-done(((f32[16,1,128]{2,1,0:T(1,128)}), f32[16,1,128]{2,1,0:T(1,128)S(1)}, u32[]{:S(2)}, u32[]{:S(2)}) %all-to-all-start.2) | async-done | bytes 8224 | tf_op jit(solution)/shard_map/all_to_all | solution.py:405
  98.9 0.1 slice.3
  99.0 0.5 sqrt_bitcast_fusion
  (5 shorter events, 0.1 us)
Async XLA Ops:
  3.5 7.1 %copy-start.2 = (f32[4,20,1280]{2,0,1:T(4,128)S(1)}, f32[4,20,1280]{2,0,1:T(4,128)}, u32[]{:S(2)}) copy-start(f32[4,20,1280]{2,0,1:T(4,128)} %param.5) | copy-start | bytes 1228804
  3.5 25.5 %collective-permute-start = (f32[4,18,56,128]{3,2,1,0:T(8,128)}, f32[4,18,56,128]{3,2,1,0:T(8,128)}, u32[]{:S(2)}, u32[]{:S(2)}) collective-permute-start(f32[4,18,56,128]{3,2,1,0:T(8,128)} %pack.1.p_ref.refs_4_), channel_id=1, source_target_pairs={{0,4},{4,12},{8,0},{12,20},{16,8},{20,28},{24,16},{28,36},{32,24},... | collective-permute-start | bytes 6193160 | tf_op jit(solution)/shard_map/ppermute | solution.py:419
  6.1 36.0 %collective-permute-start.1 = (f32[4,18,56,128]{3,2,1,0:T(8,128)}, f32[4,18,56,128]{3,2,1,0:T(8,128)}, u32[]{:S(2)}, u32[]{:S(2)}) collective-permute-start(f32[4,18,56,128]{3,2,1,0:T(8,128)} %pack.1.p_ref.refs_4_), channel_id=1, source_target_pairs={{0,4},{4,0},{8,12},{12,8},{16,20},{20,16},{24,28},{28,24},{32,36},... | collective-permute-start | bytes 6193160 | tf_op jit(solution)/shard_map/ppermute | solution.py:420
  7.0 29.1 %all-to-all-start = ((f32[4,18,56,128]{3,2,1,0:T(8,128)}), f32[4,18,56,128]{3,2,1,0:T(8,128)S(1)}, u32[]{:S(2)}, u32[]{:S(2)}) async-start(f32[4,18,56,128]{3,2,1,0:T(8,128)} %pack.1.p_ref.refs_4_), calls=%async_computation | async-start | bytes 4128768 | tf_op jit(solution)/shard_map/all_to_all | solution.py:418
  10.6 1.2 %copy-start.3 = (f32[72,72]{1,0:T(8,128)S(1)}, f32[72,72]{1,0:T(8,128)}, u32[]{:S(2)}) copy-start(f32[72,72]{1,0:T(8,128)} %param.7) | copy-start | bytes 62212
  11.9 42.9 %copy-start.4 = (f32[72]{0:T(128)}, f32[72]{0:T(128)S(1)}, u32[]{:S(2)}) copy-start(f32[72]{0:T(128)S(1)} %select_reduce_fusion.d_ref.refs_1_) | copy-start | bytes 868
  29.0 25.8 %collective-permute-start.2 = (f32[4,18,56,128]{3,2,1,0:T(8,128)}, f32[4,18,56,128]{3,2,1,0:T(8,128)}, u32[]{:S(2)}, u32[]{:S(2)}) collective-permute-start(f32[4,18,56,128]{3,2,1,0:T(8,128)} %pack.1.p_ref.refs_4_), channel_id=1, source_target_pairs={{0,8},{4,0},{8,16},{12,4},{16,24},{20,12},{24,32},{28,20},{32,40},... | collective-permute-start | bytes 6193160 | tf_op jit(solution)/shard_map/ppermute | solution.py:424
  32.9 21.9 %collective-permute-start.3 = (f32[4,18,56,128]{3,2,1,0:T(8,128)}, f32[4,18,56,128]{3,2,1,0:T(8,128)}, u32[]{:S(2)}, u32[]{:S(2)}) collective-permute-start(f32[4,18,56,128]{3,2,1,0:T(8,128)} %collective-permute-done.x_ref), channel_id=1, source_target_pairs={{0,4},{4,0},{8,12},{12,8},{16,20},{20,16},{24,28},{28,24},{32,36},... | collective-permute-start | bytes 6193160 | tf_op jit(solution)/shard_map/ppermute | solution.py:425
  39.9 21.8 %collective-permute-start.4 = (f32[18,56,128]{2,1,0:T(8,128)}, f32[18,56,128]{2,1,0:T(8,128)S(1)}, u32[]{:S(2)}, u32[]{:S(2)}) collective-permute-start(f32[18,56,128]{2,1,0:T(8,128)} %get-tuple-element.36), channel_id=1, source_target_pairs={{0,1},{1,2},{2,3},{3,0},{4,5},{5,6},{6,7},{7,4},{8,9},{9,10},{10,1... | collective-permute-start | bytes 1548296 | tf_op jit(solution)/shard_map/ppermute | solution.py:417
  40.3 23.5 %collective-permute-start.5 = (f32[18,56,128]{2,1,0:T(8,128)}, f32[18,56,128]{2,1,0:T(8,128)S(1)}, u32[]{:S(2)}, u32[]{:S(2)}) collective-permute-start(f32[18,56,128]{2,1,0:T(8,128)} %get-tuple-element.37), channel_id=1, source_target_pairs={{0,2},{1,3},{2,0},{3,1},{4,6},{5,7},{6,4},{7,5},{8,10},{9,11},{10,... | collective-permute-start | bytes 1548296 | tf_op jit(solution)/shard_map/ppermute | solution.py:417
  42.1 23.4 %collective-permute-start.6 = (f32[18,56,128]{2,1,0:T(8,128)}, f32[18,56,128]{2,1,0:T(8,128)}, u32[]{:S(2)}, u32[]{:S(2)}) collective-permute-start(f32[18,56,128]{2,1,0:T(8,128)} %get-tuple-element.38), channel_id=1, source_target_pairs={{0,3},{1,0},{2,1},{3,2},{4,7},{5,4},{6,5},{7,6},{8,11},{9,8},{10,9... | collective-permute-start | bytes 1548296 | tf_op jit(solution)/shard_map/ppermute | solution.py:417
  61.7 3.7 %copy-start = (f32[18,56,128]{2,1,0:T(8,128)}, f32[18,56,128]{2,1,0:T(8,128)S(1)}, u32[]{:S(2)}) copy-start(f32[18,56,128]{2,1,0:T(8,128)S(1)} %collective-permute-done.4.refs_1_.refs_7_) | copy-start | bytes 1548292
  63.8 1.7 %copy-start.1 = (f32[18,56,128]{2,1,0:T(8,128)}, f32[18,56,128]{2,1,0:T(8,128)S(1)}, u32[]{:S(2)}) copy-start(f32[18,56,128]{2,1,0:T(8,128)S(1)} %collective-permute-done.5.refs_2_.refs_8_) | copy-start | bytes 1548292
  68.8 17.3 %all-to-all-start.1 = ((f32[16,1,128]{2,1,0:T(1,128)}), f32[16,1,128]{2,1,0:T(1,128)S(1)}, u32[]{:S(2)}, u32[]{:S(2)}) async-start(f32[16,1,128]{2,1,0:T(1,128)} %squares.1), calls=%async_computation.1 | async-start | bytes 16384 | tf_op jit(solution)/shard_map/all_to_all | solution.py:405
  86.7 12.2 %all-to-all-start.2 = ((f32[16,1,128]{2,1,0:T(1,128)}), f32[16,1,128]{2,1,0:T(1,128)S(1)}, u32[]{:S(2)}, u32[]{:S(2)}) async-start(f32[16,1,128]{2,1,0:T(1,128)} %broadcast_in_dim.13), calls=%async_computation.2 | async-start | bytes 16384 | tf_op jit(solution)/shard_map/all_to_all | solution.py:405
